TPU v7x, 32 devices: a whole 2x2x4 slice. The times are simulated.
32 devices in a mesh: grp: 4 (over y, core), blk: 8 (over z, x).
Axes of the slice: x: 2, y: 2, z: 4, core: 2. Of those that a mesh axis runs over, the one named last changes fastest.
Arguments:
- state: float32 [4, 3, 512, 1024], P('grp', None, None, 'blk'), may hold values from -1 to 1
- material: float32 [4, 3, 512, 1024], P('grp', None, None, 'blk'), may hold values from 0.5 to 2
- occupied: int32 [4096], P(('grp', 'blk')), may hold values from 0 to 1, as said below
- brick_column: int32 [4096, 1], P(('grp', 'blk')), may hold values from 0 to 7, as said below
- brick_octant: int32 [4096], P(('grp', 'blk')), may hold values from 0 to 383
Outputs:
- new_state: float32 [4, 3, 512, 1024], P('grp', None, None, 'blk')
Inputs may be any that keep to these rules, and one draw needn't show every extreme that they name: `brick_column`: the rows of one device name at most 32 elements of one column, and exactly 32 of some column; rows of grp index 3 are not read. `brick_octant`: rows of grp index 3 are not read. The slots e < 32 of every device are occupied.
All inputs are finite; a program needn't handle non-finite values.
Results may differ from a plain program's by a relative error of at most 0.00074.
Values may be sent and summed in bfloat16 or wider, within the bound.
No kernel may reach another device: no remote copies, remote signals or barrier semaphores. Data moves between devices by JAX's collectives and lax.ppermute only.
A program may use at most 128 MiB of HBM per device.

v0:
```python
import jax
import jax.numpy as jnp
from jax import lax
from jax.experimental import pallas as pl
from jax.experimental.pallas import tpu as pltpu
from jax.sharding import PartitionSpec as P

UNIT_LENGTH = 0.02
TIME_STEP = 0.1
PENALTY = 1.0
PRESSURE_SCALE = 0.05
DILATION_SCALE = 50.0
SWEEP_STEP = 0.03
SOURCE_RATE = 2.0
CUBIC_TERM = 0.3

LANES = 128
F32, BF16 = jnp.float32, jnp.bfloat16
VMEM = pl.BlockSpec(memory_space=pltpu.VMEM)
SMEM = pl.BlockSpec(memory_space=pltpu.SMEM)


def shape_of(shape, dtype=F32):
    return jax.ShapeDtypeStruct(shape, dtype)


def call(body, args, outs, scratch=(), smem=0, name=None):
    return pl.pallas_call(
        body,
        out_shape=outs,
        in_specs=[SMEM] * smem + [VMEM] * (len(args) - smem),
        out_specs=jax.tree.map(lambda _: VMEM, outs),
        scratch_shapes=list(scratch),
        name=name,
    )(*args)


def iota(shape, dim):
    return lax.broadcasted_iota(jnp.int32, shape, dim)


def dot(a, b, dims):
    return lax.dot_general(a, b, (dims, ((), ())), preferred_element_type=F32)


def diff_i(below, here, above, i):
    if below is None:
        return above - here
    if above is None:
        return here - below
    return 0.5 * (above - below)


def diff_j(x):
    return jnp.concatenate([x[1:2] - x[0:1], 0.5 * (x[2:] - x[:-2]), x[7:8] - x[6:7]], axis=0)


def diff_k(x):
    k = iota(x.shape, 1)
    upper = jnp.where(k == 7, x, pltpu.roll(x, 7, 1))
    lower = jnp.where(k == 0, x, pltpu.roll(x, 1, 1))
    return jnp.where((k == 0) | (k == 7), 1.0, 0.5) * (upper - lower)


def slab(ref, c, i):
    rows = ref[pl.ds(c * 512 + 64 * i, 64), :]
    return rows.reshape(8, 8, rows.shape[-1])


def put_slab(ref, c, i, value):
    ref[pl.ds(c * 512 + 64 * i, 64), :] = value.reshape(64, value.shape[-1])


def gradients(ref, i):
    grads = []
    for c in range(3):
        here = UNIT_LENGTH * slab(ref, c, i)
        below = UNIT_LENGTH * slab(ref, c, i - 1) if i > 0 else None
        above = UNIT_LENGTH * slab(ref, c, i + 1) if i < 7 else None
        row = [diff_i(below, here, above, i), diff_j(here), diff_k(here)]
        row[c] = row[c] + 1.0
        grads.append(row)
    return grads


def determinant(grads):
    return (
        grads[0][0] * (grads[1][1] * grads[2][2] - grads[1][2] * grads[2][1])
        - grads[0][1] * (grads[1][0] * grads[2][2] - grads[1][2] * grads[2][0])
        + grads[0][2] * (grads[1][0] * grads[2][1] - grads[1][1] * grads[2][0])
    )


def cofactors(g):
    return [
        [
            g[1][1] * g[2][2] - g[1][2] * g[2][1],
            g[1][2] * g[2][0] - g[1][0] * g[2][2],
            g[1][0] * g[2][1] - g[1][1] * g[2][0],
        ],
        [
            g[0][2] * g[2][1] - g[0][1] * g[2][2],
            g[0][0] * g[2][2] - g[0][2] * g[2][0],
            g[0][1] * g[2][0] - g[0][0] * g[2][1],
        ],
        [
            g[0][1] * g[1][2] - g[0][2] * g[1][1],
            g[0][2] * g[1][0] - g[0][0] * g[1][2],
            g[0][0] * g[1][1] - g[0][1] * g[1][0],
        ],
    ]


def dilate(ref, filled, out):
    for i in range(8):
        change = (determinant(gradients(ref, i)) - 1.0) * filled * DILATION_SCALE
        out[pl.ds(64 * i, 64), :] = change.reshape(64, change.shape[-1]).astype(BF16)


def put_faces(ref, up, down):
    for c in range(3):
        up[pl.ds(64 * c, 64), :] = ref[pl.ds(c * 512 + 448, 64), :]
        down[pl.ds(64 * c, 64), :] = ref[pl.ds(c * 512, 64), :]


def advance(ref, mat, filled, recv, sel, low, high, fills, out, pressure, stress, partial):
    e = filled.shape[-1]
    pressure[...] = dot(recv[...], sel[...], ((0,), (0,))) * PRESSURE_SCALE
    for i in range(8):
        g = gradients(ref, i)
        shear, lame = slab(mat, 0, i), slab(mat, 1, i)
        c = {}
        for a in range(3):
            for b in range(a, 3):
                c[a, b] = g[0][a] * g[0][b] + g[1][a] * g[1][b] + g[2][a] * g[2][b]
        diag = [c[a, a] - 1.0 for a in range(3)]
        volume = lame * (0.5 * (diag[0] + diag[1] + diag[2]))
        s = {}
        for a in range(3):
            s[a, a] = shear * diag[a] + volume
            for b in range(a + 1, 3):
                s[a, b] = s[b, a] = shear * c[a, b]
        cof = cofactors(g)
        p = pressure[pl.ds(64 * i, 64), :].reshape(8, 8, e)
        for a in range(3):
            first = [
                g[a][0] * s[0, b] + g[a][1] * s[1, b] + g[a][2] * s[2, b] - p * cof[a][b]
                for b in range(3)
            ]
            put_slab(stress, a, i, first[0])
            put_slab(partial, a, i, diff_j(first[1]) + diff_k(first[2]))
    penalty = PENALTY * UNIT_LENGTH
    k = iota((8, 8, e), 1)
    fill_low, fill_high = fills[0].reshape(1, 1, e), fills[1].reshape(1, 1, e)
    lane = iota((1, 1, e), 2)
    fill_before = jnp.where(lane == 0, 0.0, pltpu.roll(filled, 1, 2)) * penalty
    fill_after = jnp.where(lane == e - 1, 0.0, pltpu.roll(filled, e - 1, 2)) * penalty
    before_scale = jnp.where(k == 0, fill_before, 0.0)
    after_scale = jnp.where(k == 7, fill_after, 0.0)
    for i in range(8):
        rate = (TIME_STEP / UNIT_LENGTH) * slab(mat, 2, i) * filled
        for a in range(3):
            here = slab(ref, a, i)
            force = slab(partial, a, i) + diff_i(
                slab(stress, a, i - 1) if i > 0 else None,
                slab(stress, a, i),
                slab(stress, a, i + 1) if i < 7 else None,
                i,
            )
            if i == 0:
                other = low[pl.ds(64 * a, 64), :].reshape(8, 8, e)
                force = force + penalty * fill_low * (other - here)
            if i == 7:
                other = high[pl.ds(64 * a, 64), :].reshape(8, 8, e)
                force = force + penalty * fill_high * (other - here)
            before = pltpu.roll(pltpu.roll(here, 1, 1), 1, 2)
            after = pltpu.roll(pltpu.roll(here, 7, 1), e - 1, 2)
            force = force + before_scale * (before - here) + after_scale * (after - here)
            put_slab(out, a, i, here + rate * force)


def permute_in(x, tables):
    x = jnp.take_along_axis(x, tables[0], axis=1, mode="promise_in_bounds")
    x = jnp.take_along_axis(x, tables[1], axis=0, mode="promise_in_bounds")
    return jnp.take_along_axis(x, tables[2], axis=1, mode="promise_in_bounds")


def tables_in():
    row, lane = iota((8, LANES), 0), iota((8, LANES), 1)
    high, low = lane // 16, lane % 16
    return (8 * low + (high - row + 8) % 8, (high - row + 8) % 8, 16 * ((high + row) % 8) + low)


def tables_out():
    row, lane = iota((8, LANES), 0), iota((8, LANES), 1)
    high, low = lane // 16, lane % 16
    return (
        16 * ((high - row + 8) % 8) + low,
        (high - row + 8) % 8,
        16 * ((lane % 8 + row) % 8) + lane // 8,
    )


def to_octants(ref, out, scale, tables, tiles):
    rows = 16 * tiles
    lane = iota((8, LANES), 1)

    def layer(x, carry):
        chunk = ref[pl.ds(pl.multiple_of(x * rows, 8), rows), :]
        for y in range(16):
            part = chunk[tiles * y : min(tiles * y + 8, rows)]
            if part.shape[0] < 8:
                pad = jnp.zeros((8 - part.shape[0], LANES), F32)
                part = jnp.concatenate([part, pad], axis=0)
            part = permute_in(part, tables)
            part = jnp.where(lane < 16 * tiles, part, 0.0)
            if scale != 1.0:
                part = part * scale
            out[x, pl.ds(8 * (y % 8), 8), pl.ds(LANES * (y // 8), LANES)] = part
        return carry

    lax.fori_loop(0, 16, layer, 0)


def from_octants(ref, out, tables, tiles):
    rows = 16 * tiles

    def layer(x, carry):
        parts = []
        for y in range(16):
            part = ref[x, pl.ds(8 * (y % 8), 8), pl.ds(LANES * (y // 8), LANES)]
            parts.append(permute_in(part, tables)[:tiles])
        out[pl.ds(pl.multiple_of(x * rows, 8), rows), :] = jnp.concatenate(parts, axis=0)
        return carry

    lax.fori_loop(0, 16, layer, 0)


def put_pressures(ref, out):
    for x in range(16):
        i, ox = x % 8, x // 8
        f = ref[x]
        f = f + CUBIC_TERM * f * f * f
        out[pl.ds(64 * i, 64), pl.ds(256 * ox, 256)] = f.astype(BF16)


def one_hot(tile):
    return jnp.concatenate(
        [jnp.where(tile == float(o + 1), 1.0, 0.0).astype(BF16) for o in range(4)], axis=1
    )


def pieces(array):
    return [array[8 * n : 8 * n + 8] for n in range(8)]


def sweep(read, kap, masks):
    low, here, high = read
    inner, outer, last, first = masks
    halves = [[v[:, LANES * o : LANES * (o + 1)].reshape(8, 8, LANES) for v in (low, here, high)] for o in range(2)]
    out = []
    for o in range(2):
        below, c, above = halves[o]
        twin = halves[1 - o][1]
        if o == 0:
            y_above = jnp.concatenate([c[1:], twin[0:1]], axis=0)
            y_below = jnp.concatenate([c[0:1], c[:-1]], axis=0)
        else:
            y_above = jnp.concatenate([c[1:], c[7:8]], axis=0)
            y_below = jnp.concatenate([twin[7:8], c[:-1]], axis=0)
        r = pltpu.roll(c, 7, 1)
        z_above = jnp.where(inner, r, jnp.where(last, c, pltpu.roll(r, LANES - 1, 2)))
        r = pltpu.roll(c, 1, 1)
        z_below = jnp.where(outer, r, jnp.where(first, c, pltpu.roll(r, 1, 2)))
        base = 1.0 + c * c
        inflow = None
        for n in (above, below, y_above, y_below, z_above, z_below):
            part = (base + n * n) * (n - c)
            inflow = part if inflow is None else inflow + part
        out.append((c + kap[o] * inflow).reshape(64, LANES))
    return jnp.concatenate(out, axis=1)


def halves_of(ref, n):
    return jnp.concatenate(
        [ref[pl.ds(128 * n, 64), :], ref[pl.ds(128 * n + 64, 64), :]], axis=1
    )


def two_sweeps(phi, low, high, kap, kap_low, kap_high, wide, middle, out, q_count):
    k, lane = iota((8, 8, LANES), 1), iota((8, 8, LANES), 2)
    masks = (k < 7, k > 0, lane == q_count - 1, lane == 0)
    for n in range(2):
        wide[n] = halves_of(low, n)
        wide[18 + n] = halves_of(high, n)
    wide[pl.ds(2, 16)] = phi[...]

    def split(layer):
        return [layer[:, LANES * o : LANES * (o + 1)].reshape(8, 8, LANES) for o in range(2)]

    def around(ref, x):
        return ref[x - 1], ref[x], ref[x + 1]

    middle[0] = sweep(around(wide, 1), split(halves_of(kap_low, 0)), masks)
    middle[17] = sweep(around(wide, 18), split(halves_of(kap_high, 0)), masks)

    def first(x, carry):
        middle[x + 1] = sweep(around(wide, x + 2), split(kap[x]), masks)
        return carry

    lax.fori_loop(0, 16, first, 0)

    def second(x, carry):
        out[x] = sweep(around(middle, x + 1), split(kap[x]), masks)
        return carry

    lax.fori_loop(0, 16, second, 0)


def prepare(n_blk, cap, tiles, solvent):
    def body(grp, state, mat, occ, col, octant, send, sel, field, phi, kap, up, down, dil):
        e = state.shape[-1]

        @pl.when(grp[0] != solvent)
        def _():
            filled = occ[...].reshape(1, 1, e)
            dilate(state, filled, dil)
            hits = jnp.where(col[...] == iota((n_blk, e), 0), 1.0, 0.0)
            earlier = jnp.where(iota((e, e), 0) < iota((e, e), 1), 1.0, 0.0).astype(BF16)
            rank = dot(hits.astype(BF16), earlier, ((1,), (0,)))
            rank = jnp.sum(rank * hits, axis=0, keepdims=True).astype(jnp.int32)
            slot = col[...] * cap + rank
            chosen = jnp.where(iota((n_blk * cap, e), 0) == slot, 1.0, 0.0).astype(BF16)
            sel[...] = chosen
            send[:, pl.ds(0, 512)] = dot(chosen, dil[...], ((1,), (1,))).astype(BF16)
            o = octant[...]
            quarter = 16 * tiles
            block = sum((jnp.where(o >= n * quarter, 1, 0) for n in range(1, 4)))
            spot = o - quarter * block
            tile = jnp.where(iota((e, LANES), 1) == spot, (block + 1).astype(F32), 0.0)
            tile = dot(chosen, tile.astype(BF16), ((1,), (0,)))
            send[:, pl.ds(512, LANES)] = tile.astype(BF16)
            put_faces(state, up, down)
            up[pl.ds(192, 8), :] = jnp.broadcast_to(occ[...], (8, e))
            down[pl.ds(192, 8), :] = jnp.broadcast_to(occ[...], (8, e))

        @pl.when(grp[0] == solvent)
        def _():
            tables = tables_in()
            to_octants(state, phi, 1.0, tables, tiles)
            put_pressures(phi, field)
            to_octants(mat, kap, 0.5 * SWEEP_STEP, tables, tiles)
            for o in range(2):
                rows, lanes = pl.ds(64 * o, 64), pl.ds(LANES * o, LANES)
                up[rows, :] = kap[15, :, lanes]
                down[rows, :] = kap[0, :, lanes]

    return body


def gather_field(grp, recv, f0, f1, f2, out):
    g = grp[0]
    field = jnp.where(g == 0, f0[...], jnp.where(g == 1, f1[...], f2[...]))
    out[...] = dot(one_hot(recv[:, pl.ds(512, LANES)].astype(F32)), field, ((1,), (1,))).astype(BF16)


def first_step(state, mat, occ, sel, recv, low, high, out, send, up, down, *scratch):
    filled = occ[...].reshape(1, 1, occ.shape[-1])
    fills = (low[pl.ds(192, 1), :], high[pl.ds(192, 1), :])
    advance(state, mat, filled, recv, sel, low, high, fills, out, *scratch[:3])
    dil = scratch[3]
    dilate(out, filled, dil)
    send[...] = dot(sel[...], dil[...], ((1,), (1,))).astype(BF16)
    put_faces(out, up, down)


def last_step(state, mat, occ, sel, recv, low, high, fill_low, fill_high, out, *scratch):
    filled = occ[...].reshape(1, 1, occ.shape[-1])
    fills = (fill_low[pl.ds(192, 1), :], fill_high[pl.ds(192, 1), :])
    advance(state, mat, filled, recv, sel, low, high, fills, out, *scratch)


def deposit(with_hot):
    def body(phi, *refs):
        values, tiles = refs[:3], refs[3:6]
        out, up, down = refs[6:]
        total = None
        for v, t in zip(values, tiles):
            hot = one_hot(t[:, pl.ds(t.shape[-1] - LANES, LANES)].astype(F32))
            part = dot(v[:, pl.ds(0, 512)], hot, ((0,), (0,)))
            total = part if total is None else total + part
        for x in range(16):
            i, ox = x % 8, x // 8
            layer = phi[x] + (SWEEP_STEP * SOURCE_RATE) * total[64 * i : 64 * i + 64, 256 * ox : 256 * ox + 256]
            out[x] = layer
            for base, ref in ((14, up), (0, down)):
                if base <= x < base + 2:
                    for o in range(2):
                        ref[pl.ds(128 * (x - base) + 64 * o, 64), :] = layer[:, LANES * o : LANES * (o + 1)]

    return body


def spread_first(q_count):
    def body(phi, low, high, kap, kap_low, kap_high, t0, t1, t2, out, s0, s1, s2, wide, middle, field):
        two_sweeps(phi, low, high, kap, kap_low, kap_high, wide, middle, out, q_count)
        put_pressures(out, field)
        for t, s in ((t0, s0), (t1, s1), (t2, s2)):
            hot = one_hot(t[:, pl.ds(512, LANES)].astype(F32))
            s[...] = dot(hot, field[...], ((1,), (1,))).astype(BF16)

    return body


def spread_last(q_count, tiles):
    def body(phi, low, high, kap, kap_low, kap_high, out, wide, middle, final):
        two_sweeps(phi, low, high, kap, kap_low, kap_high, wide, middle, final, q_count)
        from_octants(final, out, tables_out(), tiles)

    return body


def shards(state, material, occupied, brick_column, brick_octant):
    e = state.shape[-1]
    n_blk, n_grp = lax.axis_size("blk"), lax.axis_size("grp")
    solvent, groups = n_grp - 1, range(n_grp - 1)
    cap = max(2, 2 * e // n_blk)
    slots = n_blk * cap
    tiles = 6 * e // LANES
    q_count = 6 * e // 8
    axes = ("grp", "blk")
    grp = lax.axis_index("grp").astype(jnp.int32)
    grp_at = grp.reshape(1)
    is_solvent = grp == solvent
    current = state.reshape(1536, e)
    mat = material.reshape(1536, e)
    occ = occupied.astype(F32).reshape(1, e)
    col = brick_column.reshape(1, e)
    octant = brick_octant.reshape(e, 1)
    field_shape, layers = (512, 4 * LANES), (16, 64, 2 * LANES)

    def pairs(back, g):
        forth = [(g * n_blk + b, solvent * n_blk + b) for b in range(n_blk)]
        return [(j, i) for i, j in forth] if back else forth

    def planes(up, which):
        steps = [(b, b + 1) for b in range(n_blk - 1)]
        steps = steps if up else [(j, i) for i, j in steps]
        return [(g * n_blk + i, g * n_blk + j) for g in which for i, j in steps]

    def both_ways(up, down, which):
        return (
            lax.ppermute(up, axes, planes(True, which)),
            lax.ppermute(down, axes, planes(False, which)),
        )

    def swap(block):
        return lax.all_to_all(block, "blk", split_axis=0, concat_axis=0, tiled=True)

    send, sel, field, phi, kap, up, down = call(
        prepare(n_blk, cap, tiles, solvent),
        (grp_at, current, mat, occ, col, octant),
        (
            shape_of((slots, 512 + LANES), BF16),
            shape_of((slots, e), BF16),
            shape_of(field_shape, BF16),
            shape_of(layers),
            shape_of(layers),
            shape_of((200, e)),
            shape_of((200, e)),
        ),
        [pltpu.VMEM((512, e), BF16)],
        smem=1,
        name="prepare",
    )
    recv = swap(send)
    fields = [lax.ppermute(field, axes, pairs(True, g)) for g in groups]
    side_low, side_high = both_ways(up, down, range(n_grp))
    arrived = [lax.ppermute(recv, axes, pairs(False, g)) for g in groups]
    halo = shape_of((256, LANES))
    rows = shape_of((slots, 512), BF16)
    flat = shape_of((1536, e))
    work = [pltpu.VMEM((512, e), F32), pltpu.VMEM((1536, e), F32), pltpu.VMEM((1536, e), F32)]
    wide = [pltpu.VMEM((20,) + layers[1:], F32), pltpu.VMEM((18,) + layers[1:], F32)]

    def solvent_first(_):
        added, up, down = call(
            deposit(True),
            (phi, *arrived, *arrived),
            (shape_of(layers), halo, halo),
            name="deposit_first",
        )
        low, high = both_ways(up, down, [solvent])
        spread, s0, s1, s2 = call(
            spread_first(q_count),
            (added, low, high, kap, side_low, side_high, *arrived),
            (shape_of(layers), rows, rows, rows),
            wide + [pltpu.VMEM(field_shape, BF16)],
            name="spread_first",
        )
        return spread.reshape(2048, LANES), s0, s1, s2, jnp.zeros(halo.shape), jnp.zeros(halo.shape)

    def mech_first(_):
        mine = call(gather_field, (grp_at, recv, *fields), rows, smem=1, name="gather")
        mine = swap(mine)
        face = shape_of((256, e))
        moved, send, up, down = call(
            first_step,
            (current, mat, occ, sel, mine, side_low, side_high),
            (shape_of((2048, e)), rows, face, face),
            work + [pltpu.VMEM((512, e), BF16)],
            name="first_step",
        )
        recv_next = swap(send)
        return moved, recv_next, recv_next, recv_next, up, down

    moved, out0, out1, out2, up, down = lax.cond(is_solvent, solvent_first, mech_first, 0)
    back = [
        lax.ppermute(block, axes, pairs(False, g) + pairs(True, g))
        for g, block in zip(groups, (out0, out1, out2))
    ]

    def solvent_last(_):
        added, up, down = call(
            deposit(False),
            (moved.reshape(layers), *back, *arrived),
            (shape_of(layers), halo, halo),
            name="deposit_last",
        )
        low, high = both_ways(up, down, [solvent])
        return call(
            spread_last(q_count, tiles),
            (added, low, high, kap, side_low, side_high),
            flat,
            wide + [pltpu.VMEM(layers, F32)],
            name="spread_last",
        )

    def mech_last(_):
        mine = swap(back[0] + back[1] + back[2])
        low, high = both_ways(up, down, groups)
        return call(
            last_step,
            (moved, mat, occ, sel, mine, low, high, side_low, side_high),
            flat,
            work,
            name="last_step",
        )

    return lax.cond(is_solvent, solvent_last, mech_last, 0).reshape(state.shape)


def solution(mesh):
    in_specs = (
        P("grp", None, None, "blk"),
        P("grp", None, None, "blk"),
        P(("grp", "blk")),
        P(("grp", "blk"), None),
        P(("grp", "blk")),
    )
    out_specs = P("grp", None, None, "blk")
    return jax.shard_map(shards, mesh=mesh, in_specs=in_specs, out_specs=out_specs, check_vma=False)
```

profile of v0, /device:TPU:21, one launch (start us, length us, event | category | flops | bytes accessed | tf_op | source)
XLA Modules:
  0.0 111.0 jit_solution(17422999456707888518)
XLA Ops:
  2.1 8.2 %prepare.1 = (bf16[256,640]{1,0:T(8,128)(2,1)}, bf16[256,128]{1,0:T(8,128)(2,1)}, bf16[512,512]{1,0:T(8,128)(2,1)}, f32[16,64,256]{2,1,0:T(8,128)}, f32[16,64,25...) custom-call(s32[1]{0:T(128)} %bitcast.8.grp, f32[1536,128]{1,0:T(8,128)} %bitcast.20, ...), custom_call_target="tpu_custom_call" | custom-call | tf_op jit(solution)/shard_map/prepare/pallas_call | solution.py:28
  10.2 5.7 %all-to-all-start.3 = ((bf16[8,32,640]{2,1,0:T(8,128)(2,1)}), bf16[8,32,640]{2,1,0:T(8,128)(2,1)}, u32[]{:S(2)}, u32[]{:S(2)}) async-start(bf16[8,32,640]{2,1,0:T(8,128)(2,1)} %bitcast.28), calls=%async_computation.3 | async-start | bytes 655360 | tf_op jit(solution)/shard_map/all_to_all | solution.py:458
  17.3 2.1 %collective-permute-start.7 = (bf16[512,512]{1,0:T(8,128)(2,1)}, bf16[512,512]{1,0:T(8,128)(2,1)}, u32[]{:S(2)}, u32[]{:S(2)}) collective-permute-start(bf16[512,512]{1,0:T(8,128)(2,1)} %get-tuple-element.154), channel_id=1, source_target_pairs={{24,8},{25,9},{26,10},{27,11},{28,12},{29,13},{30,14},{31,15}} | collective-permute-start | bytes 1572872 | tf_op jit(solution)/shard_map/ppermute | solution.py:477
  19.4 2.1 %collective-permute-start.6 = (bf16[512,512]{1,0:T(8,128)(2,1)}, bf16[512,512]{1,0:T(8,128)(2,1)}, u32[]{:S(2)}, u32[]{:S(2)}) collective-permute-start(bf16[512,512]{1,0:T(8,128)(2,1)} %get-tuple-element.154), channel_id=1, source_target_pairs={{24,0},{25,1},{26,2},{27,3},{28,4},{29,5},{30,6},{31,7}} | collective-permute-start | bytes 1572872 | tf_op jit(solution)/shard_map/ppermute | solution.py:477
  21.5 3.1 %collective-permute-start.9 = (f32[200,128]{1,0:T(8,128)S(1)}, f32[200,128]{1,0:T(8,128)S(1)}, u32[]{:S(2)}, u32[]{:S(2)}) collective-permute-start(f32[200,128]{1,0:T(8,128)S(1)} %copy-done.15), channel_id=1, source_target_pairs={{0,1},{1,2},{2,3},{3,4},{4,5},{5,6},{6,7},{8,9},{9,10},{10,11},{11... | collective-permute-start | bytes 307208 | tf_op jit(solution)/shard_map/ppermute | solution.py:453
  24.6 3.1 %collective-permute-start.10 = (f32[200,128]{1,0:T(8,128)S(1)}, f32[200,128]{1,0:T(8,128)S(1)}, u32[]{:S(2)}, u32[]{:S(2)}) collective-permute-start(f32[200,128]{1,0:T(8,128)S(1)} %copy-done.14), channel_id=1, source_target_pairs={{1,0},{2,1},{3,2},{4,3},{5,4},{6,5},{7,6},{9,8},{10,9},{11,10},{12... | collective-permute-start | bytes 307208 | tf_op jit(solution)/shard_map/ppermute | solution.py:454
  32.6 7.0 %collective-permute-done.12 = bf16[256,640]{1,0:T(8,128)(2,1)S(1)} collective-permute-done((bf16[256,640]{1,0:T(8,128)(2,1)}, bf16[256,640]{1,0:T(8,128)(2,1)S(1)}, u32[]{:S(2)}, u32[]{:S(2)}) %collective-permute-start.12) | collective-permute-done | bytes 327712 | tf_op jit(solution)/shard_map/ppermute | solution.py:479
  39.6 2.3 %collective-permute-done.11 = bf16[256,640]{1,0:T(8,128)(2,1)S(1)} collective-permute-done((bf16[256,640]{1,0:T(8,128)(2,1)}, bf16[256,640]{1,0:T(8,128)(2,1)S(1)}, u32[]{:S(2)}, u32[]{:S(2)}) %collective-permute-start.11) | collective-permute-done | bytes 327712 | tf_op jit(solution)/shard_map/ppermute | solution.py:479
  41.9 23.1 %conditional.2 = (f32[2048,128]{1,0:T(8,128)}, bf16[256,512]{1,0:T(8,128)(2,1)S(1)}, bf16[256,512]{1,0:T(8,128)(2,1)}, bf16[256,512]{1,0:T(8,128)(2,1)}, f32[256,128]{1,0:T(8,128)S(1)}, /*index=5*/f32[256,128]{1,0:T(8,128)}) conditional(s32[]{:T(128)} %convert_element_type.7, (s32[1]{0:T(128)}, bf16[256,640]{1,0:T(8,128)(2,1)}, ...), branch_computations={%region_0.0_spmd, %region_1.0_spmd} | conditional | bytes 4456640 | solution.py:517
  41.9 2.9 %deposit_first.1 = (f32[16,64,256]{2,1,0:T(8,128)}, f32[256,128]{1,0:T(8,128)}, f32[256,128]{1,0:T(8,128)}) custom-call(f32[16,64,256]{2,1,0:T(8,128)} %get-tuple-element.102.phi, bf16[256,640]{1,0:T(8,128)(2,1)S(1)} %get-tuple-element.103.refs_0_.refs_3_.t0, bf16[256,640]{1,0:T(8,128)(2,1)S(1)} %get-tuple-element.104.refs_1_.refs_4_.t1, ...), custom_call_target="tpu_custom_call" | custom-call | tf_op jit(solution)/shard_map/cond/branch_1_fun/deposit_first/pallas_call | solution.py:28
  44.8 4.0 %collective-permute-start = (f32[256,128]{1,0:T(8,128)}, f32[256,128]{1,0:T(8,128)S(1)}, u32[]{:S(2)}, u32[]{:S(2)}) collective-permute-start(f32[256,128]{1,0:T(8,128)} %get-tuple-element.107), channel_id=1, source_target_pairs={{24,25},{25,26},{26,27},{27,28},{28,29},{29,30},{30,31}} | collective-permute-start | bytes 393224 | tf_op jit(solution)/shard_map/cond/branch_1_fun/ppermute | solution.py:453
  48.8 2.2 %collective-permute-start.1 = (f32[256,128]{1,0:T(8,128)}, f32[256,128]{1,0:T(8,128)S(1)}, u32[]{:S(2)}, u32[]{:S(2)}) collective-permute-start(f32[256,128]{1,0:T(8,128)} %get-tuple-element.108), channel_id=1, source_target_pairs={{25,24},{26,25},{27,26},{28,27},{29,28},{30,29},{31,30}} | collective-permute-start | bytes 393224 | tf_op jit(solution)/shard_map/cond/branch_1_fun/ppermute | solution.py:454
  51.6 3.1 %collective-permute-done.1.high = f32[256,128]{1,0:T(8,128)S(1)} collective-permute-done((f32[256,128]{1,0:T(8,128)}, f32[256,128]{1,0:T(8,128)S(1)}, u32[]{:S(2)}, u32[]{:S(2)}) %collective-permute-start.1) | collective-permute-done | bytes 131104 | tf_op jit(solution)/shard_map/cond/branch_1_fun/ppermute | solution.py:454
  55.3 6.7 %spread_first.1 = (f32[16,64,256]{2,1,0:T(8,128)}, bf16[256,512]{1,0:T(8,128)(2,1)S(1)}, bf16[256,512]{1,0:T(8,128)(2,1)}, bf16[256,512]{1,0:T(8,128)(2,1)}) custom-call(f32[16,64,256]{2,1,0:T(8,128)} %get-tuple-element.106.phi, f32[256,128]{1,0:T(8,128)} %copy-done.4, f32[256,128]{1,0:T(8,128)} %copy-done.5, f32[16,64,256]{2,1,0:T(8,128)S(1)} %get-tuple-element.109.kap, ...), custom_call_target="tpu_custom_call" | custom-call | tf_op jit(solution)/shard_map/cond/branch_1_fun/spread_first/pallas_call | solution.py:28
  62.1 2.3 %reshape.29 = f32[2048,128]{1,0:T(8,128)} reshape(f32[16,64,256]{2,1,0:T(8,128)} %get-tuple-element.112) | data formatting | bytes 2097152 | tf_op jit(solution)/shard_map/cond/branch_1_fun/reshape | solution.py:501
  65.7 11.2 %collective-permute-start.14 = (bf16[256,512]{1,0:T(8,128)(2,1)S(1)}, bf16[256,512]{1,0:T(8,128)(2,1)S(1)}, u32[]{:S(2)}, u32[]{:S(2)}) collective-permute-start(bf16[256,512]{1,0:T(8,128)(2,1)S(1)} %get-tuple-element.160), channel_id=1, source_target_pairs={{0,24},{1,25},{2,26},{3,27},{4,28},{5,29},{6,30},{7,31},{24,0},{25... | collective-permute-start | bytes 786440 | tf_op jit(solution)/shard_map/ppermute | solution.py:519
  81.0 3.4 %collective-permute-done.15 = bf16[256,512]{1,0:T(8,128)(2,1)} collective-permute-done((bf16[256,512]{1,0:T(8,128)(2,1)}, bf16[256,512]{1,0:T(8,128)(2,1)}, u32[]{:S(2)}, u32[]{:S(2)}) %collective-permute-start.15) | collective-permute-done | bytes 262176 | tf_op jit(solution)/shard_map/ppermute | solution.py:519
  84.4 26.7 %conditional.3 = (f32[1,3,512,128]{3,2,1,0:T(8,128)}) conditional(s32[]{:T(128)} %convert_element_type.7, (bf16[256,512]{1,0:T(8,128)(2,1)S(1)}, bf16[256,512]{1,0:T(8,128)(2,1)}, bf16[256,512]{1,0:T(8,128)(2,1)}, f32[256,128]{1,0:T(8,128)}, f32[256,128]{1,0:T(8,128)}, /*index=5*/f32[2048,128]{1,0:T(8,128)}, f32[1536,128]{1,0:T(8,128)S(1)}, ...), branch_computations={%region_2.0_spmd, %region_3.0_spmd} | conditional | flops 262144 | bytes 6291744 | solution.py:550
  84.4 2.5 %reshape.31.phi = f32[16,64,256]{2,1,0:T(8,128)} reshape(f32[2048,128]{1,0:T(8,128)} %get-tuple-element.127) | data formatting | bytes 2097152 | tf_op jit(solution)/shard_map/cond/branch_1_fun/reshape | solution.py:526
  86.9 3.0 %deposit_last.1 = (f32[16,64,256]{2,1,0:T(8,128)}, f32[256,128]{1,0:T(8,128)}, f32[256,128]{1,0:T(8,128)}) custom-call(f32[16,64,256]{2,1,0:T(8,128)} %reshape.31.phi, bf16[256,512]{1,0:T(8,128)(2,1)S(1)} %get-tuple-element.128.refs_0_, bf16[256,512]{1,0:T(8,128)(2,1)} %get-tuple-element.129.refs_1_, bf16[256,512]{1,0:T(8,128)(2,1)} %get-tuple-element.130.refs_2_, ...), custom_call_target="tpu_custom_call" | custom-call | tf_op jit(solution)/shard_map/cond/branch_1_fun/deposit_last/pallas_call | solution.py:28
  91.8 4.3 %collective-permute-start.3 = (f32[256,128]{1,0:T(8,128)}, f32[256,128]{1,0:T(8,128)S(1)}, u32[]{:S(2)}, u32[]{:S(2)}) collective-permute-start(f32[256,128]{1,0:T(8,128)} %get-tuple-element.136), channel_id=1, source_target_pairs={{25,24},{26,25},{27,26},{28,27},{29,28},{30,29},{31,30}} | collective-permute-start | bytes 393224 | tf_op jit(solution)/shard_map/cond/branch_1_fun/ppermute | solution.py:454
  96.1 2.4 %collective-permute-done.2.low = f32[256,128]{1,0:T(8,128)S(1)} collective-permute-done((f32[256,128]{1,0:T(8,128)}, f32[256,128]{1,0:T(8,128)S(1)}, u32[]{:S(2)}, u32[]{:S(2)}) %collective-permute-start.2) | collective-permute-done | bytes 131104 | tf_op jit(solution)/shard_map/cond/branch_1_fun/ppermute | solution.py:453
  98.4 3.1 %collective-permute-done.3.high = f32[256,128]{1,0:T(8,128)S(1)} collective-permute-done((f32[256,128]{1,0:T(8,128)}, f32[256,128]{1,0:T(8,128)S(1)}, u32[]{:S(2)}, u32[]{:S(2)}) %collective-permute-start.3) | collective-permute-done | bytes 131104 | tf_op jit(solution)/shard_map/cond/branch_1_fun/ppermute | solution.py:454
  102.2 8.8 %spread_last.1 = f32[1536,128]{1,0:T(8,128)} custom-call(f32[16,64,256]{2,1,0:T(8,128)} %get-tuple-element.134.phi, f32[256,128]{1,0:T(8,128)} %copy-done.7, f32[256,128]{1,0:T(8,128)} %copy-done.9, f32[16,64,256]{2,1,0:T(8,128)S(1)} %get-tuple-element.137.kap, f32[200,128]{1,0:T(8,128)S(1)} %get-tuple-element.138.kap_low, ...), custom_call_target="tpu_custom_call" | custom-call | tf_op jit(solution)/shard_map/cond/branch_1_fun/spread_last/pallas_call | solution.py:28
  (41 shorter events, 17.5 us)
Async XLA Ops:
  2.1 39.9 %copy-start = (f32[1,3,512,128]{3,2,1,0:T(8,128)S(1)}, f32[1,3,512,128]{3,2,1,0:T(8,128)}, u32[]{:S(2)}) copy-start(f32[1,3,512,128]{3,2,1,0:T(8,128)} %param.10) | copy-start | bytes 2359300
  10.2 11.2 %copy-start.15 = (f32[200,128]{1,0:T(8,128)S(1)}, f32[200,128]{1,0:T(8,128)}, u32[]{:S(2)}) copy-start(f32[200,128]{1,0:T(8,128)} %get-tuple-element.156) | copy-start | bytes 307204
  10.2 14.3 %copy-start.14 = (f32[200,128]{1,0:T(8,128)S(1)}, f32[200,128]{1,0:T(8,128)}, u32[]{:S(2)}) copy-start(f32[200,128]{1,0:T(8,128)} %get-tuple-element.157) | copy-start | bytes 307204
  10.2 17.5 %all-to-all-start.3 = ((bf16[8,32,640]{2,1,0:T(8,128)(2,1)}), bf16[8,32,640]{2,1,0:T(8,128)(2,1)}, u32[]{:S(2)}, u32[]{:S(2)}) async-start(bf16[8,32,640]{2,1,0:T(8,128)(2,1)} %bitcast.28), calls=%async_computation.3 | async-start | bytes 655360 | tf_op jit(solution)/shard_map/all_to_all | solution.py:458
  16.0 15.3 %collective-permute-start.8 = (bf16[512,512]{1,0:T(8,128)(2,1)}, bf16[512,512]{1,0:T(8,128)(2,1)S(1)}, u32[]{:S(2)}, u32[]{:S(2)}) collective-permute-start(bf16[512,512]{1,0:T(8,128)(2,1)} %get-tuple-element.154), channel_id=1, source_target_pairs={{24,16},{25,17},{26,18},{27,19},{28,20},{29,21},{30,22},{31,23}} | collective-permute-start | bytes 1572872 | tf_op jit(solution)/shard_map/ppermute | solution.py:477
  17.3 15.3 %collective-permute-start.7 = (bf16[512,512]{1,0:T(8,128)(2,1)}, bf16[512,512]{1,0:T(8,128)(2,1)}, u32[]{:S(2)}, u32[]{:S(2)}) collective-permute-start(bf16[512,512]{1,0:T(8,128)(2,1)} %get-tuple-element.154), channel_id=1, source_target_pairs={{24,8},{25,9},{26,10},{27,11},{28,12},{29,13},{30,14},{31,15}} | collective-permute-start | bytes 1572872 | tf_op jit(solution)/shard_map/ppermute | solution.py:477
  19.4 13.2 %collective-permute-start.6 = (bf16[512,512]{1,0:T(8,128)(2,1)}, bf16[512,512]{1,0:T(8,128)(2,1)}, u32[]{:S(2)}, u32[]{:S(2)}) collective-permute-start(bf16[512,512]{1,0:T(8,128)(2,1)} %get-tuple-element.154), channel_id=1, source_target_pairs={{24,0},{25,1},{26,2},{27,3},{28,4},{29,5},{30,6},{31,7}} | collective-permute-start | bytes 1572872 | tf_op jit(solution)/shard_map/ppermute | solution.py:477
  21.5 6.3 %collective-permute-start.9 = (f32[200,128]{1,0:T(8,128)S(1)}, f32[200,128]{1,0:T(8,128)S(1)}, u32[]{:S(2)}, u32[]{:S(2)}) collective-permute-start(f32[200,128]{1,0:T(8,128)S(1)} %copy-done.15), channel_id=1, source_target_pairs={{0,1},{1,2},{2,3},{3,4},{4,5},{5,6},{6,7},{8,9},{9,10},{10,11},{11... | collective-permute-start | bytes 307208 | tf_op jit(solution)/shard_map/ppermute | solution.py:453
  24.6 5.4 %collective-permute-start.10 = (f32[200,128]{1,0:T(8,128)S(1)}, f32[200,128]{1,0:T(8,128)S(1)}, u32[]{:S(2)}, u32[]{:S(2)}) collective-permute-start(f32[200,128]{1,0:T(8,128)S(1)} %copy-done.14), channel_id=1, source_target_pairs={{1,0},{2,1},{3,2},{4,3},{5,4},{6,5},{7,6},{9,8},{10,9},{11,10},{12... | collective-permute-start | bytes 307208 | tf_op jit(solution)/shard_map/ppermute | solution.py:454
  27.8 4.8 %collective-permute-start.13 = (bf16[256,640]{1,0:T(8,128)(2,1)}, bf16[256,640]{1,0:T(8,128)(2,1)S(1)}, u32[]{:S(2)}, u32[]{:S(2)}) collective-permute-start(bf16[256,640]{1,0:T(8,128)(2,1)} %bitcast.15), channel_id=1, source_target_pairs={{16,24},{17,25},{18,26},{19,27},{20,28},{21,29},{22,30},{23,31}} | collective-permute-start | bytes 983048 | tf_op jit(solution)/shard_map/ppermute | solution.py:479
  30.0 9.6 %collective-permute-start.12 = (bf16[256,640]{1,0:T(8,128)(2,1)}, bf16[256,640]{1,0:T(8,128)(2,1)S(1)}, u32[]{:S(2)}, u32[]{:S(2)}) collective-permute-start(bf16[256,640]{1,0:T(8,128)(2,1)} %bitcast.15), channel_id=1, source_target_pairs={{8,24},{9,25},{10,26},{11,27},{12,28},{13,29},{14,30},{15,31}} | collective-permute-start | bytes 983048 | tf_op jit(solution)/shard_map/ppermute | solution.py:479
  31.3 10.6 %collective-permute-start.11 = (bf16[256,640]{1,0:T(8,128)(2,1)}, bf16[256,640]{1,0:T(8,128)(2,1)S(1)}, u32[]{:S(2)}, u32[]{:S(2)}) collective-permute-start(bf16[256,640]{1,0:T(8,128)(2,1)} %bitcast.15), channel_id=1, source_target_pairs={{0,24},{1,25},{2,26},{3,27},{4,28},{5,29},{6,30},{7,31}} | collective-permute-start | bytes 983048 | tf_op jit(solution)/shard_map/ppermute | solution.py:479
  44.8 6.8 %collective-permute-start = (f32[256,128]{1,0:T(8,128)}, f32[256,128]{1,0:T(8,128)S(1)}, u32[]{:S(2)}, u32[]{:S(2)}) collective-permute-start(f32[256,128]{1,0:T(8,128)} %get-tuple-element.107), channel_id=1, source_target_pairs={{24,25},{25,26},{26,27},{27,28},{28,29},{29,30},{30,31}} | collective-permute-start | bytes 393224 | tf_op jit(solution)/shard_map/cond/branch_1_fun/ppermute | solution.py:453
  48.8 5.9 %collective-permute-start.1 = (f32[256,128]{1,0:T(8,128)}, f32[256,128]{1,0:T(8,128)S(1)}, u32[]{:S(2)}, u32[]{:S(2)}) collective-permute-start(f32[256,128]{1,0:T(8,128)} %get-tuple-element.108), channel_id=1, source_target_pairs={{25,24},{26,25},{27,26},{28,27},{29,28},{30,29},{31,30}} | collective-permute-start | bytes 393224 | tf_op jit(solution)/shard_map/cond/branch_1_fun/ppermute | solution.py:454
  51.6 3.1 %copy-start.4 = (f32[256,128]{1,0:T(8,128)}, f32[256,128]{1,0:T(8,128)S(1)}, u32[]{:S(2)}) copy-start(f32[256,128]{1,0:T(8,128)S(1)} %collective-permute-done.low) | copy-start | bytes 393220 | tf_op jit(solution)/shard_map/cond
  54.7 0.7 copy-start.5
  65.0 0.7 copy-start.11
  65.7 15.3 %collective-permute-start.14 = (bf16[256,512]{1,0:T(8,128)(2,1)S(1)}, bf16[256,512]{1,0:T(8,128)(2,1)S(1)}, u32[]{:S(2)}, u32[]{:S(2)}) collective-permute-start(bf16[256,512]{1,0:T(8,128)(2,1)S(1)} %get-tuple-element.160), channel_id=1, source_target_pairs={{0,24},{1,25},{2,26},{3,27},{4,28},{5,29},{6,30},{7,31},{24,0},{25... | collective-permute-start | bytes 786440 | tf_op jit(solution)/shard_map/ppermute | solution.py:519
  77.0 7.4 %collective-permute-start.15 = (bf16[256,512]{1,0:T(8,128)(2,1)}, bf16[256,512]{1,0:T(8,128)(2,1)}, u32[]{:S(2)}, u32[]{:S(2)}) collective-permute-start(bf16[256,512]{1,0:T(8,128)(2,1)} %get-tuple-element.161), channel_id=1, source_target_pairs={{8,24},{9,25},{10,26},{11,27},{12,28},{13,29},{14,30},{15,31},{24,... | collective-permute-start | bytes 786440 | tf_op jit(solution)/shard_map/ppermute | solution.py:519
  78.9 5.5 %collective-permute-start.16 = (bf16[256,512]{1,0:T(8,128)(2,1)}, bf16[256,512]{1,0:T(8,128)(2,1)}, u32[]{:S(2)}, u32[]{:S(2)}) collective-permute-start(bf16[256,512]{1,0:T(8,128)(2,1)} %get-tuple-element.162), channel_id=1, source_target_pairs={{16,24},{17,25},{18,26},{19,27},{20,28},{21,29},{22,30},{23,31},{2... | collective-permute-start | bytes 786440 | tf_op jit(solution)/shard_map/ppermute | solution.py:519
  89.9 8.5 %collective-permute-start.2 = (f32[256,128]{1,0:T(8,128)}, f32[256,128]{1,0:T(8,128)S(1)}, u32[]{:S(2)}, u32[]{:S(2)}) collective-permute-start(f32[256,128]{1,0:T(8,128)} %get-tuple-element.135), channel_id=1, source_target_pairs={{24,25},{25,26},{26,27},{27,28},{28,29},{29,30},{30,31}} | collective-permute-start | bytes 393224 | tf_op jit(solution)/shard_map/cond/branch_1_fun/ppermute | solution.py:453
  91.8 9.8 %collective-permute-start.3 = (f32[256,128]{1,0:T(8,128)}, f32[256,128]{1,0:T(8,128)S(1)}, u32[]{:S(2)}, u32[]{:S(2)}) collective-permute-start(f32[256,128]{1,0:T(8,128)} %get-tuple-element.136), channel_id=1, source_target_pairs={{25,24},{26,25},{27,26},{28,27},{29,28},{30,29},{31,30}} | collective-permute-start | bytes 393224 | tf_op jit(solution)/shard_map/cond/branch_1_fun/ppermute | solution.py:454
  98.4 3.1 %copy-start.7 = (f32[256,128]{1,0:T(8,128)}, f32[256,128]{1,0:T(8,128)S(1)}, u32[]{:S(2)}) copy-start(f32[256,128]{1,0:T(8,128)S(1)} %collective-permute-done.2.low) | copy-start | bytes 393220 | tf_op jit(solution)/shard_map/cond
  101.6 0.7 copy-start.9
  (2 other events, 1.3 us)
where the time goes:
time: 112 us; the launch traced here: 111 us
  starting transfers between devices  48.7 us (43%)
  Pallas kernels  29.6 us (26%)
  waiting for transfers between devices  23.1 us (21%)
  local copies, waits for them, and re-layouts  9.49 us (8%)
    pallas_call x5, Pallas kernels, call(): pl.pallas_call(body, out_shape=outs, in_specs=[SMEM] * smem + [VMEM] * (l...  29.6 us
    ppermute x3, starting transfers between devices, shards(): lax.ppermute(block, axes, pairs(False, g) + pairs(True, g))  15.1 us
    ppermute x3, starting transfers between devices, both_ways(): lax.ppermute(down, axes, planes(False, which))  9.54 us
    ppermute x3, waiting for transfers between devices, shards(): arrived = [lax.ppermute(recv, axes, pairs(False, g)) for g in groups]  9.29 us
    ppermute x3, starting transfers between devices, both_ways(): lax.ppermute(up, axes, planes(True, which))  8.96 us
    ppermute x3, waiting for transfers between devices, both_ways(): lax.ppermute(down, axes, planes(False, which))  7.14 us
    all_to_all x1, starting transfers between devices, swap(): return lax.all_to_all(block, 'blk', split_axis=0, concat_axis=0, tiled=True)  5.71 us
    ppermute x3, starting transfers between devices, shards(): fields = [lax.ppermute(field, axes, pairs(True, g)) for g in groups]  5.51 us
  transfers between devices with their start and end apart: 16, of which 10 were waited for; matrix products, arithmetic and copies ran while one was open for 0% of the time, Pallas kernels for 0%

commit v1 on v0

--- a/solution.py
+++ b/solution.py
@@ -18,19 +18,22 @@
 F32, BF16 = jnp.float32, jnp.bfloat16
 VMEM = pl.BlockSpec(memory_space=pltpu.VMEM)
 SMEM = pl.BlockSpec(memory_space=pltpu.SMEM)
+ANY = pl.BlockSpec(memory_space=pl.ANY)
 
 
 def shape_of(shape, dtype=F32):
     return jax.ShapeDtypeStruct(shape, dtype)
 
 
-def call(body, args, outs, scratch=(), smem=0, name=None):
+def call(body, args, outs, scratch=(), smem=0, name=None, away=(), unused=(), alias=None):
+    specs = [SMEM] * smem + [VMEM] * (len(args) - smem)
     return pl.pallas_call(
         body,
         out_shape=outs,
-        in_specs=[SMEM] * smem + [VMEM] * (len(args) - smem),
-        out_specs=jax.tree.map(lambda _: VMEM, outs),
+        in_specs=[ANY if n in away else spec for n, spec in enumerate(specs)],
+        out_specs=tuple(ANY if n in unused else VMEM for n in range(len(outs))),
         scratch_shapes=list(scratch),
+        input_output_aliases=alias or {},
         name=name,
     )(*args)
 
@@ -201,67 +204,60 @@
     )
 
 
+def layer_to_octants(chunk, scale, tables, tiles):
+    rows = chunk.shape[0]
+    lane = iota((8, LANES), 1)
+    parts = []
+    for y in range(16):
+        part = chunk[tiles * y : min(tiles * y + 8, rows)]
+        if part.shape[0] < 8:
+            pad = jnp.zeros((8 - part.shape[0], LANES), F32)
+            part = jnp.concatenate([part, pad], axis=0)
+        part = permute_in(part, tables)
+        parts.append(jnp.where(lane < 16 * tiles, part, 0.0))
+    layer = jnp.concatenate(parts, axis=0)
+    return layer * scale if scale != 1.0 else layer
+
+
 def to_octants(ref, out, scale, tables, tiles):
     rows = 16 * tiles
-    lane = iota((8, LANES), 1)
 
     def layer(x, carry):
         chunk = ref[pl.ds(pl.multiple_of(x * rows, 8), rows), :]
-        for y in range(16):
-            part = chunk[tiles * y : min(tiles * y + 8, rows)]
-            if part.shape[0] < 8:
-                pad = jnp.zeros((8 - part.shape[0], LANES), F32)
-                part = jnp.concatenate([part, pad], axis=0)
-            part = permute_in(part, tables)
-            part = jnp.where(lane < 16 * tiles, part, 0.0)
-            if scale != 1.0:
-                part = part * scale
-            out[x, pl.ds(8 * (y % 8), 8), pl.ds(LANES * (y // 8), LANES)] = part
+        out[layer_rows(x), :] = layer_to_octants(chunk, scale, tables, tiles)
         return carry
 
     lax.fori_loop(0, 16, layer, 0)
 
 
-def from_octants(ref, out, tables, tiles):
-    rows = 16 * tiles
-
-    def layer(x, carry):
-        parts = []
-        for y in range(16):
-            part = ref[x, pl.ds(8 * (y % 8), 8), pl.ds(LANES * (y // 8), LANES)]
-            parts.append(permute_in(part, tables)[:tiles])
-        out[pl.ds(pl.multiple_of(x * rows, 8), rows), :] = jnp.concatenate(parts, axis=0)
-        return carry
-
-    lax.fori_loop(0, 16, layer, 0)
-
-
-def put_pressures(ref, out):
-    for x in range(16):
-        i, ox = x % 8, x // 8
-        f = ref[x]
-        f = f + CUBIC_TERM * f * f * f
-        out[pl.ds(64 * i, 64), pl.ds(256 * ox, 256)] = f.astype(BF16)
-
-
-def one_hot(tile):
+def layer_from_octants(layer, tables, tiles):
     return jnp.concatenate(
-        [jnp.where(tile == float(o + 1), 1.0, 0.0).astype(BF16) for o in range(4)], axis=1
+        [permute_in(layer[8 * y : 8 * y + 8], tables)[:tiles] for y in range(16)], axis=0
     )
 
 
-def pieces(array):
-    return [array[8 * n : 8 * n + 8] for n in range(8)]
-
-
-def sweep(read, kap, masks):
-    low, here, high = read
+def layer_rows(x):
+    return pl.ds(pl.multiple_of(x * LANES, LANES), LANES)
+
+
+def pressures(layer):
+    return (layer + CUBIC_TERM * layer * layer * layer).astype(BF16)
+
+
+def one_hot(tile, width):
+    return jnp.concatenate(
+        [jnp.where(tile == float(o + 1), 1.0, 0.0).astype(BF16)[:, :width] for o in range(4)],
+        axis=1,
+    )
+
+
+def sweep(below, here, above, kap, masks):
     inner, outer, last, first = masks
-    halves = [[v[:, LANES * o : LANES * (o + 1)].reshape(8, 8, LANES) for v in (low, here, high)] for o in range(2)]
+    halves = [v.reshape(2, 8, 8, LANES) for v in (below, here, above, kap)]
     out = []
     for o in range(2):
-        below, c, above = halves[o]
-        twin = halves[1 - o][1]
+        low, c, high, rate = (v[o] for v in halves)
+        twin = halves[1][1 - o]
         if o == 0:
             y_above = jnp.concatenate([c[1:], twin[0:1]], axis=0)
             y_below = jnp.concatenate([c[0:1], c[:-1]], axis=0)
@@ -274,52 +270,64 @@
         z_below = jnp.where(outer, r, jnp.where(first, c, pltpu.roll(r, 1, 2)))
         base = 1.0 + c * c
         inflow = None
-        for n in (above, below, y_above, y_below, z_above, z_below):
+        for n in (high, low, y_above, y_below, z_above, z_below):
             part = (base + n * n) * (n - c)
             inflow = part if inflow is None else inflow + part
-        out.append((c + kap[o] * inflow).reshape(64, LANES))
-    return jnp.concatenate(out, axis=1)
-
-
-def halves_of(ref, n):
-    return jnp.concatenate(
-        [ref[pl.ds(128 * n, 64), :], ref[pl.ds(128 * n + 64, 64), :]], axis=1
-    )
-
-
-def two_sweeps(phi, low, high, kap, kap_low, kap_high, wide, middle, out, q_count):
+        out.append((c + rate * inflow).reshape(64, LANES))
+    return jnp.concatenate(out, axis=0)
+
+
+def sweep_masks(q_count):
     k, lane = iota((8, 8, LANES), 1), iota((8, 8, LANES), 2)
-    masks = (k < 7, k > 0, lane == q_count - 1, lane == 0)
-    for n in range(2):
-        wide[n] = halves_of(low, n)
-        wide[18 + n] = halves_of(high, n)
-    wide[pl.ds(2, 16)] = phi[...]
-
-    def split(layer):
-        return [layer[:, LANES * o : LANES * (o + 1)].reshape(8, 8, LANES) for o in range(2)]
+    return k < 7, k > 0, lane == q_count - 1, lane == 0
+
+
+def inner_sweeps(phi, kap, middle, edges, put, q_count):
+    masks = sweep_masks(q_count)
 
     def around(ref, x):
-        return ref[x - 1], ref[x], ref[x + 1]
-
-    middle[0] = sweep(around(wide, 1), split(halves_of(kap_low, 0)), masks)
-    middle[17] = sweep(around(wide, 18), split(halves_of(kap_high, 0)), masks)
+        return ref[layer_rows(x - 1), :], ref[layer_rows(x), :], ref[layer_rows(x + 1), :]
 
     def first(x, carry):
-        middle[x + 1] = sweep(around(wide, x + 2), split(kap[x]), masks)
+        middle[layer_rows(x), :] = sweep(*around(phi, x), kap[layer_rows(x), :], masks)
         return carry
 
-    lax.fori_loop(0, 16, first, 0)
-
     def second(x, carry):
-        out[x] = sweep(around(middle, x + 1), split(kap[x]), masks)
+        put(x, sweep(*around(middle, x), kap[layer_rows(x), :], masks))
         return carry
 
-    lax.fori_loop(0, 16, second, 0)
+    lax.fori_loop(1, 15, first, 0)
+    for n, x in enumerate((1, 2, 13, 14)):
+        edges[layer_rows(n), :] = middle[layer_rows(x), :]
+    lax.fori_loop(2, 14, second, 0)
+
+
+def edge_sweeps(top, bottom, low, high, kap_edge, kap_low, kap_high, middle, q_count):
+    masks = sweep_masks(q_count)
+
+    def of(ref, n):
+        return ref[LANES * n : LANES * (n + 1), :]
+
+    k = [of(kap_edge, n) for n in range(4)]
+    far_low, near_low, a, b = of(low, 0), of(low, 1), of(bottom, 0), of(bottom, 1)
+    c, d, near_high, far_high = of(top, 0), of(top, 1), of(high, 0), of(high, 1)
+    m = [of(middle, n) for n in range(4)]
+    before = sweep(far_low, near_low, a, of(kap_low, 0), masks)
+    zero = sweep(near_low, a, b, k[0], masks)
+    last = sweep(c, d, near_high, k[3], masks)
+    after = sweep(d, near_high, far_high, of(kap_high, 0), masks)
+    return [
+        sweep(before, zero, m[0], k[0], masks),
+        sweep(zero, m[0], m[1], k[1], masks),
+        sweep(m[2], m[3], last, k[2], masks),
+        sweep(m[3], last, after, k[3], masks),
+    ]
 
 
 def prepare(n_blk, cap, tiles, solvent):
-    def body(grp, state, mat, occ, col, octant, send, sel, field, phi, kap, up, down, dil):
+    def body(grp, state, mat, occ, col, octant, send, sel, field, phi, up, down, dil, edge, sem):
         e = state.shape[-1]
+        quarter, rows = 16 * tiles, 16 * tiles
 
         @pl.when(grp[0] != solvent)
         def _():
@@ -334,11 +342,10 @@
             sel[...] = chosen
             send[:, pl.ds(0, 512)] = dot(chosen, dil[...], ((1,), (1,))).astype(BF16)
             o = octant[...]
-            quarter = 16 * tiles
             block = sum((jnp.where(o >= n * quarter, 1, 0) for n in range(1, 4)))
             spot = o - quarter * block
-            tile = jnp.where(iota((e, LANES), 1) == spot, (block + 1).astype(F32), 0.0)
-            tile = dot(chosen, tile.astype(BF16), ((1,), (0,)))
+            tile = jnp.where(iota((LANES, e), 0) == spot, (block + 1).astype(F32), 0.0)
+            tile = dot(chosen, tile.astype(BF16), ((1,), (1,)))
             send[:, pl.ds(512, LANES)] = tile.astype(BF16)
             put_faces(state, up, down)
             up[pl.ds(192, 8), :] = jnp.broadcast_to(occ[...], (8, e))
@@ -346,22 +353,45 @@
 
         @pl.when(grp[0] == solvent)
         def _():
+            copies = [
+                pltpu.make_async_copy(mat.at[pl.ds(rows * x, rows)], edge.at[n], sem.at[n])
+                for n, x in enumerate((0, 15))
+            ]
+            for copy in copies:
+                copy.start()
             tables = tables_in()
             to_octants(state, phi, 1.0, tables, tiles)
-            put_pressures(phi, field)
-            to_octants(mat, kap, 0.5 * SWEEP_STEP, tables, tiles)
-            for o in range(2):
-                rows, lanes = pl.ds(64 * o, 64), pl.ds(LANES * o, LANES)
-                up[rows, :] = kap[15, :, lanes]
-                down[rows, :] = kap[0, :, lanes]
-
-    return body
-
-
-def gather_field(grp, recv, f0, f1, f2, out):
-    g = grp[0]
-    field = jnp.where(g == 0, f0[...], jnp.where(g == 1, f1[...], f2[...]))
-    out[...] = dot(one_hot(recv[:, pl.ds(512, LANES)].astype(F32)), field, ((1,), (1,))).astype(BF16)
+            for i in range(8):
+                parts = []
+                for ox in range(2):
+                    for oy in range(2):
+                        p = pressures(phi[pl.ds(LANES * (8 * ox + i) + 64 * oy, 64), :])
+                        parts.append(p[:, :quarter])
+                field[pl.ds(64 * i, 64), :] = jnp.concatenate(parts, axis=1)
+            for copy in copies:
+                copy.wait()
+            for n, ref in enumerate((down, up)):
+                layer = layer_to_octants(edge[n], 0.5 * SWEEP_STEP, tables, tiles)
+                ref[pl.ds(0, LANES), :] = layer
+
+    return body
+
+
+def rates(tiles):
+    def body(mat, kap, edge, *unused):
+        to_octants(mat, kap, 0.5 * SWEEP_STEP, tables_in(), tiles)
+        for n, x in enumerate((0, 1, 14, 15)):
+            edge[layer_rows(n), :] = kap[layer_rows(x), :]
+
+    return body
+
+
+def gather_field(quarter):
+    def body(recv, field, out):
+        hot = one_hot(recv[:, pl.ds(512, LANES)].astype(F32), quarter)
+        out[...] = dot(hot, field[...], ((1,), (1,))).astype(BF16)
+
+    return body
 
 
 def first_step(state, mat, occ, sel, recv, low, high, out, send, up, down, *scratch):
@@ -380,42 +410,99 @@
     advance(state, mat, filled, recv, sel, low, high, fills, out, *scratch)
 
 
-def deposit(with_hot):
+def deposit(edged):
     def body(phi, *refs):
+        edge = refs[0] if edged else None
+        refs = refs[1:] if edged else refs
         values, tiles = refs[:3], refs[3:6]
         out, up, down = refs[6:]
         total = None
         for v, t in zip(values, tiles):
-            hot = one_hot(t[:, pl.ds(t.shape[-1] - LANES, LANES)].astype(F32))
+            hot = one_hot(t[:, pl.ds(512, LANES)].astype(F32), LANES)
             part = dot(v[:, pl.ds(0, 512)], hot, ((0,), (0,)))
             total = part if total is None else total + part
         for x in range(16):
             i, ox = x % 8, x // 8
-            layer = phi[x] + (SWEEP_STEP * SOURCE_RATE) * total[64 * i : 64 * i + 64, 256 * ox : 256 * ox + 256]
-            out[x] = layer
-            for base, ref in ((14, up), (0, down)):
-                if base <= x < base + 2:
-                    for o in range(2):
-                        ref[pl.ds(128 * (x - base) + 64 * o, 64), :] = layer[:, LANES * o : LANES * (o + 1)]
-
-    return body
-
-
-def spread_first(q_count):
-    def body(phi, low, high, kap, kap_low, kap_high, t0, t1, t2, out, s0, s1, s2, wide, middle, field):
-        two_sweeps(phi, low, high, kap, kap_low, kap_high, wide, middle, out, q_count)
-        put_pressures(out, field)
+            if edged and x in (0, 1, 14, 15):
+                layer = edge[layer_rows((0, 1, 14, 15).index(x)), :]
+            else:
+                layer = phi[layer_rows(x), :]
+            added = jnp.concatenate(
+                [
+                    total[64 * i : 64 * i + 64, 256 * ox + LANES * o : 256 * ox + LANES * (o + 1)]
+                    for o in range(2)
+                ],
+                axis=0,
+            )
+            layer = layer + (SWEEP_STEP * SOURCE_RATE) * added
+            out[layer_rows(x), :] = layer
+            if x < 2:
+                down[layer_rows(x), :] = layer
+            if x >= 14:
+                up[layer_rows(x - 14), :] = layer
+
+    return body
+
+
+def inner_first(q_count):
+    def body(phi, kap, out, edges, middle):
+        def put(x, layer):
+            out[layer_rows(x), :] = layer
+
+        inner_sweeps(phi, kap, middle, edges, put, q_count)
+
+    return body
+
+
+def outer_first(q_count):
+    def body(up, down, low, high, kap_edge, kap_low, kap_high, mid, phi, t0, t1, t2, edge, s0, s1, s2, field):
+        final = edge_sweeps(up, down, low, high, kap_edge, kap_low, kap_high, mid, q_count)
+        for n in range(4):
+            edge[layer_rows(n), :] = final[n]
+        for x in range(16):
+            i, ox = x % 8, x // 8
+            layer = final[(0, 1, 14, 15).index(x)] if x in (0, 1, 14, 15) else phi[layer_rows(x), :]
+            p = pressures(layer)
+            for o in range(2):
+                field[pl.ds(64 * i, 64), pl.ds(256 * ox + LANES * o, LANES)] = p[64 * o : 64 * o + 64]
         for t, s in ((t0, s0), (t1, s1), (t2, s2)):
-            hot = one_hot(t[:, pl.ds(512, LANES)].astype(F32))
+            hot = one_hot(t[:, pl.ds(512, LANES)].astype(F32), LANES)
             s[...] = dot(hot, field[...], ((1,), (1,))).astype(BF16)
 
     return body
 
 
-def spread_last(q_count, tiles):
-    def body(phi, low, high, kap, kap_low, kap_high, out, wide, middle, final):
-        two_sweeps(phi, low, high, kap, kap_low, kap_high, wide, middle, final, q_count)
-        from_octants(final, out, tables_out(), tiles)
+def inner_last(q_count, tiles):
+    def body(phi, kap, out, edges, middle):
+        tables = tables_out()
+        rows = 16 * tiles
+
+        def put(x, layer):
+            spot = pl.ds(pl.multiple_of(x * rows, 8), rows)
+            out[spot, :] = layer_from_octants(layer, tables, tiles)
+
+        inner_sweeps(phi, kap, middle, edges, put, q_count)
+
+    return body
+
+
+def outer_last(q_count, tiles):
+    def body(up, down, low, high, kap_edge, kap_low, kap_high, mid, _, out, ends, sem):
+        final = edge_sweeps(up, down, low, high, kap_edge, kap_low, kap_high, mid, q_count)
+        tables = tables_out()
+        rows = 16 * tiles
+        for n in range(4):
+            ends[pl.ds(rows * n, rows), :] = layer_from_octants(final[n], tables, tiles)
+        copies = [
+            pltpu.make_async_copy(
+                ends.at[pl.ds(2 * rows * n, 2 * rows)], out.at[pl.ds(start, 2 * rows)], sem.at[n]
+            )
+            for n, start in enumerate((0, 14 * rows))
+        ]
+        for copy in copies:
+            copy.start()
+        for copy in copies:
+            copy.wait()
 
     return body
 
@@ -431,13 +518,13 @@
     axes = ("grp", "blk")
     grp = lax.axis_index("grp").astype(jnp.int32)
     grp_at = grp.reshape(1)
-    is_solvent = grp == solvent
     current = state.reshape(1536, e)
     mat = material.reshape(1536, e)
     occ = occupied.astype(F32).reshape(1, e)
     col = brick_column.reshape(1, e)
-    octant = brick_octant.reshape(e, 1)
-    field_shape, layers = (512, 4 * LANES), (16, 64, 2 * LANES)
+    octant = brick_octant.reshape(1, e)
+    layers, ends, halo = shape_of((2048, LANES)), shape_of((512, LANES)), shape_of((256, LANES))
+    rows, flat, face = shape_of((slots, 512), BF16), shape_of((1536, e)), shape_of((256, e))
 
     def pairs(back, g):
         forth = [(g * n_blk + b, solvent * n_blk + b) for b in range(n_blk)]
@@ -457,97 +544,135 @@
     def swap(block):
         return lax.all_to_all(block, "blk", split_axis=0, concat_axis=0, tiled=True)
 
-    send, sel, field, phi, kap, up, down = call(
+    send, sel, field, phi, up, down = call(
         prepare(n_blk, cap, tiles, solvent),
         (grp_at, current, mat, occ, col, octant),
         (
             shape_of((slots, 512 + LANES), BF16),
             shape_of((slots, e), BF16),
-            shape_of(field_shape, BF16),
-            shape_of(layers),
-            shape_of(layers),
+            shape_of((512, 4 * q_count), BF16),
+            layers,
             shape_of((200, e)),
             shape_of((200, e)),
         ),
-        [pltpu.VMEM((512, e), BF16)],
+        [
+            pltpu.VMEM((512, e), BF16),
+            pltpu.VMEM((2, 16 * tiles, LANES), F32),
+            pltpu.SemaphoreType.DMA((2,)),
+        ],
         smem=1,
+        away=(2,),
         name="prepare",
     )
     recv = swap(send)
     fields = [lax.ppermute(field, axes, pairs(True, g)) for g in groups]
     side_low, side_high = both_ways(up, down, range(n_grp))
     arrived = [lax.ppermute(recv, axes, pairs(False, g)) for g in groups]
-    halo = shape_of((256, LANES))
-    rows = shape_of((slots, 512), BF16)
-    flat = shape_of((1536, e))
     work = [pltpu.VMEM((512, e), F32), pltpu.VMEM((1536, e), F32), pltpu.VMEM((1536, e), F32)]
-    wide = [pltpu.VMEM((20,) + layers[1:], F32), pltpu.VMEM((18,) + layers[1:], F32)]
-
-    def solvent_first(_):
-        added, up, down = call(
-            deposit(True),
-            (phi, *arrived, *arrived),
-            (shape_of(layers), halo, halo),
-            name="deposit_first",
+    middle = pltpu.VMEM(layers.shape, F32)
+
+    def solvent_rates():
+        outs = (layers, ends, rows, face, face)
+        kap, edge, dummy, up, down = call(rates(tiles), (mat,), outs, unused=(2, 3, 4), name="rates")
+        return kap, edge, dummy, up, down
+
+    def mech_first(g):
+        def run():
+            (mine,) = call(gather_field(q_count), (recv, fields[g]), (rows,), name="gather")
+            mine = swap(mine)
+            moved, send, up, down, spare = call(
+                lambda *refs: first_step(*refs[:11], *refs[12:]),
+                (current, mat, occ, sel, mine, side_low, side_high),
+                (shape_of((2048, e)), rows, face, face, ends),
+                work + [pltpu.VMEM((512, e), BF16)],
+                unused=(4,),
+                name="first_step",
+            )
+            return moved, spare, send, up, down
+
+        return run
+
+    branches = [mech_first(g) for g in groups] + [solvent_rates]
+    moved, kap_edge, send, up, down = lax.switch(grp, branches)
+    face_low, face_high = both_ways(up, down, groups)
+
+    def solvent_first():
+        added, top, bottom = call(
+            deposit(False), (phi, *arrived, *arrived), (layers, halo, halo), name="deposit_first"
         )
-        low, high = both_ways(up, down, [solvent])
-        spread, s0, s1, s2 = call(
-            spread_first(q_count),
-            (added, low, high, kap, side_low, side_high, *arrived),
-            (shape_of(layers), rows, rows, rows),
-            wide + [pltpu.VMEM(field_shape, BF16)],
-            name="spread_first",
+        low, high = both_ways(top, bottom, [solvent])
+        inner, mid = call(
+            inner_first(q_count), (added, moved), (layers, ends), [middle], name="inner_first"
         )
-        return spread.reshape(2048, LANES), s0, s1, s2, jnp.zeros(halo.shape), jnp.zeros(halo.shape)
-
-    def mech_first(_):
-        mine = call(gather_field, (grp_at, recv, *fields), rows, smem=1, name="gather")
-        mine = swap(mine)
-        face = shape_of((256, e))
-        moved, send, up, down = call(
-            first_step,
-            (current, mat, occ, sel, mine, side_low, side_high),
-            (shape_of((2048, e)), rows, face, face),
-            work + [pltpu.VMEM((512, e), BF16)],
-            name="first_step",
+        edge, s0, s1, s2 = call(
+            outer_first(q_count),
+            (top, bottom, low, high, kap_edge, side_low, side_high, mid, inner, *arrived),
+            (ends, rows, rows, rows),
+            [pltpu.VMEM((512, 4 * LANES), BF16)],
+            name="outer_first",
         )
-        recv_next = swap(send)
-        return moved, recv_next, recv_next, recv_next, up, down
-
-    moved, out0, out1, out2, up, down = lax.cond(is_solvent, solvent_first, mech_first, 0)
+        return inner, edge, s0, s1, s2
+
+    def mech_turn(g):
+        def run():
+            mine = swap(send)
+            spare = call(
+                lambda *refs: None,
+                (),
+                (layers, ends, rows, rows),
+                unused=(0, 1, 2, 3),
+                name="spare",
+            )
+            blocks = list(spare[2:])
+            blocks.insert(g, mine)
+            return spare[0], spare[1], *blocks
+
+        return run
+
+    inner, edge, *blocks = lax.switch(grp, [mech_turn(g) for g in groups] + [solvent_first])
     back = [
         lax.ppermute(block, axes, pairs(False, g) + pairs(True, g))
-        for g, block in zip(groups, (out0, out1, out2))
+        for g, block in zip(groups, blocks)
     ]
 
-    def solvent_last(_):
-        added, up, down = call(
-            deposit(False),
-            (moved.reshape(layers), *back, *arrived),
-            (shape_of(layers), halo, halo),
+    def solvent_last():
+        added, top, bottom = call(
+            deposit(True),
+            (inner, edge, *back, *arrived),
+            (layers, halo, halo),
             name="deposit_last",
         )
-        low, high = both_ways(up, down, [solvent])
-        return call(
-            spread_last(q_count, tiles),
-            (added, low, high, kap, side_low, side_high),
-            flat,
-            wide + [pltpu.VMEM(layers, F32)],
-            name="spread_last",
+        low, high = both_ways(top, bottom, [solvent])
+        out, mid = call(
+            inner_last(q_count, tiles), (added, moved), (flat, ends), [middle], name="inner_last"
         )
-
-    def mech_last(_):
-        mine = swap(back[0] + back[1] + back[2])
-        low, high = both_ways(up, down, groups)
-        return call(
-            last_step,
-            (moved, mat, occ, sel, mine, low, high, side_low, side_high),
-            flat,
-            work,
-            name="last_step",
+        (out,) = call(
+            outer_last(q_count, tiles),
+            (top, bottom, low, high, kap_edge, side_low, side_high, mid, out),
+            (flat,),
+            [pltpu.VMEM((4 * 16 * tiles, LANES), F32), pltpu.SemaphoreType.DMA((2,))],
+            away=(8,),
+            unused=(0,),
+            alias={8: 0},
+            name="outer_last",
         )
-
-    return lax.cond(is_solvent, solvent_last, mech_last, 0).reshape(state.shape)
+        return out
+
+    def mech_last(g):
+        def run():
+            mine = swap(back[g])
+            (out,) = call(
+                last_step,
+                (moved, mat, occ, sel, mine, face_low, face_high, side_low, side_high),
+                (flat,),
+                work,
+                name="last_step",
+            )
+            return out
+
+        return run
+
+    return lax.switch(grp, [mech_last(g) for g in groups] + [solvent_last]).reshape(state.shape)
 
 
 def solution(mesh):

time: 112 us -> 99.6 us (0.89)
  the two profiles are of different devices: /device:TPU:21 before, /device:TPU:0 now
where the time goes in v1:
time: 99.6 us; the launch traced here: 98.7 us
  starting transfers between devices  34 us (34%)
  blocking collectives  29.5 us (30%)
  waiting for transfers between devices  18.8 us (19%)
  Pallas kernels  15.6 us (16%)
    all_to_all x2, blocking collectives, swap(): return lax.all_to_all(block, 'blk', split_axis=0, concat_axis=0, tiled=True)  29.5 us
    pallas_call x5, Pallas kernels, call(): pl.pallas_call(body, out_shape=outs, in_specs=[ANY if n in away else spec...  15.6 us
    all_to_all x2, starting transfers between devices, swap(): return lax.all_to_all(block, 'blk', split_axis=0, concat_axis=0, tiled=True)  11.5 us
    all_to_all x2, waiting for transfers between devices, swap(): return lax.all_to_all(block, 'blk', split_axis=0, concat_axis=0, tiled=True)  11.1 us
    ppermute x3, starting transfers between devices, shards(): arrived = [lax.ppermute(recv, axes, pairs(False, g)) for g in groups]  7.47 us
    ppermute x2, starting transfers between devices, both_ways(): lax.ppermute(up, axes, planes(True, which))  5.83 us
    ppermute x2, waiting for transfers between devices, both_ways(): lax.ppermute(down, axes, planes(False, which))  4.26 us
    ppermute x3, starting transfers between devices, shards(): lax.ppermute(block, axes, pairs(False, g) + pairs(True, g))  3.97 us
  transfers between devices with their start and end apart: 15, of which 5 were waited for; matrix products, arithmetic and copies ran while one was open for 0% of the time, Pallas kernels for 8%

profile of v1, /device:TPU:0, one launch (start us, length us, event | category | flops | bytes accessed | tf_op | source)
XLA Modules:
  0.0 98.7 jit_solution(10572517578098000654)
XLA Ops:
  0.7 3.4 %prepare.1 = (bf16[256,640]{1,0:T(8,128)(2,1)}, bf16[256,128]{1,0:T(8,128)(2,1)S(1)}, bf16[512,384]{1,0:T(8,128)(2,1)}, f32[2048,128]{1,0:T(8,128)}, f32[200,128]{1,0:T(8,128)}, /*index=5*/f32[200,128]{1,0:T(8,128)}) custom-call(s32[1]{0:T(128)} %bitcast.22.grp, f32[1536,128]{1,0:T(8,128)} %bitcast.39, f32[1536,128]{1,0:T(8,128)} %bitcast.31, ...), custom_call_target="tpu_custom_call" | custom-call | tf_op jit(solution)/shard_map/prepare/pallas_call | solution.py:30
  4.1 7.4 %all-to-all-start.9 = ((bf16[8,32,640]{2,1,0:T(8,128)(2,1)}), bf16[8,32,640]{2,1,0:T(8,128)(2,1)}, u32[]{:S(2)}, u32[]{:S(2)}) async-start(bf16[8,32,640]{2,1,0:T(8,128)(2,1)} %bitcast.57), calls=%async_computation.9 | async-start | bytes 655360 | tf_op jit(solution)/shard_map/all_to_all | solution.py:545
  12.2 3.9 %collective-permute-start.5 = (f32[200,128]{1,0:T(8,128)S(1)}, f32[200,128]{1,0:T(8,128)S(1)}, u32[]{:S(2)}, u32[]{:S(2)}) collective-permute-start(f32[200,128]{1,0:T(8,128)S(1)} %copy-done.9), channel_id=1, source_target_pairs={{0,1},{1,2},{2,3},{3,4},{4,5},{5,6},{6,7},{8,9},{9,10},{10,11},{11... | collective-permute-start | bytes 307208 | tf_op jit(solution)/shard_map/ppermute | solution.py:540
  16.2 1.3 %collective-permute-start.6 = (f32[200,128]{1,0:T(8,128)S(1)}, f32[200,128]{1,0:T(8,128)S(1)}, u32[]{:S(2)}, u32[]{:S(2)}) collective-permute-start(f32[200,128]{1,0:T(8,128)S(1)} %copy-done.8), channel_id=1, source_target_pairs={{1,0},{2,1},{3,2},{4,3},{5,4},{6,5},{7,6},{9,8},{10,9},{11,10},{12... | collective-permute-start | bytes 307208 | tf_op jit(solution)/shard_map/ppermute | solution.py:541
  18.2 1.3 %collective-permute-start.4 = (bf16[512,384]{1,0:T(8,128)(2,1)}, bf16[512,384]{1,0:T(8,128)(2,1)}, u32[]{:S(2)}, u32[]{:S(2)}) collective-permute-start(bf16[512,384]{1,0:T(8,128)(2,1)} %get-tuple-element.286), channel_id=1, source_target_pairs={{24,0},{25,1},{26,2},{27,3},{28,4},{29,5},{30,6},{31,7}} | collective-permute-start | bytes 1179656 | tf_op jit(solution)/shard_map/ppermute | solution.py:568
  19.5 2.8 %all-to-all-done.9 = bf16[8,32,640]{2,1,0:T(8,128)(2,1)} async-done(((bf16[8,32,640]{2,1,0:T(8,128)(2,1)}), bf16[8,32,640]{2,1,0:T(8,128)(2,1)}, u32[]{:S(2)}, u32[]{:S(2)}) %all-to-all-start.9) | async-done | bytes 327712 | tf_op jit(solution)/shard_map/all_to_all | solution.py:545
  23.7 6.1 %collective-permute-start.9 = (bf16[256,640]{1,0:T(8,128)(2,1)}, bf16[256,640]{1,0:T(8,128)(2,1)}, u32[]{:S(2)}, u32[]{:S(2)}) collective-permute-start(bf16[256,640]{1,0:T(8,128)(2,1)} %bitcast.29), channel_id=1, source_target_pairs={{0,24},{1,25},{2,26},{3,27},{4,28},{5,29},{6,30},{7,31}} | collective-permute-start | bytes 983048 | tf_op jit(solution)/shard_map/ppermute | solution.py:570
  29.8 1.9 %collective-permute-done.4 = bf16[512,384]{1,0:T(8,128)(2,1)} collective-permute-done((bf16[512,384]{1,0:T(8,128)(2,1)}, bf16[512,384]{1,0:T(8,128)(2,1)}, u32[]{:S(2)}, u32[]{:S(2)}) %collective-permute-start.4) | collective-permute-done | bytes 393248 | tf_op jit(solution)/shard_map/ppermute | solution.py:568
  31.7 22.2 %conditional.3 = ((f32[2048,128]{1,0:T(8,128)S(1)}, f32[512,128]{1,0:T(8,128)}, bf16[256,512]{1,0:T(8,128)(2,1)}, f32[256,128]{1,0:T(8,128)}, f32[256,128]{1,0:T(8,128)})) conditional(s32[]{:T(128)} %clamp.2, (bf16[256,640]{1,0:T(8,128)(2,1)}, bf16[512,384]{1,0:T(8,128)(2,1)}, f32[1536,128]{1,0:T(8,128)S(1)}, ...), branch_computations={%region_0.0_spmd, %region_1.0_spmd, %region_2.0_spmd, %region_3.0_... | conditional | bytes 524336 | solution.py:596
  31.7 2.1 %gather.3 = bf16[256,512]{1,0:T(8,128)(2,1)} custom-call(bf16[256,640]{1,0:T(8,128)(2,1)} %get-tuple-element.161.recv, bf16[512,384]{1,0:T(8,128)(2,1)} %get-tuple-element.162.field), custom_call_target="tpu_custom_call" | custom-call | tf_op jit(solution)/shard_map/cond/branch_0_fun/gather/pallas_call | solution.py:30
  33.9 14.7 %all_to_all.87 = bf16[8,32,512]{2,1,0:T(8,128)(2,1)} all-to-all(bf16[8,32,512]{2,1,0:T(8,128)(2,1)} %bitcast.54), channel_id=1, replica_groups=mesh['grp'=4,'blk'=8] {'blk'}, dimensions={0} | all-to-all | bytes 524288 | tf_op jit(solution)/shard_map/cond/branch_0_fun/all_to_all | solution.py:545
  48.5 5.4 %first_step.3 = (f32[2048,128]{1,0:T(8,128)S(1)}, bf16[256,512]{1,0:T(8,128)(2,1)}, f32[256,128]{1,0:T(8,128)}, f32[256,128]{1,0:T(8,128)}, f32[512,128]{1,0:T(8,128)}) custom-call(f32[1536,128]{1,0:T(8,128)S(1)} %get-tuple-element.157.refs_0_, f32[1536,128]{1,0:T(8,128)S(1)} %get-tuple-element.158.refs_1_, f32[1,128]{1,0:T(1,128)S(1)} %get-tuple-element.159.refs_2_, ...), custom_call_target="tpu_custom_call" | custom-call | tf_op jit(solution)/shard_map/cond/branch_0_fun/first_step/pallas_call | solution.py:30
  53.9 12.3 %conditional.4 = (f32[2048,128]{1,0:T(8,128)}, f32[512,128]{1,0:T(8,128)}, bf16[256,512]{1,0:T(8,128)(2,1)}, bf16[256,512]{1,0:T(8,128)(2,1)}, bf16[256,512]{1,0:T(8,128)(2,1)}) conditional(s32[]{:T(128)} %clamp.2, bf16[256,512]{1,0:T(8,128)(2,1)} %get-tuple-element.290, ...), branch_computations={%region_4.0_spmd, %region_5.0_spmd, %region_6.0_spmd, %region_7.0_... | conditional | bytes 3145932 | solution.py:632
  53.9 4.1 %all-to-all-start.3 = ((bf16[8,32,512]{2,1,0:T(8,128)(2,1)}), bf16[8,32,512]{2,1,0:T(8,128)(2,1)}, u32[]{:S(2)}, u32[]{:S(2)}) async-start(bf16[8,32,512]{2,1,0:T(8,128)(2,1)} %bitcast.43), calls=%async_computation.3 | async-start | bytes 524288 | tf_op jit(solution)/shard_map/cond/branch_0_fun/all_to_all | solution.py:545
  58.0 8.2 %all-to-all-done.3 = bf16[8,32,512]{2,1,0:T(8,128)(2,1)} async-done(((bf16[8,32,512]{2,1,0:T(8,128)(2,1)}), bf16[8,32,512]{2,1,0:T(8,128)(2,1)}, u32[]{:S(2)}, u32[]{:S(2)}) %all-to-all-start.3) | async-done | bytes 262176 | tf_op jit(solution)/shard_map/cond/branch_0_fun/all_to_all | solution.py:545
  66.2 1.9 %collective-permute-start.12 = (bf16[256,512]{1,0:T(8,128)(2,1)}, bf16[256,512]{1,0:T(8,128)(2,1)S(1)}, u32[]{:S(2)}, u32[]{:S(2)}) collective-permute-start(bf16[256,512]{1,0:T(8,128)(2,1)} %get-tuple-element.294), channel_id=1, source_target_pairs={{0,24},{1,25},{2,26},{3,27},{4,28},{5,29},{6,30},{7,31},{24,0},{25... | collective-permute-start | bytes 786440 | tf_op jit(solution)/shard_map/ppermute | solution.py:634
  68.8 1.4 %collective-permute-start.16 = (bf16[256,512]{1,0:T(8,128)(2,1)}, bf16[256,512]{1,0:T(8,128)(2,1)}, u32[]{:S(2)}, u32[]{:S(2)}) collective-permute-start(bf16[256,512]{1,0:T(8,128)(2,1)} %get-tuple-element.298), channel_id=1, source_target_pairs={{16,24},{17,25},{18,26},{19,27},{20,28},{21,29},{22,30},{23,31},{2... | collective-permute-start | bytes 786440 | tf_op jit(solution)/shard_map/ppermute | solution.py:634
  70.2 1.9 %collective-permute-start.13 = (f32[256,128]{1,0:T(8,128)}, f32[256,128]{1,0:T(8,128)S(1)}, u32[]{:S(2)}, u32[]{:S(2)}) collective-permute-start(f32[256,128]{1,0:T(8,128)} %get-tuple-element.295), channel_id=1, source_target_pairs={{0,1},{1,2},{2,3},{3,4},{4,5},{5,6},{6,7},{8,9},{9,10},{10,11},{11... | collective-permute-start | bytes 393224 | tf_op jit(solution)/shard_map/ppermute | solution.py:540
  72.1 1.3 %collective-permute-start.14 = (f32[256,128]{1,0:T(8,128)}, f32[256,128]{1,0:T(8,128)S(1)}, u32[]{:S(2)}, u32[]{:S(2)}) collective-permute-start(f32[256,128]{1,0:T(8,128)} %get-tuple-element.296), channel_id=1, source_target_pairs={{1,0},{2,1},{3,2},{4,3},{5,4},{6,5},{7,6},{9,8},{10,9},{11,10},{12... | collective-permute-start | bytes 393224 | tf_op jit(solution)/shard_map/ppermute | solution.py:541
  73.4 1.5 %collective-permute-done.13 = f32[256,128]{1,0:T(8,128)S(1)} collective-permute-done((f32[256,128]{1,0:T(8,128)}, f32[256,128]{1,0:T(8,128)S(1)}, u32[]{:S(2)}, u32[]{:S(2)}) %collective-permute-start.13) | collective-permute-done | bytes 131104 | tf_op jit(solution)/shard_map/ppermute | solution.py:540
  74.9 4.3 %collective-permute-done.14 = f32[256,128]{1,0:T(8,128)S(1)} collective-permute-done((f32[256,128]{1,0:T(8,128)}, f32[256,128]{1,0:T(8,128)S(1)}, u32[]{:S(2)}, u32[]{:S(2)}) %collective-permute-start.14) | collective-permute-done | bytes 131104 | tf_op jit(solution)/shard_map/ppermute | solution.py:541
  79.2 19.5 %conditional.5 = (f32[1,3,512,128]{3,2,1,0:T(8,128)}) conditional(s32[]{:T(128)} %clamp.2, (bf16[256,512]{1,0:T(8,128)(2,1)S(1)}, f32[2048,128]{1,0:T(8,128)S(1)}, f32[1536,128]{1,0:T(8,128)S(1)}, f32[1,128]{1,0:T(1,128)S(1)}, bf16[256,128]{1,0:T(8,128)(2,1)S(1)}, /*index=5*/f32[256,128]{1,0:T(8,128)S(1)}, ...), branch_computations={%region_8.0_spmd, %region_9.0_spmd, %region_10.0_spmd, %region_11.... | conditional | bytes 3145900 | solution.py:675
  79.2 14.8 %all_to_all.90 = bf16[8,32,512]{2,1,0:T(8,128)(2,1)} all-to-all(bf16[8,32,512]{2,1,0:T(8,128)(2,1)S(1)} %bitcast.46), channel_id=1, replica_groups=mesh['grp'=4,'blk'=8] {'blk'}, dimensions={0} | all-to-all | bytes 524288 | tf_op jit(solution)/shard_map/cond/branch_0_fun/all_to_all | solution.py:545
  94.0 4.7 %last_step.3 = f32[1536,128]{1,0:T(8,128)} custom-call(f32[2048,128]{1,0:T(8,128)S(1)} %get-tuple-element.225.state, f32[1536,128]{1,0:T(8,128)S(1)} %get-tuple-element.226.mat, f32[1,128]{1,0:T(1,128)S(1)} %get-tuple-element.227.occ, bf16[256,128]{1,0:T(8,128)(2,1)S(1)} %get-tuple-element.228.sel, bf16[256,512]{1,0:T(8,128)(2,1)} %bitcast.51, ...), custom_call_target="tpu_custom_call" | custom-call | tf_op jit(solution)/shard_map/cond/branch_0_fun/last_step/pallas_call | solution.py:30
  (27 shorter events, 4.1 us)
Async XLA Ops:
  0.0 0.7 copy-start.10
  0.7 31.0 %copy-start = (f32[1,3,512,128]{3,2,1,0:T(8,128)S(1)}, f32[1,3,512,128]{3,2,1,0:T(8,128)}, u32[]{:S(2)}) copy-start(f32[1,3,512,128]{3,2,1,0:T(8,128)} %param.18) | copy-start | bytes 2359300
  0.7 31.1 %copy-start.1 = (f32[1,3,512,128]{3,2,1,0:T(8,128)S(1)}, f32[1,3,512,128]{3,2,1,0:T(8,128)}, u32[]{:S(2)}) copy-start(f32[1,3,512,128]{3,2,1,0:T(8,128)} %param.17) | copy-start | bytes 2359300
  4.1 8.1 %copy-start.9 = (f32[200,128]{1,0:T(8,128)S(1)}, f32[200,128]{1,0:T(8,128)}, u32[]{:S(2)}) copy-start(f32[200,128]{1,0:T(8,128)} %get-tuple-element.288) | copy-start | bytes 307204
  4.1 12.1 %copy-start.8 = (f32[200,128]{1,0:T(8,128)S(1)}, f32[200,128]{1,0:T(8,128)}, u32[]{:S(2)}) copy-start(f32[200,128]{1,0:T(8,128)} %get-tuple-element.289) | copy-start | bytes 307204
  4.1 18.2 %all-to-all-start.9 = ((bf16[8,32,640]{2,1,0:T(8,128)(2,1)}), bf16[8,32,640]{2,1,0:T(8,128)(2,1)}, u32[]{:S(2)}, u32[]{:S(2)}) async-start(bf16[8,32,640]{2,1,0:T(8,128)(2,1)} %bitcast.57), calls=%async_computation.9 | async-start | bytes 655360 | tf_op jit(solution)/shard_map/all_to_all | solution.py:545
  11.5 12.2 %collective-permute-start.8 = (bf16[512,384]{1,0:T(8,128)(2,1)}, bf16[512,384]{1,0:T(8,128)(2,1)S(1)}, u32[]{:S(2)}, u32[]{:S(2)}) collective-permute-start(bf16[512,384]{1,0:T(8,128)(2,1)} %get-tuple-element.286), channel_id=1, source_target_pairs={{24,16},{25,17},{26,18},{27,19},{28,20},{29,21},{30,22},{31,23}} | collective-permute-start | bytes 1179656 | tf_op jit(solution)/shard_map/ppermute | solution.py:568
  12.2 7.2 %collective-permute-start.5 = (f32[200,128]{1,0:T(8,128)S(1)}, f32[200,128]{1,0:T(8,128)S(1)}, u32[]{:S(2)}, u32[]{:S(2)}) collective-permute-start(f32[200,128]{1,0:T(8,128)S(1)} %copy-done.9), channel_id=1, source_target_pairs={{0,1},{1,2},{2,3},{3,4},{4,5},{5,6},{6,7},{8,9},{9,10},{10,11},{11... | collective-permute-start | bytes 307208 | tf_op jit(solution)/shard_map/ppermute | solution.py:540
  16.2 6.8 %collective-permute-start.6 = (f32[200,128]{1,0:T(8,128)S(1)}, f32[200,128]{1,0:T(8,128)S(1)}, u32[]{:S(2)}, u32[]{:S(2)}) collective-permute-start(f32[200,128]{1,0:T(8,128)S(1)} %copy-done.8), channel_id=1, source_target_pairs={{1,0},{2,1},{3,2},{4,3},{5,4},{6,5},{7,6},{9,8},{10,9},{11,10},{12... | collective-permute-start | bytes 307208 | tf_op jit(solution)/shard_map/ppermute | solution.py:541
  17.5 12.3 %collective-permute-start.7 = (bf16[512,384]{1,0:T(8,128)(2,1)}, bf16[512,384]{1,0:T(8,128)(2,1)S(1)}, u32[]{:S(2)}, u32[]{:S(2)}) collective-permute-start(bf16[512,384]{1,0:T(8,128)(2,1)} %get-tuple-element.286), channel_id=1, source_target_pairs={{24,8},{25,9},{26,10},{27,11},{28,12},{29,13},{30,14},{31,15}} | collective-permute-start | bytes 1179656 | tf_op jit(solution)/shard_map/ppermute | solution.py:568
  18.2 13.6 %collective-permute-start.4 = (bf16[512,384]{1,0:T(8,128)(2,1)}, bf16[512,384]{1,0:T(8,128)(2,1)}, u32[]{:S(2)}, u32[]{:S(2)}) collective-permute-start(bf16[512,384]{1,0:T(8,128)(2,1)} %get-tuple-element.286), channel_id=1, source_target_pairs={{24,0},{25,1},{26,2},{27,3},{28,4},{29,5},{30,6},{31,7}} | collective-permute-start | bytes 1179656 | tf_op jit(solution)/shard_map/ppermute | solution.py:568
  22.3 31.6 %collective-permute-start.11 = (bf16[256,640]{1,0:T(8,128)(2,1)}, bf16[256,640]{1,0:T(8,128)(2,1)S(1)}, u32[]{:S(2)}, u32[]{:S(2)}) collective-permute-start(bf16[256,640]{1,0:T(8,128)(2,1)} %bitcast.29), channel_id=1, source_target_pairs={{16,24},{17,25},{18,26},{19,27},{20,28},{21,29},{22,30},{23,31}} | collective-permute-start | bytes 983048 | tf_op jit(solution)/shard_map/ppermute | solution.py:570
  23.0 30.9 %collective-permute-start.10 = (bf16[256,640]{1,0:T(8,128)(2,1)}, bf16[256,640]{1,0:T(8,128)(2,1)S(1)}, u32[]{:S(2)}, u32[]{:S(2)}) collective-permute-start(bf16[256,640]{1,0:T(8,128)(2,1)} %bitcast.29), channel_id=1, source_target_pairs={{8,24},{9,25},{10,26},{11,27},{12,28},{13,29},{14,30},{15,31}} | collective-permute-start | bytes 983048 | tf_op jit(solution)/shard_map/ppermute | solution.py:570
  23.7 30.2 %collective-permute-start.9 = (bf16[256,640]{1,0:T(8,128)(2,1)}, bf16[256,640]{1,0:T(8,128)(2,1)}, u32[]{:S(2)}, u32[]{:S(2)}) collective-permute-start(bf16[256,640]{1,0:T(8,128)(2,1)} %bitcast.29), channel_id=1, source_target_pairs={{0,24},{1,25},{2,26},{3,27},{4,28},{5,29},{6,30},{7,31}} | collective-permute-start | bytes 983048 | tf_op jit(solution)/shard_map/ppermute | solution.py:570
  53.9 12.3 %all-to-all-start.3 = ((bf16[8,32,512]{2,1,0:T(8,128)(2,1)}), bf16[8,32,512]{2,1,0:T(8,128)(2,1)}, u32[]{:S(2)}, u32[]{:S(2)}) async-start(bf16[8,32,512]{2,1,0:T(8,128)(2,1)} %bitcast.43), calls=%async_computation.3 | async-start | bytes 524288 | tf_op jit(solution)/shard_map/cond/branch_0_fun/all_to_all | solution.py:545
  66.2 13.0 %collective-permute-start.12 = (bf16[256,512]{1,0:T(8,128)(2,1)}, bf16[256,512]{1,0:T(8,128)(2,1)S(1)}, u32[]{:S(2)}, u32[]{:S(2)}) collective-permute-start(bf16[256,512]{1,0:T(8,128)(2,1)} %get-tuple-element.294), channel_id=1, source_target_pairs={{0,24},{1,25},{2,26},{3,27},{4,28},{5,29},{6,30},{7,31},{24,0},{25... | collective-permute-start | bytes 786440 | tf_op jit(solution)/shard_map/ppermute | solution.py:634
  68.1 11.1 %collective-permute-start.15 = (bf16[256,512]{1,0:T(8,128)(2,1)}, bf16[256,512]{1,0:T(8,128)(2,1)S(1)}, u32[]{:S(2)}, u32[]{:S(2)}) collective-permute-start(bf16[256,512]{1,0:T(8,128)(2,1)} %get-tuple-element.297), channel_id=1, source_target_pairs={{8,24},{9,25},{10,26},{11,27},{12,28},{13,29},{14,30},{15,31},{24,... | collective-permute-start | bytes 786440 | tf_op jit(solution)/shard_map/ppermute | solution.py:634
  68.8 10.4 %collective-permute-start.16 = (bf16[256,512]{1,0:T(8,128)(2,1)}, bf16[256,512]{1,0:T(8,128)(2,1)}, u32[]{:S(2)}, u32[]{:S(2)}) collective-permute-start(bf16[256,512]{1,0:T(8,128)(2,1)} %get-tuple-element.298), channel_id=1, source_target_pairs={{16,24},{17,25},{18,26},{19,27},{20,28},{21,29},{22,30},{23,31},{2... | collective-permute-start | bytes 786440 | tf_op jit(solution)/shard_map/ppermute | solution.py:634
  70.2 4.7 %collective-permute-start.13 = (f32[256,128]{1,0:T(8,128)}, f32[256,128]{1,0:T(8,128)S(1)}, u32[]{:S(2)}, u32[]{:S(2)}) collective-permute-start(f32[256,128]{1,0:T(8,128)} %get-tuple-element.295), channel_id=1, source_target_pairs={{0,1},{1,2},{2,3},{3,4},{4,5},{5,6},{6,7},{8,9},{9,10},{10,11},{11... | collective-permute-start | bytes 393224 | tf_op jit(solution)/shard_map/ppermute | solution.py:540
  72.1 7.1 %collective-permute-start.14 = (f32[256,128]{1,0:T(8,128)}, f32[256,128]{1,0:T(8,128)S(1)}, u32[]{:S(2)}, u32[]{:S(2)}) collective-permute-start(f32[256,128]{1,0:T(8,128)} %get-tuple-element.296), channel_id=1, source_target_pairs={{1,0},{2,1},{3,2},{4,3},{5,4},{6,5},{7,6},{9,8},{10,9},{11,10},{12... | collective-permute-start | bytes 393224 | tf_op jit(solution)/shard_map/ppermute | solution.py:541

commit v2 on v1

--- a/solution.py
+++ b/solution.py
@@ -15,6 +15,7 @@
 CUBIC_TERM = 0.3
 
 LANES = 128
+VMEM_LIMIT = 24 << 20
 F32, BF16 = jnp.float32, jnp.bfloat16
 VMEM = pl.BlockSpec(memory_space=pltpu.VMEM)
 SMEM = pl.BlockSpec(memory_space=pltpu.SMEM)
@@ -34,6 +35,7 @@
         out_specs=tuple(ANY if n in unused else VMEM for n in range(len(outs))),
         scratch_shapes=list(scratch),
         input_output_aliases=alias or {},
+        compiler_params=pltpu.CompilerParams(vmem_limit_bytes=VMEM_LIMIT),
         name=name,
     )(*args)
 
@@ -126,9 +128,8 @@
         down[pl.ds(64 * c, 64), :] = ref[pl.ds(c * 512, 64), :]
 
 
-def advance(ref, mat, filled, recv, sel, low, high, fills, out, pressure, stress, partial):
+def elastic(ref, mat, filled, out, stress, partial):
     e = filled.shape[-1]
-    pressure[...] = dot(recv[...], sel[...], ((0,), (0,))) * PRESSURE_SCALE
     for i in range(8):
         g = gradients(ref, i)
         shear, lame = slab(mat, 0, i), slab(mat, 1, i)
@@ -143,28 +144,49 @@
             s[a, a] = shear * diag[a] + volume
             for b in range(a + 1, 3):
                 s[a, b] = s[b, a] = shear * c[a, b]
-        cof = cofactors(g)
-        p = pressure[pl.ds(64 * i, 64), :].reshape(8, 8, e)
         for a in range(3):
-            first = [
-                g[a][0] * s[0, b] + g[a][1] * s[1, b] + g[a][2] * s[2, b] - p * cof[a][b]
-                for b in range(3)
-            ]
+            first = [g[a][0] * s[0, b] + g[a][1] * s[1, b] + g[a][2] * s[2, b] for b in range(3)]
             put_slab(stress, a, i, first[0])
             put_slab(partial, a, i, diff_j(first[1]) + diff_k(first[2]))
+    k = iota((8, 8, e), 1)
+    lane = iota((1, 1, e), 2)
     penalty = PENALTY * UNIT_LENGTH
-    k = iota((8, 8, e), 1)
-    fill_low, fill_high = fills[0].reshape(1, 1, e), fills[1].reshape(1, 1, e)
-    lane = iota((1, 1, e), 2)
     fill_before = jnp.where(lane == 0, 0.0, pltpu.roll(filled, 1, 2)) * penalty
     fill_after = jnp.where(lane == e - 1, 0.0, pltpu.roll(filled, e - 1, 2)) * penalty
     before_scale = jnp.where(k == 0, fill_before, 0.0)
     after_scale = jnp.where(k == 7, fill_after, 0.0)
     for i in range(8):
+        for a in range(3):
+            here = slab(ref, a, i)
+            force = slab(partial, a, i) + diff_i(
+                slab(stress, a, i - 1) if i > 0 else None,
+                slab(stress, a, i),
+                slab(stress, a, i + 1) if i < 7 else None,
+                i,
+            )
+            before = pltpu.roll(pltpu.roll(here, 1, 1), 1, 2)
+            after = pltpu.roll(pltpu.roll(here, 7, 1), e - 1, 2)
+            force = force + before_scale * (before - here) + after_scale * (after - here)
+            put_slab(out, a, i, force)
+
+
+def advance(ref, mat, filled, base, recv, sel, low, high, fills, out, pressure, stress, partial):
+    e = filled.shape[-1]
+    pressure[...] = dot(recv[...], sel[...], ((0,), (0,))) * PRESSURE_SCALE
+    for i in range(8):
+        cof = cofactors(gradients(ref, i))
+        p = pressure[pl.ds(64 * i, 64), :].reshape(8, 8, e)
+        for a in range(3):
+            first = [p * cof[a][b] for b in range(3)]
+            put_slab(stress, a, i, first[0])
+            put_slab(partial, a, i, slab(base, a, i) - (diff_j(first[1]) + diff_k(first[2])))
+    penalty = PENALTY * UNIT_LENGTH
+    fill_low, fill_high = fills[0].reshape(1, 1, e), fills[1].reshape(1, 1, e)
+    for i in range(8):
         rate = (TIME_STEP / UNIT_LENGTH) * slab(mat, 2, i) * filled
         for a in range(3):
             here = slab(ref, a, i)
-            force = slab(partial, a, i) + diff_i(
+            force = slab(partial, a, i) - diff_i(
                 slab(stress, a, i - 1) if i > 0 else None,
                 slab(stress, a, i),
                 slab(stress, a, i + 1) if i < 7 else None,
@@ -176,9 +198,6 @@
             if i == 7:
                 other = high[pl.ds(64 * a, 64), :].reshape(8, 8, e)
                 force = force + penalty * fill_high * (other - here)
-            before = pltpu.roll(pltpu.roll(here, 1, 1), 1, 2)
-            after = pltpu.roll(pltpu.roll(here, 7, 1), e - 1, 2)
-            force = force + before_scale * (before - here) + after_scale * (after - here)
             put_slab(out, a, i, here + rate * force)
 
 
@@ -325,9 +344,9 @@
 
 
 def prepare(n_blk, cap, tiles, solvent):
-    def body(grp, state, mat, occ, col, octant, send, sel, field, phi, up, down, dil, edge, sem):
+    def body(grp, state, occ, col, octant, send, sel, field, phi, up, down, dil):
         e = state.shape[-1]
-        quarter, rows = 16 * tiles, 16 * tiles
+        quarter = 16 * tiles
 
         @pl.when(grp[0] != solvent)
         def _():
@@ -353,12 +372,6 @@
 
         @pl.when(grp[0] == solvent)
         def _():
-            copies = [
-                pltpu.make_async_copy(mat.at[pl.ds(rows * x, rows)], edge.at[n], sem.at[n])
-                for n, x in enumerate((0, 15))
-            ]
-            for copy in copies:
-                copy.start()
             tables = tables_in()
             to_octants(state, phi, 1.0, tables, tiles)
             for i in range(8):
@@ -368,18 +381,15 @@
                         p = pressures(phi[pl.ds(LANES * (8 * ox + i) + 64 * oy, 64), :])
                         parts.append(p[:, :quarter])
                 field[pl.ds(64 * i, 64), :] = jnp.concatenate(parts, axis=1)
-            for copy in copies:
-                copy.wait()
-            for n, ref in enumerate((down, up)):
-                layer = layer_to_octants(edge[n], 0.5 * SWEEP_STEP, tables, tiles)
-                ref[pl.ds(0, LANES), :] = layer
 
     return body
 
 
 def rates(tiles):
-    def body(mat, kap, edge, *unused):
+    def body(mat, kap, edge, up, down, *unused):
         to_octants(mat, kap, 0.5 * SWEEP_STEP, tables_in(), tiles)
+        up[pl.ds(0, LANES), :] = kap[layer_rows(15), :]
+        down[pl.ds(0, LANES), :] = kap[layer_rows(0), :]
         for n, x in enumerate((0, 1, 14, 15)):
             edge[layer_rows(n), :] = kap[layer_rows(x), :]
 
@@ -394,31 +404,42 @@
     return body
 
 
-def first_step(state, mat, occ, sel, recv, low, high, out, send, up, down, *scratch):
+def elastic_forces(state, mat, occ, out, *scratch):
+    elastic(state, mat, occ[...].reshape(1, 1, occ.shape[-1]), out, *scratch)
+
+
+def turn(state, mat, occ, out, *scratch):
+    elastic_forces(state, mat, occ, out, *scratch[-2:])
+
+
+def first_step(state, mat, occ, base, sel, recv, low, high, out, send, up, down, _, *scratch):
     filled = occ[...].reshape(1, 1, occ.shape[-1])
     fills = (low[pl.ds(192, 1), :], high[pl.ds(192, 1), :])
-    advance(state, mat, filled, recv, sel, low, high, fills, out, *scratch[:3])
+    advance(state, mat, filled, base, recv, sel, low, high, fills, out, *scratch[:3])
     dil = scratch[3]
     dilate(out, filled, dil)
     send[...] = dot(sel[...], dil[...], ((1,), (1,))).astype(BF16)
     put_faces(out, up, down)
 
 
-def last_step(state, mat, occ, sel, recv, low, high, fill_low, fill_high, out, *scratch):
+def last_step(state, mat, occ, base, sel, recv, low, high, fill_low, fill_high, out, *scratch):
     filled = occ[...].reshape(1, 1, occ.shape[-1])
     fills = (fill_low[pl.ds(192, 1), :], fill_high[pl.ds(192, 1), :])
-    advance(state, mat, filled, recv, sel, low, high, fills, out, *scratch)
+    advance(state, mat, filled, base, recv, sel, low, high, fills, out, *scratch)
 
 
 def deposit(edged):
     def body(phi, *refs):
-        edge = refs[0] if edged else None
-        refs = refs[1:] if edged else refs
-        values, tiles = refs[:3], refs[3:6]
-        out, up, down = refs[6:]
+        if edged:
+            edge, v0, v1, v2, tile, out, up, down = refs
+        else:
+            v0, v1, v2, out, up, down, tile, _ = refs
         total = None
-        for v, t in zip(values, tiles):
-            hot = one_hot(t[:, pl.ds(512, LANES)].astype(F32), LANES)
+        for n, v in enumerate((v0, v1, v2)):
+            spot = pl.ds(n * v.shape[0], v.shape[0])
+            if not edged:
+                tile[spot, :] = v[:, pl.ds(512, LANES)]
+            hot = one_hot(tile[spot, :].astype(F32), LANES)
             part = dot(v[:, pl.ds(0, 512)], hot, ((0,), (0,)))
             total = part if total is None else total + part
         for x in range(16):
@@ -455,7 +476,7 @@
 
 
 def outer_first(q_count):
-    def body(up, down, low, high, kap_edge, kap_low, kap_high, mid, phi, t0, t1, t2, edge, s0, s1, s2, field):
+    def body(up, down, low, high, kap_edge, kap_low, kap_high, mid, phi, tile, edge, s0, s1, s2, field):
         final = edge_sweeps(up, down, low, high, kap_edge, kap_low, kap_high, mid, q_count)
         for n in range(4):
             edge[layer_rows(n), :] = final[n]
@@ -465,8 +486,9 @@
             p = pressures(layer)
             for o in range(2):
                 field[pl.ds(64 * i, 64), pl.ds(256 * ox + LANES * o, LANES)] = p[64 * o : 64 * o + 64]
-        for t, s in ((t0, s0), (t1, s1), (t2, s2)):
-            hot = one_hot(t[:, pl.ds(512, LANES)].astype(F32), LANES)
+        for n, s in enumerate((s0, s1, s2)):
+            spot = pl.ds(n * s.shape[0], s.shape[0])
+            hot = one_hot(tile[spot, :].astype(F32), LANES)
             s[...] = dot(hot, field[...], ((1,), (1,))).astype(BF16)
 
     return body
@@ -524,7 +546,9 @@
     col = brick_column.reshape(1, e)
     octant = brick_octant.reshape(1, e)
     layers, ends, halo = shape_of((2048, LANES)), shape_of((512, LANES)), shape_of((256, LANES))
-    rows, flat, face = shape_of((slots, 512), BF16), shape_of((1536, e)), shape_of((256, e))
+    rows, flat = shape_of((slots, 512), BF16), shape_of((1536, e))
+    face, side = shape_of((256, e)), shape_of((200, e))
+    tile = shape_of((slots * (n_grp - 1), LANES), BF16)
 
     def pairs(back, g):
         forth = [(g * n_blk + b, solvent * n_blk + b) for b in range(n_blk)]
@@ -546,59 +570,67 @@
 
     send, sel, field, phi, up, down = call(
         prepare(n_blk, cap, tiles, solvent),
-        (grp_at, current, mat, occ, col, octant),
+        (grp_at, current, occ, col, octant),
         (
             shape_of((slots, 512 + LANES), BF16),
             shape_of((slots, e), BF16),
             shape_of((512, 4 * q_count), BF16),
             layers,
-            shape_of((200, e)),
-            shape_of((200, e)),
+            side,
+            side,
         ),
-        [
-            pltpu.VMEM((512, e), BF16),
-            pltpu.VMEM((2, 16 * tiles, LANES), F32),
-            pltpu.SemaphoreType.DMA((2,)),
-        ],
+        [pltpu.VMEM((512, e), BF16)],
         smem=1,
-        away=(2,),
         name="prepare",
     )
     recv = swap(send)
     fields = [lax.ppermute(field, axes, pairs(True, g)) for g in groups]
-    side_low, side_high = both_ways(up, down, range(n_grp))
     arrived = [lax.ppermute(recv, axes, pairs(False, g)) for g in groups]
     work = [pltpu.VMEM((512, e), F32), pltpu.VMEM((1536, e), F32), pltpu.VMEM((1536, e), F32)]
     middle = pltpu.VMEM(layers.shape, F32)
 
     def solvent_rates():
-        outs = (layers, ends, rows, face, face)
-        kap, edge, dummy, up, down = call(rates(tiles), (mat,), outs, unused=(2, 3, 4), name="rates")
-        return kap, edge, dummy, up, down
-
-    def mech_first(g):
+        kap, edge, up, down, *spare = call(
+            rates(tiles),
+            (mat,),
+            (layers, ends, side, side, rows, face, face),
+            unused=(4, 5, 6),
+            name="rates",
+        )
+        return kap, edge, *both_ways(up, down, [solvent]), *spare
+
+    def gathered(g):
         def run():
-            (mine,) = call(gather_field(q_count), (recv, fields[g]), (rows,), name="gather")
-            mine = swap(mine)
-            moved, send, up, down, spare = call(
-                lambda *refs: first_step(*refs[:11], *refs[12:]),
-                (current, mat, occ, sel, mine, side_low, side_high),
-                (shape_of((2048, e)), rows, face, face, ends),
-                work + [pltpu.VMEM((512, e), BF16)],
-                unused=(4,),
-                name="first_step",
-            )
-            return moved, spare, send, up, down
+            return call(gather_field(q_count), (recv, fields[g]), (rows,), name="gather")[0]
 
         return run
 
-    branches = [mech_first(g) for g in groups] + [solvent_rates]
-    moved, kap_edge, send, up, down = lax.switch(grp, branches)
-    face_low, face_high = both_ways(up, down, groups)
+    def mech_first():
+        mine = swap(lax.switch(grp, [gathered(g) for g in groups]))
+        low, high = both_ways(up, down, groups)
+        (base,) = call(elastic_forces, (current, mat, occ), (flat,), work[1:], name="elastic")
+        moved, send, fore, back, spare = call(
+            first_step,
+            (current, mat, occ, base, sel, mine, low, high),
+            (shape_of((2048, e)), rows, face, face, ends),
+            work + [pltpu.VMEM((512, e), BF16)],
+            unused=(4,),
+            name="first_step",
+        )
+        return moved, spare, low, high, send, fore, back
+
+    is_solvent = grp == solvent
+    moved, kap_edge, side_low, side_high, send, fore, aft = lax.cond(
+        is_solvent, solvent_rates, mech_first
+    )
 
     def solvent_first():
-        added, top, bottom = call(
-            deposit(False), (phi, *arrived, *arrived), (layers, halo, halo), name="deposit_first"
+        added, top, bottom, hot, spare = call(
+            deposit(False),
+            (phi, *arrived),
+            (layers, halo, halo, tile, flat),
+            unused=(4,),
+            name="deposit_first",
         )
         low, high = both_ways(top, bottom, [solvent])
         inner, mid = call(
@@ -606,30 +638,33 @@
         )
         edge, s0, s1, s2 = call(
             outer_first(q_count),
-            (top, bottom, low, high, kap_edge, side_low, side_high, mid, inner, *arrived),
+            (top, bottom, low, high, kap_edge, side_low, side_high, mid, inner, hot),
             (ends, rows, rows, rows),
             [pltpu.VMEM((512, 4 * LANES), BF16)],
             name="outer_first",
         )
-        return inner, edge, s0, s1, s2
+        return inner, edge, hot, spare, low, high, s0, s1, s2
 
     def mech_turn(g):
         def run():
             mine = swap(send)
-            spare = call(
-                lambda *refs: None,
-                (),
-                (layers, ends, rows, rows),
-                unused=(0, 1, 2, 3),
-                name="spare",
+            low, high = both_ways(fore, aft, [g])
+            base, *spare = call(
+                turn,
+                (moved, mat, occ),
+                (flat, layers, ends, tile, rows, rows),
+                work[1:],
+                unused=range(1, 6),
+                name="elastic",
             )
-            blocks = list(spare[2:])
+            blocks = list(spare[3:])
             blocks.insert(g, mine)
-            return spare[0], spare[1], *blocks
+            return *spare[:3], base, low, high, *blocks
 
         return run
 
-    inner, edge, *blocks = lax.switch(grp, [mech_turn(g) for g in groups] + [solvent_first])
+    turns = [mech_turn(g) for g in groups] + [solvent_first]
+    inner, edge, hot, base, face_low, face_high, *blocks = lax.switch(grp, turns)
     back = [
         lax.ppermute(block, axes, pairs(False, g) + pairs(True, g))
         for g, block in zip(groups, blocks)
@@ -638,7 +673,7 @@
     def solvent_last():
         added, top, bottom = call(
             deposit(True),
-            (inner, edge, *back, *arrived),
+            (inner, edge, *back, hot),
             (layers, halo, halo),
             name="deposit_last",
         )
@@ -658,21 +693,21 @@
         )
         return out
 
-    def mech_last(g):
-        def run():
-            mine = swap(back[g])
-            (out,) = call(
-                last_step,
-                (moved, mat, occ, sel, mine, face_low, face_high, side_low, side_high),
-                (flat,),
-                work,
-                name="last_step",
-            )
-            return out
-
-        return run
-
-    return lax.switch(grp, [mech_last(g) for g in groups] + [solvent_last]).reshape(state.shape)
+    def swapped(g):
+        return lambda: swap(back[g])
+
+    def mech_last():
+        mine = lax.switch(grp, [swapped(g) for g in groups])
+        (out,) = call(
+            last_step,
+            (moved, mat, occ, base, sel, mine, face_low, face_high, side_low, side_high),
+            (flat,),
+            work,
+            name="last_step",
+        )
+        return out
+
+    return lax.cond(is_solvent, solvent_last, mech_last).reshape(state.shape)
 
 
 def solution(mesh):

time: 99.6 us -> 95.6 us (0.960)
  the two profiles are of different devices: /device:TPU:0 before, /device:TPU:21 now
where the time goes in v2:
time: 95.6 us; the launch traced here: 94.8 us
  starting transfers between devices  54.2 us (57%)
  Pallas kernels  29.1 us (30%)
  waiting for transfers between devices  9.52 us (10%)
  local copies, waits for them, and re-layouts  1.33 us (1%)
    pallas_call x8, Pallas kernels, call(): pl.pallas_call(body, out_shape=outs, in_specs=[ANY if n in away else spec...  29.1 us
    ppermute x3, starting transfers between devices, shards(): lax.ppermute(block, axes, pairs(False, g) + pairs(True, g))  21.5 us
    ppermute x3, starting transfers between devices, both_ways(): lax.ppermute(down, axes, planes(False, which))  10.8 us
    ppermute x3, starting transfers between devices, both_ways(): lax.ppermute(up, axes, planes(True, which))  8.52 us
    all_to_all x1, starting transfers between devices, swap(): return lax.all_to_all(block, 'blk', split_axis=0, concat_axis=0, tiled=True)  5.58 us
    all_to_all x1, waiting for transfers between devices, swap(): return lax.all_to_all(block, 'blk', split_axis=0, concat_axis=0, tiled=True)  4.25 us
    ppermute x3, starting transfers between devices, shards(): fields = [lax.ppermute(field, axes, pairs(True, g)) for g in groups]  3.93 us
    ppermute x3, starting transfers between devices, shards(): arrived = [lax.ppermute(recv, axes, pairs(False, g)) for g in groups]  3.86 us
  transfers between devices with their start and end apart: 16, of which 5 were waited for; matrix products, arithmetic and copies ran while one was open for 0% of the time, Pallas kernels for 13%

profile of v2, /device:TPU:21, one launch (start us, length us, event | category | flops | bytes accessed | tf_op | source)
XLA Modules:
  0.0 94.8 jit_solution(16857434549433615531)
XLA Ops:
  1.3 5.1 %prepare.1 = (bf16[256,640]{1,0:T(8,128)(2,1)}, bf16[256,128]{1,0:T(8,128)(2,1)}, bf16[512,384]{1,0:T(8,128)(2,1)S(1)}, f32[2048,128]{1,0:T(8,128)}, f32[200,128]{1,0:T(8,128)S(1)}, /*index=5*/f32[200,128]{1,0:T(8,128)}) custom-call(s32[1]{0:T(128)} %bitcast.19.grp, f32[1536,128]{1,0:T(8,128)} %bitcast.34, f32[1,128]{1,0:T(1,128)S(1)} %convert_bitcast_fusion.occ, ...), custom_call_target="tpu_custom_call" | custom-call | tf_op jit(solution)/shard_map/prepare/pallas_call | solution.py:31
  6.5 5.6 %all-to-all-start.7 = ((bf16[8,32,640]{2,1,0:T(8,128)(2,1)}), bf16[8,32,640]{2,1,0:T(8,128)(2,1)}, u32[]{:S(2)}, u32[]{:S(2)}) async-start(bf16[8,32,640]{2,1,0:T(8,128)(2,1)} %bitcast.22), calls=%async_computation.7 | async-start | bytes 655360 | tf_op jit(solution)/shard_map/all_to_all | solution.py:569
  16.0 4.2 %all-to-all-done.7 = bf16[8,32,640]{2,1,0:T(8,128)(2,1)} async-done(((bf16[8,32,640]{2,1,0:T(8,128)(2,1)}), bf16[8,32,640]{2,1,0:T(8,128)(2,1)}, u32[]{:S(2)}, u32[]{:S(2)}) %all-to-all-start.7) | async-done | bytes 327712 | tf_op jit(solution)/shard_map/all_to_all | solution.py:569
  24.2 10.7 %conditional.5 = (f32[2048,128]{1,0:T(8,128)S(1)}, f32[512,128]{1,0:T(8,128)S(1)}, f32[200,128]{1,0:T(8,128)}, f32[200,128]{1,0:T(8,128)}, bf16[256,512]{1,0:T(8...) conditional(s32[]{:T(128)} %convert_element_type.7, (f32[1536,128]{1,0:T(8,128)}, f32[1536,128]{1,0:T(8,128)S(1)}, ...), branch_computations={%region_0.0_spmd, %region_4.0_spmd} | conditional | flops 1 | bytes 5013800 | solution.py:623
  24.2 2.7 %rates.1 = (f32[2048,128]{1,0:T(8,128)S(1)}, f32[512,128]{1,0:T(8,128)S(1)}, f32[200,128]{1,0:T(8,128)S(1)}, f32[200,128]{1,0:T(8,128)S(1)}, bf16[256,512]{1,0:T...) custom-call(f32[1536,128]{1,0:T(8,128)S(1)} %mat), custom_call_target="tpu_custom_call" | custom-call | tf_op jit(solution)/shard_map/cond/branch_1_fun/rates/pallas_call | solution.py:31
  26.9 2.5 %collective-permute-start.2 = (f32[200,128]{1,0:T(8,128)S(1)}, f32[200,128]{1,0:T(8,128)}, u32[]{:S(2)}, u32[]{:S(2)}) collective-permute-start(f32[200,128]{1,0:T(8,128)S(1)} %get-tuple-element.177), channel_id=1, source_target_pairs={{24,25},{25,26},{26,27},{27,28},{28,29},{29,30},{30,31}} | collective-permute-start | bytes 307208 | tf_op jit(solution)/shard_map/cond/branch_1_fun/ppermute | solution.py:564
  29.4 3.7 %collective-permute-start.3 = (f32[200,128]{1,0:T(8,128)S(1)}, f32[200,128]{1,0:T(8,128)}, u32[]{:S(2)}, u32[]{:S(2)}) collective-permute-start(f32[200,128]{1,0:T(8,128)S(1)} %get-tuple-element.178), channel_id=1, source_target_pairs={{25,24},{26,25},{27,26},{28,27},{29,28},{30,29},{31,30}} | collective-permute-start | bytes 307208 | tf_op jit(solution)/shard_map/cond/branch_1_fun/ppermute | solution.py:565
  33.3 1.6 %collective-permute-done.3 = f32[200,128]{1,0:T(8,128)} collective-permute-done((f32[200,128]{1,0:T(8,128)S(1)}, f32[200,128]{1,0:T(8,128)}, u32[]{:S(2)}, u32[]{:S(2)}) %collective-permute-start.3) | collective-permute-done | bytes 102432 | tf_op jit(solution)/shard_map/cond/branch_1_fun/ppermute | solution.py:565
  34.9 17.4 %conditional.6 = (f32[2048,128]{1,0:T(8,128)}, f32[512,128]{1,0:T(8,128)S(1)}, bf16[768,128]{1,0:T(8,128)(2,1)}, f32[1536,128]{1,0:T(8,128)}, f32[256,128]{1,0:T...) conditional(s32[]{:T(128)} %clamp.9, ...), branch_computations={%region_5.0_spmd, %region_6.0_spmd, %region_7.0_spmd, %region_8.0_... | conditional | bytes 1835192 | solution.py:667
  35.1 2.4 %deposit_first.1 = (f32[2048,128]{1,0:T(8,128)S(1)}, f32[256,128]{1,0:T(8,128)S(1)}, f32[256,128]{1,0:T(8,128)S(1)}, bf16[768,128]{1,0:T(8,128)(2,1)}, f32[1536,128]{1,0:T(8,128)}) custom-call(f32[2048,128]{1,0:T(8,128)} %get-tuple-element.218.phi, bf16[256,640]{1,0:T(8,128)(2,1)} %get-tuple-element.219.refs_0_, ...), custom_call_target="tpu_custom_call" | custom-call | tf_op jit(solution)/shard_map/cond/branch_3_fun/deposit_first/pallas_call | solution.py:31
  37.6 4.0 %collective-permute-start.10 = (f32[256,128]{1,0:T(8,128)S(1)}, f32[256,128]{1,0:T(8,128)}, u32[]{:S(2)}, u32[]{:S(2)}) collective-permute-start(f32[256,128]{1,0:T(8,128)S(1)} %get-tuple-element.225.up), channel_id=1, source_target_pairs={{24,25},{25,26},{26,27},{27,28},{28,29},{29,30},{30,31}} | collective-permute-start | bytes 393224 | tf_op jit(solution)/shard_map/cond/branch_3_fun/ppermute | solution.py:564
  41.6 3.0 %collective-permute-start.11 = (f32[256,128]{1,0:T(8,128)S(1)}, f32[256,128]{1,0:T(8,128)}, u32[]{:S(2)}, u32[]{:S(2)}) collective-permute-start(f32[256,128]{1,0:T(8,128)S(1)} %get-tuple-element.226.down), channel_id=1, source_target_pairs={{25,24},{26,25},{27,26},{28,27},{29,28},{30,29},{31,30}} | collective-permute-start | bytes 393224 | tf_op jit(solution)/shard_map/cond/branch_3_fun/ppermute | solution.py:565
  44.5 4.1 %inner_first.1 = (f32[2048,128]{1,0:T(8,128)}, f32[512,128]{1,0:T(8,128)S(1)}) custom-call(f32[2048,128]{1,0:T(8,128)S(1)} %get-tuple-element.222.phi, f32[2048,128]{1,0:T(8,128)S(1)} %get-tuple-element.223.kap), custom_call_target="tpu_custom_call" | custom-call | tf_op jit(solution)/shard_map/cond/branch_3_fun/inner_first/pallas_call | solution.py:31
  48.7 3.7 %outer_first.1 = (f32[512,128]{1,0:T(8,128)S(1)}, bf16[256,512]{1,0:T(8,128)(2,1)S(1)}, bf16[256,512]{1,0:T(8,128)(2,1)}, bf16[256,512]{1,0:T(8,128)(2,1)}) custom-call(f32[256,128]{1,0:T(8,128)S(1)} %get-tuple-element.225.up, f32[256,128]{1,0:T(8,128)S(1)} %get-tuple-element.226.down, f32[256,128]{1,0:T(8,128)} %collective-permute-done.10.low, ...), custom_call_target="tpu_custom_call" | custom-call | tf_op jit(solution)/shard_map/cond/branch_3_fun/outer_first/pallas_call | solution.py:31
  52.4 17.7 %collective-permute-start.20 = (bf16[256,512]{1,0:T(8,128)(2,1)S(1)}, bf16[256,512]{1,0:T(8,128)(2,1)S(1)}, u32[]{:S(2)}, u32[]{:S(2)}) collective-permute-start(bf16[256,512]{1,0:T(8,128)(2,1)S(1)} %get-tuple-element.300), channel_id=1, source_target_pairs={{0,24},{1,25},{2,26},{3,27},{4,28},{5,29},{6,30},{7,31},{24,0},{25... | collective-permute-start | bytes 786440 | tf_op jit(solution)/shard_map/ppermute | solution.py:669
  70.1 1.9 %collective-permute-start.21 = (bf16[256,512]{1,0:T(8,128)(2,1)}, bf16[256,512]{1,0:T(8,128)(2,1)S(1)}, u32[]{:S(2)}, u32[]{:S(2)}) collective-permute-start(bf16[256,512]{1,0:T(8,128)(2,1)} %get-tuple-element.301), channel_id=1, source_target_pairs={{8,24},{9,25},{10,26},{11,27},{12,28},{13,29},{14,30},{15,31},{24,... | collective-permute-start | bytes 786440 | tf_op jit(solution)/shard_map/ppermute | solution.py:669
  72.0 1.9 %collective-permute-start.22 = (bf16[256,512]{1,0:T(8,128)(2,1)}, bf16[256,512]{1,0:T(8,128)(2,1)S(1)}, u32[]{:S(2)}, u32[]{:S(2)}) collective-permute-start(bf16[256,512]{1,0:T(8,128)(2,1)} %get-tuple-element.302), channel_id=1, source_target_pairs={{16,24},{17,25},{18,26},{19,27},{20,28},{21,29},{22,30},{23,31},{2... | collective-permute-start | bytes 786440 | tf_op jit(solution)/shard_map/ppermute | solution.py:669
  74.1 3.3 %collective-permute-done.21 = bf16[256,512]{1,0:T(8,128)(2,1)S(1)} collective-permute-done((bf16[256,512]{1,0:T(8,128)(2,1)}, bf16[256,512]{1,0:T(8,128)(2,1)S(1)}, u32[]{:S(2)}, u32[]{:S(2)}) %collective-permute-start.21) | collective-permute-done | bytes 262176 | tf_op jit(solution)/shard_map/ppermute | solution.py:669
  77.4 17.3 %conditional.7 = (f32[1,3,512,128]{3,2,1,0:T(8,128)}) conditional(s32[]{:T(128)} %convert_element_type.7, (s32[]{:T(128)}, bf16[256,512]{1,0:T(8,128)(2,1)S(1)}, bf16[256,512]{1,0:T(8,128)(2,1)S(1)}, bf16[256,512]{1,0:T(8,128)(2,1)S(1)}, f32[2048,128]{1,0:T(8,128)S(1)}, /*index=5*/f32[1536,128]{1,0:T(8,128)S(1)}, f32[1,128]{1,0:T(1,128)S(1)}, ...), branch_computations={%region_9.0_spmd, %region_13.0_spmd} | conditional | flops 1 | bytes 1048664 | solution.py:710
  77.4 1.8 %deposit_last.1 = (f32[2048,128]{1,0:T(8,128)S(1)}, f32[256,128]{1,0:T(8,128)S(1)}, f32[256,128]{1,0:T(8,128)S(1)}) custom-call(f32[2048,128]{1,0:T(8,128)} %get-tuple-element.250.phi, f32[512,128]{1,0:T(8,128)S(1)} %get-tuple-element.251.refs_0_, bf16[256,512]{1,0:T(8,128)(2,1)S(1)} %get-tuple-element.252.refs_1_, ...), custom_call_target="tpu_custom_call" | custom-call | tf_op jit(solution)/shard_map/cond/branch_1_fun/deposit_last/pallas_call | solution.py:31
  79.2 2.1 %collective-permute-start.12 = (f32[256,128]{1,0:T(8,128)S(1)}, f32[256,128]{1,0:T(8,128)S(1)}, u32[]{:S(2)}, u32[]{:S(2)}) collective-permute-start(f32[256,128]{1,0:T(8,128)S(1)} %get-tuple-element.256.up), channel_id=1, source_target_pairs={{24,25},{25,26},{26,27},{27,28},{28,29},{29,30},{30,31}} | collective-permute-start | bytes 393224 | tf_op jit(solution)/shard_map/cond/branch_1_fun/ppermute | solution.py:564
  81.3 4.1 %collective-permute-start.13 = (f32[256,128]{1,0:T(8,128)S(1)}, f32[256,128]{1,0:T(8,128)S(1)}, u32[]{:S(2)}, u32[]{:S(2)}) collective-permute-start(f32[256,128]{1,0:T(8,128)S(1)} %get-tuple-element.257.down), channel_id=1, source_target_pairs={{25,24},{26,25},{27,26},{28,27},{29,28},{30,29},{31,30}} | collective-permute-start | bytes 393224 | tf_op jit(solution)/shard_map/cond/branch_1_fun/ppermute | solution.py:565
  85.4 5.7 %inner_last.1 = (f32[1536,128]{1,0:T(8,128)}, f32[512,128]{1,0:T(8,128)S(1)}) custom-call(f32[2048,128]{1,0:T(8,128)S(1)} %get-tuple-element.261.phi, f32[2048,128]{1,0:T(8,128)S(1)} %get-tuple-element.262.kap), custom_call_target="tpu_custom_call" | custom-call | tf_op jit(solution)/shard_map/cond/branch_1_fun/inner_last/pallas_call | solution.py:31
  91.1 3.5 %outer_last.1 = f32[1536,128]{1,0:T(8,128)} custom-call(f32[256,128]{1,0:T(8,128)S(1)} %get-tuple-element.256.up, f32[256,128]{1,0:T(8,128)S(1)} %get-tuple-element.257.down, f32[256,128]{1,0:T(8,128)S(1)} %collective-permute-done.12.low, f32[256,128]{1,0:T(8,128)S(1)} %collective-permute-done.13.high, ...), custom_call_target="tpu_custom_call", output_to_operand_aliasing={{}: (8, {})} | custom-call | tf_op jit(solution)/shard_map/cond/branch_1_fun/outer_last/pallas_call | solution.py:31
  (30 shorter events, 9.6 us)
Async XLA Ops:
  0.0 0.7 copy-start.6
  0.7 0.7 copy-start
  0.7 0.7 copy-start.1
  0.7 23.5 %copy-start.2 = (f32[1,3,512,128]{3,2,1,0:T(8,128)S(1)}, f32[1,3,512,128]{3,2,1,0:T(8,128)}, u32[]{:S(2)}) copy-start(f32[1,3,512,128]{3,2,1,0:T(8,128)} %param.20) | copy-start | bytes 2359300
  6.5 13.8 %all-to-all-start.7 = ((bf16[8,32,640]{2,1,0:T(8,128)(2,1)}), bf16[8,32,640]{2,1,0:T(8,128)(2,1)}, u32[]{:S(2)}, u32[]{:S(2)}) async-start(bf16[8,32,640]{2,1,0:T(8,128)(2,1)} %bitcast.22), calls=%async_computation.7 | async-start | bytes 655360 | tf_op jit(solution)/shard_map/all_to_all | solution.py:569
  12.1 10.8 %collective-permute-start.16 = (bf16[512,384]{1,0:T(8,128)(2,1)S(1)}, bf16[512,384]{1,0:T(8,128)(2,1)S(1)}, u32[]{:S(2)}, u32[]{:S(2)}) collective-permute-start(bf16[512,384]{1,0:T(8,128)(2,1)S(1)} %get-tuple-element.288), channel_id=1, source_target_pairs={{24,16},{25,17},{26,18},{27,19},{28,20},{29,21},{30,22},{31,23}} | collective-permute-start | bytes 1179656 | tf_op jit(solution)/shard_map/ppermute | solution.py:587
  13.4 10.8 %collective-permute-start.15 = (bf16[512,384]{1,0:T(8,128)(2,1)S(1)}, bf16[512,384]{1,0:T(8,128)(2,1)S(1)}, u32[]{:S(2)}, u32[]{:S(2)}) collective-permute-start(bf16[512,384]{1,0:T(8,128)(2,1)S(1)} %get-tuple-element.288), channel_id=1, source_target_pairs={{24,8},{25,9},{26,10},{27,11},{28,12},{29,13},{30,14},{31,15}} | collective-permute-start | bytes 1179656 | tf_op jit(solution)/shard_map/ppermute | solution.py:587
  14.7 9.5 %collective-permute-start.14 = (bf16[512,384]{1,0:T(8,128)(2,1)S(1)}, bf16[512,384]{1,0:T(8,128)(2,1)S(1)}, u32[]{:S(2)}, u32[]{:S(2)}) collective-permute-start(bf16[512,384]{1,0:T(8,128)(2,1)S(1)} %get-tuple-element.288), channel_id=1, source_target_pairs={{24,0},{25,1},{26,2},{27,3},{28,4},{29,5},{30,6},{31,7}} | collective-permute-start | bytes 1179656 | tf_op jit(solution)/shard_map/ppermute | solution.py:587
  20.3 14.6 %collective-permute-start.19 = (bf16[256,640]{1,0:T(8,128)(2,1)}, bf16[256,640]{1,0:T(8,128)(2,1)}, u32[]{:S(2)}, u32[]{:S(2)}) collective-permute-start(bf16[256,640]{1,0:T(8,128)(2,1)} %bitcast.23), channel_id=1, source_target_pairs={{16,24},{17,25},{18,26},{19,27},{20,28},{21,29},{22,30},{23,31}} | collective-permute-start | bytes 983048 | tf_op jit(solution)/shard_map/ppermute | solution.py:588
  21.5 13.3 %collective-permute-start.18 = (bf16[256,640]{1,0:T(8,128)(2,1)}, bf16[256,640]{1,0:T(8,128)(2,1)}, u32[]{:S(2)}, u32[]{:S(2)}) collective-permute-start(bf16[256,640]{1,0:T(8,128)(2,1)} %bitcast.23), channel_id=1, source_target_pairs={{8,24},{9,25},{10,26},{11,27},{12,28},{13,29},{14,30},{15,31}} | collective-permute-start | bytes 983048 | tf_op jit(solution)/shard_map/ppermute | solution.py:588
  22.9 12.0 %collective-permute-start.17 = (bf16[256,640]{1,0:T(8,128)(2,1)}, bf16[256,640]{1,0:T(8,128)(2,1)}, u32[]{:S(2)}, u32[]{:S(2)}) collective-permute-start(bf16[256,640]{1,0:T(8,128)(2,1)} %bitcast.23), channel_id=1, source_target_pairs={{0,24},{1,25},{2,26},{3,27},{4,28},{5,29},{6,30},{7,31}} | collective-permute-start | bytes 983048 | tf_op jit(solution)/shard_map/ppermute | solution.py:588
  26.9 6.4 %collective-permute-start.2 = (f32[200,128]{1,0:T(8,128)S(1)}, f32[200,128]{1,0:T(8,128)}, u32[]{:S(2)}, u32[]{:S(2)}) collective-permute-start(f32[200,128]{1,0:T(8,128)S(1)} %get-tuple-element.177), channel_id=1, source_target_pairs={{24,25},{25,26},{26,27},{27,28},{28,29},{29,30},{30,31}} | collective-permute-start | bytes 307208 | tf_op jit(solution)/shard_map/cond/branch_1_fun/ppermute | solution.py:564
  29.4 5.5 %collective-permute-start.3 = (f32[200,128]{1,0:T(8,128)S(1)}, f32[200,128]{1,0:T(8,128)}, u32[]{:S(2)}, u32[]{:S(2)}) collective-permute-start(f32[200,128]{1,0:T(8,128)S(1)} %get-tuple-element.178), channel_id=1, source_target_pairs={{25,24},{26,25},{27,26},{28,27},{29,28},{30,29},{31,30}} | collective-permute-start | bytes 307208 | tf_op jit(solution)/shard_map/cond/branch_1_fun/ppermute | solution.py:565
  34.9 42.5 %copy-start.4 = (bf16[256,128]{1,0:T(8,128)(2,1)S(1)}, bf16[256,128]{1,0:T(8,128)(2,1)}, u32[]{:S(2)}) copy-start(bf16[256,128]{1,0:T(8,128)(2,1)} %get-tuple-element.291) | copy-start | bytes 196612
  37.6 11.1 %collective-permute-start.10 = (f32[256,128]{1,0:T(8,128)S(1)}, f32[256,128]{1,0:T(8,128)}, u32[]{:S(2)}, u32[]{:S(2)}) collective-permute-start(f32[256,128]{1,0:T(8,128)S(1)} %get-tuple-element.225.up), channel_id=1, source_target_pairs={{24,25},{25,26},{26,27},{27,28},{28,29},{29,30},{30,31}} | collective-permute-start | bytes 393224 | tf_op jit(solution)/shard_map/cond/branch_3_fun/ppermute | solution.py:564
  41.6 7.1 %collective-permute-start.11 = (f32[256,128]{1,0:T(8,128)S(1)}, f32[256,128]{1,0:T(8,128)}, u32[]{:S(2)}, u32[]{:S(2)}) collective-permute-start(f32[256,128]{1,0:T(8,128)S(1)} %get-tuple-element.226.down), channel_id=1, source_target_pairs={{25,24},{26,25},{27,26},{28,27},{29,28},{30,29},{31,30}} | collective-permute-start | bytes 393224 | tf_op jit(solution)/shard_map/cond/branch_3_fun/ppermute | solution.py:565
  52.4 21.7 %collective-permute-start.20 = (bf16[256,512]{1,0:T(8,128)(2,1)S(1)}, bf16[256,512]{1,0:T(8,128)(2,1)S(1)}, u32[]{:S(2)}, u32[]{:S(2)}) collective-permute-start(bf16[256,512]{1,0:T(8,128)(2,1)S(1)} %get-tuple-element.300), channel_id=1, source_target_pairs={{0,24},{1,25},{2,26},{3,27},{4,28},{5,29},{6,30},{7,31},{24,0},{25... | collective-permute-start | bytes 786440 | tf_op jit(solution)/shard_map/ppermute | solution.py:669
  70.1 7.3 %collective-permute-start.21 = (bf16[256,512]{1,0:T(8,128)(2,1)}, bf16[256,512]{1,0:T(8,128)(2,1)S(1)}, u32[]{:S(2)}, u32[]{:S(2)}) collective-permute-start(bf16[256,512]{1,0:T(8,128)(2,1)} %get-tuple-element.301), channel_id=1, source_target_pairs={{8,24},{9,25},{10,26},{11,27},{12,28},{13,29},{14,30},{15,31},{24,... | collective-permute-start | bytes 786440 | tf_op jit(solution)/shard_map/ppermute | solution.py:669
  72.0 5.4 %collective-permute-start.22 = (bf16[256,512]{1,0:T(8,128)(2,1)}, bf16[256,512]{1,0:T(8,128)(2,1)S(1)}, u32[]{:S(2)}, u32[]{:S(2)}) collective-permute-start(bf16[256,512]{1,0:T(8,128)(2,1)} %get-tuple-element.302), channel_id=1, source_target_pairs={{16,24},{17,25},{18,26},{19,27},{20,28},{21,29},{22,30},{23,31},{2... | collective-permute-start | bytes 786440 | tf_op jit(solution)/shard_map/ppermute | solution.py:669
  79.2 11.9 %collective-permute-start.12 = (f32[256,128]{1,0:T(8,128)S(1)}, f32[256,128]{1,0:T(8,128)S(1)}, u32[]{:S(2)}, u32[]{:S(2)}) collective-permute-start(f32[256,128]{1,0:T(8,128)S(1)} %get-tuple-element.256.up), channel_id=1, source_target_pairs={{24,25},{25,26},{26,27},{27,28},{28,29},{29,30},{30,31}} | collective-permute-start | bytes 393224 | tf_op jit(solution)/shard_map/cond/branch_1_fun/ppermute | solution.py:564
  81.3 9.8 %collective-permute-start.13 = (f32[256,128]{1,0:T(8,128)S(1)}, f32[256,128]{1,0:T(8,128)S(1)}, u32[]{:S(2)}, u32[]{:S(2)}) collective-permute-start(f32[256,128]{1,0:T(8,128)S(1)} %get-tuple-element.257.down), channel_id=1, source_target_pairs={{25,24},{26,25},{27,26},{28,27},{29,28},{30,29},{31,30}} | collective-permute-start | bytes 393224 | tf_op jit(solution)/shard_map/cond/branch_1_fun/ppermute | solution.py:565

commit v3 on v2

--- a/solution.py
+++ b/solution.py
@@ -4,6 +4,7 @@
 from jax.experimental import pallas as pl
 from jax.experimental.pallas import tpu as pltpu
 from jax.sharding import PartitionSpec as P
+
 
 UNIT_LENGTH = 0.02
 TIME_STEP = 0.1
@@ -26,7 +27,7 @@
     return jax.ShapeDtypeStruct(shape, dtype)
 
 
-def call(body, args, outs, scratch=(), smem=0, name=None, away=(), unused=(), alias=None):
+def call(body, args, outs, scratch=(), smem=0, away=(), unused=(), alias=None):
     specs = [SMEM] * smem + [VMEM] * (len(args) - smem)
     return pl.pallas_call(
         body,
@@ -36,7 +37,6 @@
         scratch_shapes=list(scratch),
         input_output_aliases=alias or {},
         compiler_params=pltpu.CompilerParams(vmem_limit_bytes=VMEM_LIMIT),
-        name=name,
     )(*args)
 
 
@@ -48,7 +48,7 @@
     return lax.dot_general(a, b, (dims, ((), ())), preferred_element_type=F32)
 
 
-def diff_i(below, here, above, i):
+def diff_i(below, here, above):
     if below is None:
         return above - here
     if above is None:
@@ -82,7 +82,7 @@
         here = UNIT_LENGTH * slab(ref, c, i)
         below = UNIT_LENGTH * slab(ref, c, i - 1) if i > 0 else None
         above = UNIT_LENGTH * slab(ref, c, i + 1) if i < 7 else None
-        row = [diff_i(below, here, above, i), diff_j(here), diff_k(here)]
+        row = [diff_i(below, here, above), diff_j(here), diff_k(here)]
         row[c] = row[c] + 1.0
         grads.append(row)
     return grads
@@ -162,7 +162,6 @@
                 slab(stress, a, i - 1) if i > 0 else None,
                 slab(stress, a, i),
                 slab(stress, a, i + 1) if i < 7 else None,
-                i,
             )
             before = pltpu.roll(pltpu.roll(here, 1, 1), 1, 2)
             after = pltpu.roll(pltpu.roll(here, 7, 1), e - 1, 2)
@@ -190,7 +189,6 @@
                 slab(stress, a, i - 1) if i > 0 else None,
                 slab(stress, a, i),
                 slab(stress, a, i + 1) if i < 7 else None,
-                i,
             )
             if i == 0:
                 other = low[pl.ds(64 * a, 64), :].reshape(8, 8, e)
@@ -331,10 +329,10 @@
     far_low, near_low, a, b = of(low, 0), of(low, 1), of(bottom, 0), of(bottom, 1)
     c, d, near_high, far_high = of(top, 0), of(top, 1), of(high, 0), of(high, 1)
     m = [of(middle, n) for n in range(4)]
-    before = sweep(far_low, near_low, a, of(kap_low, 0), masks)
+    before = sweep(far_low, near_low, a, of(kap_low, 2), masks)
     zero = sweep(near_low, a, b, k[0], masks)
     last = sweep(c, d, near_high, k[3], masks)
-    after = sweep(d, near_high, far_high, of(kap_high, 0), masks)
+    after = sweep(d, near_high, far_high, of(kap_high, 2), masks)
     return [
         sweep(before, zero, m[0], k[0], masks),
         sweep(zero, m[0], m[1], k[1], masks),
@@ -386,10 +384,8 @@
 
 
 def rates(tiles):
-    def body(mat, kap, edge, up, down, *unused):
+    def body(mat, kap, edge):
         to_octants(mat, kap, 0.5 * SWEEP_STEP, tables_in(), tiles)
-        up[pl.ds(0, LANES), :] = kap[layer_rows(15), :]
-        down[pl.ds(0, LANES), :] = kap[layer_rows(0), :]
         for n, x in enumerate((0, 1, 14, 15)):
             edge[layer_rows(n), :] = kap[layer_rows(x), :]
 
@@ -405,14 +401,14 @@
 
 
 def elastic_forces(state, mat, occ, out, *scratch):
-    elastic(state, mat, occ[...].reshape(1, 1, occ.shape[-1]), out, *scratch)
-
-
-def turn(state, mat, occ, out, *scratch):
-    elastic_forces(state, mat, occ, out, *scratch[-2:])
-
-
-def first_step(state, mat, occ, base, sel, recv, low, high, out, send, up, down, _, *scratch):
+    elastic(state, mat, occ[...].reshape(1, 1, occ.shape[-1]), out, *scratch[-2:])
+
+
+def idle(*refs):
+    pass
+
+
+def first_step(state, mat, occ, base, sel, recv, low, high, out, send, up, down, *scratch):
     filled = occ[...].reshape(1, 1, occ.shape[-1])
     fills = (low[pl.ds(192, 1), :], high[pl.ds(192, 1), :])
     advance(state, mat, filled, base, recv, sel, low, high, fills, out, *scratch[:3])
@@ -433,7 +429,9 @@
         if edged:
             edge, v0, v1, v2, tile, out, up, down = refs
         else:
-            v0, v1, v2, out, up, down, tile, _ = refs
+            border, v0, v1, v2, out, up, down, tile, _ = refs
+            down[layer_rows(2), :] = border[layer_rows(0), :]
+            up[layer_rows(2), :] = border[layer_rows(3), :]
         total = None
         for n, v in enumerate((v0, v1, v2)):
             spot = pl.ds(n * v.shape[0], v.shape[0])
@@ -547,7 +545,7 @@
     octant = brick_octant.reshape(1, e)
     layers, ends, halo = shape_of((2048, LANES)), shape_of((512, LANES)), shape_of((256, LANES))
     rows, flat = shape_of((slots, 512), BF16), shape_of((1536, e))
-    face, side = shape_of((256, e)), shape_of((200, e))
+    face, side, wide = shape_of((192, e)), shape_of((200, e)), shape_of((384, e))
     tile = shape_of((slots * (n_grp - 1), LANES), BF16)
 
     def pairs(back, g):
@@ -581,129 +579,117 @@
         ),
         [pltpu.VMEM((512, e), BF16)],
         smem=1,
-        name="prepare",
     )
     recv = swap(send)
-    fields = [lax.ppermute(field, axes, pairs(True, g)) for g in groups]
-    arrived = [lax.ppermute(recv, axes, pairs(False, g)) for g in groups]
+    fields = []
+    for g in groups:
+        fields.append(lax.ppermute(field, axes, pairs(True, g)))
+    side_low, side_high = both_ways(up, down, groups)
     work = [pltpu.VMEM((512, e), F32), pltpu.VMEM((1536, e), F32), pltpu.VMEM((1536, e), F32)]
     middle = pltpu.VMEM(layers.shape, F32)
 
-    def solvent_rates():
-        kap, edge, up, down, *spare = call(
-            rates(tiles),
-            (mat,),
-            (layers, ends, side, side, rows, face, face),
-            unused=(4, 5, 6),
-            name="rates",
-        )
-        return kap, edge, *both_ways(up, down, [solvent]), *spare
-
     def gathered(g):
         def run():
-            return call(gather_field(q_count), (recv, fields[g]), (rows,), name="gather")[0]
+            return call(gather_field(q_count), (recv, fields[g]), (rows,))[0]
 
         return run
 
+    def nothing(*outs):
+        return lambda: call(idle, (), outs, unused=range(len(outs)))
+
+    mine = lax.switch(grp, [gathered(g) for g in groups] + [lambda: nothing(rows)()[0]])
+    mine, recv = lax.optimization_barrier((mine, recv))
+    mine = swap(mine)
+    arrived = []
+    for g in groups:
+        arrived.append(lax.ppermute(recv, axes, pairs(False, g)))
+
+    def solvent_rates():
+        return tuple(call(rates(tiles), (mat,), (layers, ends)))
+
+    def mech_elastic():
+        return tuple(
+            call(elastic_forces, (current, mat, occ), (layers, ends), work[1:], unused=(1,))
+        )
+
     def mech_first():
-        mine = swap(lax.switch(grp, [gathered(g) for g in groups]))
-        low, high = both_ways(up, down, groups)
-        (base,) = call(elastic_forces, (current, mat, occ), (flat,), work[1:], name="elastic")
-        moved, send, fore, back, spare = call(
-            first_step,
-            (current, mat, occ, base, sel, mine, low, high),
-            (shape_of((2048, e)), rows, face, face, ends),
-            work + [pltpu.VMEM((512, e), BF16)],
-            unused=(4,),
-            name="first_step",
+        return tuple(
+            call(
+                first_step,
+                (current, mat, occ, base, sel, mine, side_low, side_high),
+                (layers, rows, face, face),
+                work + [pltpu.VMEM((512, e), BF16)],
+            )
         )
-        return moved, spare, low, high, send, fore, back
 
     is_solvent = grp == solvent
-    moved, kap_edge, side_low, side_high, send, fore, aft = lax.cond(
-        is_solvent, solvent_rates, mech_first
-    )
+    base, kap_edge = lax.cond(is_solvent, solvent_rates, mech_elastic)
+    kap = base
+    idle_first = lambda: tuple(nothing(layers, rows, face, face)())
+    moved, send, fore, aft = lax.cond(is_solvent, idle_first, mech_first)
 
     def solvent_first():
         added, top, bottom, hot, spare = call(
-            deposit(False),
-            (phi, *arrived),
-            (layers, halo, halo, tile, flat),
-            unused=(4,),
-            name="deposit_first",
+            deposit(False), (phi, kap_edge, *arrived), (layers, wide, wide, tile, flat), unused=(4,)
         )
         low, high = both_ways(top, bottom, [solvent])
-        inner, mid = call(
-            inner_first(q_count), (added, moved), (layers, ends), [middle], name="inner_first"
-        )
+        inner, mid = call(inner_first(q_count), (added, kap), (layers, ends), [middle])
         edge, s0, s1, s2 = call(
             outer_first(q_count),
-            (top, bottom, low, high, kap_edge, side_low, side_high, mid, inner, hot),
+            (top, bottom, low, high, kap_edge, low, high, mid, inner, hot),
             (ends, rows, rows, rows),
             [pltpu.VMEM((512, 4 * LANES), BF16)],
-            name="outer_first",
         )
         return inner, edge, hot, spare, low, high, s0, s1, s2
 
     def mech_turn(g):
         def run():
             mine = swap(send)
-            low, high = both_ways(fore, aft, [g])
-            base, *spare = call(
-                turn,
+            force, *spare = call(
+                elastic_forces,
                 (moved, mat, occ),
-                (flat, layers, ends, tile, rows, rows),
+                (flat, layers, ends, tile, wide, wide, rows, rows),
                 work[1:],
-                unused=range(1, 6),
-                name="elastic",
+                unused=range(1, 8),
             )
-            blocks = list(spare[3:])
+            blocks = list(spare[5:])
             blocks.insert(g, mine)
-            return *spare[:3], base, low, high, *blocks
+            return *spare[:3], force, *spare[3:5], *blocks
 
         return run
 
     turns = [mech_turn(g) for g in groups] + [solvent_first]
-    inner, edge, hot, base, face_low, face_high, *blocks = lax.switch(grp, turns)
+    inner, edge, hot, force, far_low, far_high, *blocks = lax.switch(grp, turns)
     back = [
         lax.ppermute(block, axes, pairs(False, g) + pairs(True, g))
         for g, block in zip(groups, blocks)
     ]
 
     def solvent_last():
-        added, top, bottom = call(
-            deposit(True),
-            (inner, edge, *back, hot),
-            (layers, halo, halo),
-            name="deposit_last",
-        )
+        added, top, bottom = call(deposit(True), (inner, edge, *back, hot), (layers, halo, halo))
         low, high = both_ways(top, bottom, [solvent])
-        out, mid = call(
-            inner_last(q_count, tiles), (added, moved), (flat, ends), [middle], name="inner_last"
-        )
+        out, mid = call(inner_last(q_count, tiles), (added, kap), (flat, ends), [middle])
         (out,) = call(
             outer_last(q_count, tiles),
-            (top, bottom, low, high, kap_edge, side_low, side_high, mid, out),
+            (top, bottom, low, high, kap_edge, far_low, far_high, mid, out),
             (flat,),
             [pltpu.VMEM((4 * 16 * tiles, LANES), F32), pltpu.SemaphoreType.DMA((2,))],
             away=(8,),
             unused=(0,),
             alias={8: 0},
-            name="outer_last",
         )
         return out
 
     def swapped(g):
-        return lambda: swap(back[g])
+        return lambda: (swap(back[g]), *both_ways(fore, aft, [g]))
 
     def mech_last():
-        mine = lax.switch(grp, [swapped(g) for g in groups])
+        mine, low, high = lax.switch(grp, [swapped(g) for g in groups])
         (out,) = call(
             last_step,
-            (moved, mat, occ, base, sel, mine, face_low, face_high, side_low, side_high),
+            (moved, mat, occ, force, sel, mine, low, high, side_low, side_high),
             (flat,),
             work,
-            name="last_step",
         )
         return out
 

time: 95.6 us -> 95.8 us (level)
  the two profiles are of different devices: /device:TPU:21 before, /device:TPU:1 now
where the time goes in v3:
time: 95.8 us; the launch traced here: 94.9 us
  starting transfers between devices  53.1 us (55%)
  waiting for transfers between devices  23 us (24%)
  Pallas kernels  16.4 us (17%)
  local copies, waits for them, and re-layouts  2.22 us (2%)
    all_to_all x4, starting transfers between devices, swap(): return lax.all_to_all(block, 'blk', split_axis=0, concat_axis=0, tiled=True)  20.7 us
    pallas_call x6, Pallas kernels, call(): pl.pallas_call(body, out_shape=outs, in_specs=[ANY if n in away else spec...  16.4 us
    ppermute x3, starting transfers between devices, shards(): lax.ppermute(block, axes, pairs(False, g) + pairs(True, g))  11.2 us
    all_to_all x4, waiting for transfers between devices, swap(): return lax.all_to_all(block, 'blk', split_axis=0, concat_axis=0, tiled=True)  10 us
    ppermute x3, starting transfers between devices, shards(): arrived.append(lax.ppermute(recv, axes, pairs(False, g)))  8.15 us
    ppermute x2, starting transfers between devices, both_ways(): lax.ppermute(up, axes, planes(True, which))  7.86 us
    ppermute x2, waiting for transfers between devices, both_ways(): lax.ppermute(down, axes, planes(False, which))  6.01 us
    ppermute x3, waiting for transfers between devices, shards(): lax.ppermute(block, axes, pairs(False, g) + pairs(True, g))  3.56 us
  transfers between devices with their start and end apart: 17, of which 7 were waited for; matrix products, arithmetic and copies ran while one was open for 0% of the time, Pallas kernels for 5%

profile of v3, /device:TPU:1, one launch (start us, length us, event | category | flops | bytes accessed | tf_op | source)
XLA Modules:
  0.0 94.9 jit_solution(8987184369439459706)
XLA Ops:
  1.3 3.1 %shard_map.57 = (bf16[256,640]{1,0:T(8,128)(2,1)}, bf16[256,128]{1,0:T(8,128)(2,1)S(1)}, bf16[512,384]{1,0:T(8,128)(2,1)S(1)}, f32[2048,128]{1,0:T(8,128)}, f32[...) custom-call(s32[1]{0:T(128)} %bitcast.15.grp, f32[1536,128]{1,0:T(8,128)} %bitcast.34, f32[1,128]{1,0:T(1,128)S(1)} %convert_bitcast_fusion.occ, ...), custom_call_target="tpu_custom_call" | custom-call | tf_op jit(solution)/shard_map/pallas_call | solution.py:32
  4.4 6.3 %all-to-all-start.6 = ((bf16[8,32,640]{2,1,0:T(8,128)(2,1)}), bf16[8,32,640]{2,1,0:T(8,128)(2,1)S(1)}, u32[]{:S(2)}, u32[]{:S(2)}) async-start(bf16[8,32,640]{2,1,0:T(8,128)(2,1)} %bitcast.20), calls=%async_computation.6 | async-start | bytes 655360 | tf_op jit(solution)/shard_map/all_to_all | solution.py:567
  13.4 5.6 %all-to-all-done.6 = bf16[8,32,640]{2,1,0:T(8,128)(2,1)S(1)} async-done(((bf16[8,32,640]{2,1,0:T(8,128)(2,1)}), bf16[8,32,640]{2,1,0:T(8,128)(2,1)S(1)}, u32[]{:S(2)}, u32[]{:S(2)}) %all-to-all-start.6) | async-done | bytes 327712 | tf_op jit(solution)/shard_map/all_to_all | solution.py:567
  19.0 2.7 %collective-permute-done.11 = bf16[512,384]{1,0:T(8,128)(2,1)S(1)} collective-permute-done((bf16[512,384]{1,0:T(8,128)(2,1)S(1)}, bf16[512,384]{1,0:T(8,128)(2,1)S(1)}, u32[]{:S(2)}, u32[]{:S(2)}) %collective-permute-start.11) | collective-permute-done | bytes 393248 | tf_op jit(solution)/shard_map/ppermute | solution.py:586
  22.8 5.4 %all-to-all-start.7 = ((bf16[8,32,512]{2,1,0:T(8,128)(2,1)}), bf16[8,32,512]{2,1,0:T(8,128)(2,1)}, u32[]{:S(2)}, u32[]{:S(2)}) async-start(bf16[8,32,512]{2,1,0:T(8,128)(2,1)} %bitcast.22), calls=%async_computation.7 | async-start | bytes 524288 | tf_op jit(solution)/shard_map/all_to_all | solution.py:567
  29.7 5.4 %collective-permute-start.16 = (bf16[256,640]{1,0:T(8,128)(2,1)S(1)}, bf16[256,640]{1,0:T(8,128)(2,1)}, u32[]{:S(2)}, u32[]{:S(2)}) collective-permute-start(bf16[256,640]{1,0:T(8,128)(2,1)S(1)} %bitcast.41), channel_id=1, source_target_pairs={{8,24},{9,25},{10,26},{11,27},{12,28},{13,29},{14,30},{15,31}} | collective-permute-start | bytes 983048 | tf_op jit(solution)/shard_map/ppermute | solution.py:605
  36.4 4.0 %collective-permute-start.13 = (f32[200,128]{1,0:T(8,128)S(1)}, f32[200,128]{1,0:T(8,128)}, u32[]{:S(2)}, u32[]{:S(2)}) collective-permute-start(f32[200,128]{1,0:T(8,128)S(1)} %get-tuple-element.288), channel_id=1, source_target_pairs={{0,1},{1,2},{2,3},{3,4},{4,5},{5,6},{6,7},{8,9},{9,10},{10,11},{11... | collective-permute-start | bytes 307208 | tf_op jit(solution)/shard_map/ppermute | solution.py:562
  41.7 2.0 %conditional.7 = ((f32[2048,128]{1,0:T(8,128)S(1)}, f32[512,128]{1,0:T(8,128)S(1)})) conditional(s32[]{:T(128)} %convert_element_type.8, (f32[1536,128]{1,0:T(8,128)S(1)}, f32[1536,128]{1,0:T(8,128)S(1)}, f32[1,128]{1,0:T(1,128)S(1)}) %tuple.107, f32[1536,128]{1,0:T(8,128)S(1)} %bitcast.27), branch_computations={%region_0.0_spmd, %region_1.0_spmd} | conditional | bytes 8 | solution.py:626
  41.7 2.0 %branch_0_fun.5 = (f32[2048,128]{1,0:T(8,128)S(1)}, f32[512,128]{1,0:T(8,128)S(1)}) custom-call(f32[1536,128]{1,0:T(8,128)S(1)} %get-tuple-element.150.state, f32[1536,128]{1,0:T(8,128)S(1)} %get-tuple-element.151.mat, f32[1,128]{1,0:T(1,128)S(1)} %get-tuple-element.152.occ), custom_call_target="tpu_custom_call" | custom-call | tf_op jit(solution)/shard_map/cond/branch_0_fun/pallas_call | solution.py:32
  43.8 2.1 %collective-permute-done.14 = f32[200,128]{1,0:T(8,128)} collective-permute-done((f32[200,128]{1,0:T(8,128)S(1)}, f32[200,128]{1,0:T(8,128)}, u32[]{:S(2)}, u32[]{:S(2)}) %collective-permute-start.14) | collective-permute-done | bytes 102432 | tf_op jit(solution)/shard_map/ppermute | solution.py:563
  45.9 5.0 %conditional.8 = ((f32[2048,128]{1,0:T(8,128)S(1)}, bf16[256,512]{1,0:T(8,128)(2,1)}, f32[192,128]{1,0:T(8,128)}, f32[192,128]{1,0:T(8,128)})) conditional(s32[]{:T(128)} %convert_element_type.8, (bf16[8,32,512]{2,1,0:T(8,128)(2,1)}, f32[1536,128]{1,0:T(8,128)S(1)}, f32[1536,128]{1,0:T(8,128)S(1)}, f32[1,128]{1,0:T(1,128)S(1)}, ...), branch_computations={%region_6.0_spmd, %region_7.0_spmd} | conditional | bytes 3145764 | solution.py:629
  46.8 4.1 %branch_0_fun.7 = (f32[2048,128]{1,0:T(8,128)S(1)}, bf16[256,512]{1,0:T(8,128)(2,1)}, f32[192,128]{1,0:T(8,128)}, f32[192,128]{1,0:T(8,128)}) custom-call(f32[1536,128]{1,0:T(8,128)} %copy-done.4, f32[1536,128]{1,0:T(8,128)S(1)} %get-tuple-element.160.mat, f32[1,128]{1,0:T(1,128)S(1)} %get-tuple-element.161.occ, f32[2048,128]{1,0:T(8,128)S(1)} %get-tuple-element.162.base, ...), custom_call_target="tpu_custom_call" | custom-call | tf_op jit(solution)/shard_map/cond/branch_0_fun/pallas_call | solution.py:32
  50.9 12.0 %conditional.9 = (f32[2048,128]{1,0:T(8,128)}, f32[512,128]{1,0:T(8,128)S(1)}, bf16[768,128]{1,0:T(8,128)(2,1)}, f32[1536,128]{1,0:T(8,128)}, f32[384,128]{1,0:T...) conditional(s32[]{:T(128)} %clamp.7, ...), branch_computations={%region_8.0_spmd, %region_9.0_spmd, %region_10.0_spmd, %region_11.... | conditional | bytes 5767348 | solution.py:662
  50.9 4.7 %all-to-all-start.1 = ((bf16[8,32,512]{2,1,0:T(8,128)(2,1)}), bf16[8,32,512]{2,1,0:T(8,128)(2,1)}, u32[]{:S(2)}, u32[]{:S(2)}) async-start(bf16[8,32,512]{2,1,0:T(8,128)(2,1)} %bitcast.3), calls=%async_computation.1 | async-start | bytes 524288 | tf_op jit(solution)/shard_map/cond/branch_1_fun/all_to_all | solution.py:567
  55.6 2.8 %branch_1_fun.10 = (f32[1536,128]{1,0:T(8,128)}, f32[2048,128]{1,0:T(8,128)}, f32[512,128]{1,0:T(8,128)S(1)}, bf16[768,128]{1,0:T(8,128)(2,1)}, f32[384,128]{1,0...) custom-call(f32[2048,128]{1,0:T(8,128)S(1)} %get-tuple-element.179.state, ...), custom_call_target="tpu_custom_call" | custom-call | tf_op jit(solution)/shard_map/cond/branch_1_fun/pallas_call | solution.py:32
  58.5 4.4 %all-to-all-done.1 = bf16[8,32,512]{2,1,0:T(8,128)(2,1)} async-done(((bf16[8,32,512]{2,1,0:T(8,128)(2,1)}), bf16[8,32,512]{2,1,0:T(8,128)(2,1)}, u32[]{:S(2)}, u32[]{:S(2)}) %all-to-all-start.1) | async-done | bytes 262176 | tf_op jit(solution)/shard_map/cond/branch_1_fun/all_to_all | solution.py:567
  64.3 8.4 %collective-permute-start.19 = (bf16[256,512]{1,0:T(8,128)(2,1)}, bf16[256,512]{1,0:T(8,128)(2,1)}, u32[]{:S(2)}, u32[]{:S(2)}) collective-permute-start(bf16[256,512]{1,0:T(8,128)(2,1)} %get-tuple-element.298), channel_id=1, source_target_pairs={{8,24},{9,25},{10,26},{11,27},{12,28},{13,29},{14,30},{15,31},{24,... | collective-permute-start | bytes 786440 | tf_op jit(solution)/shard_map/ppermute | solution.py:664
  74.1 3.6 %collective-permute-done.19 = bf16[256,512]{1,0:T(8,128)(2,1)} collective-permute-done((bf16[256,512]{1,0:T(8,128)(2,1)}, bf16[256,512]{1,0:T(8,128)(2,1)}, u32[]{:S(2)}, u32[]{:S(2)}) %collective-permute-start.19) | collective-permute-done | bytes 262176 | tf_op jit(solution)/shard_map/ppermute | solution.py:664
  77.7 17.3 %conditional.10 = (f32[1,3,512,128]{3,2,1,0:T(8,128)}) conditional(s32[]{:T(128)} %convert_element_type.8, (s32[]{:T(128)}, bf16[256,512]{1,0:T(8,128)(2,1)}, f32[192,128]{1,0:T(8,128)}, f32[192,128]{1,0:T(8,128)}, bf16[256,512]{1,0:T(8,128)(2,1)}, /*index=5*/bf16[256,512]{1,0:T(8,128)(2,1)}, f32[2048,128]{1,0:T(8,128)S(1)}, ...), branch_computations={%region_12.0_spmd, %region_16.0_spmd} | conditional | flops 1 | bytes 5505340 | solution.py:696
  77.7 13.9 %conditional = (bf16[256,512]{1,0:T(8,128)(2,1)}, f32[192,128]{1,0:T(8,128)}, f32[192,128]{1,0:T(8,128)}) conditional(s32[]{:T(128)} %clamp.1, (bf16[256,512]{1,0:T(8,128)(2,1)}, f32[192,128]{1,0:T(8,128)}, f32[192,128]{1,0:T(8,128)}) %tuple.49, (bf16[256,512]{1,0:T(8,128)(2,1)}, f32[192,128]{1,0:T(8,128)}, ...), branch_computations={%region_13.0_spmd, %region_14.0_spmd, %region_15.0_spmd} | conditional | bytes 2359488 | solution.py:687
  77.7 4.2 %all-to-all-start.4 = ((bf16[8,32,512]{2,1,0:T(8,128)(2,1)}), bf16[8,32,512]{2,1,0:T(8,128)(2,1)}, u32[]{:S(2)}, u32[]{:S(2)}) async-start(bf16[8,32,512]{2,1,0:T(8,128)(2,1)} %bitcast.9), calls=%async_computation.4 | async-start | bytes 524288 | tf_op jit(solution)/shard_map/cond/branch_0_fun/cond/branch_1_fun/all_to_all | solution.py:567
  81.9 3.9 %collective-permute-start.4 = (f32[192,128]{1,0:T(8,128)S(1)}, f32[192,128]{1,0:T(8,128)}, u32[]{:S(2)}, u32[]{:S(2)}) collective-permute-start(f32[192,128]{1,0:T(8,128)S(1)} %copy-done.7), channel_id=1, source_target_pairs={{8,9},{9,10},{10,11},{11,12},{12,13},{13,14},{14,15}} | collective-permute-start | bytes 294920 | tf_op jit(solution)/shard_map/cond/branch_0_fun/cond/branch_1_fun/ppermute | solution.py:562
  87.6 3.9 %collective-permute-done.5 = f32[192,128]{1,0:T(8,128)} collective-permute-done((f32[192,128]{1,0:T(8,128)S(1)}, f32[192,128]{1,0:T(8,128)}, u32[]{:S(2)}, u32[]{:S(2)}) %collective-permute-start.5) | collective-permute-done | bytes 98336 | tf_op jit(solution)/shard_map/cond/branch_0_fun/cond/branch_1_fun/ppermute | solution.py:563
  91.5 3.4 %branch_0_fun.9 = f32[1536,128]{1,0:T(8,128)} custom-call(f32[2048,128]{1,0:T(8,128)S(1)} %get-tuple-element.229.state, f32[1536,128]{1,0:T(8,128)S(1)} %get-tuple-element.230.mat, f32[1,128]{1,0:T(1,128)S(1)} %get-tuple-element.231.occ, f32[1536,128]{1,0:T(8,128)S(1)} %copy-done.6, bf16[256,128]{1,0:T(8,128)(2,1)S(1)} %get-tuple-element.233.sel, ...), custom_call_target="tpu_custom_call" | custom-call | tf_op jit(solution)/shard_map/cond/branch_0_fun/pallas_call | solution.py:32
  (41 shorter events, 15.7 us)
Async XLA Ops:
  0.7 0.7 copy-start.1
  4.4 14.6 %all-to-all-start.6 = ((bf16[8,32,640]{2,1,0:T(8,128)(2,1)}), bf16[8,32,640]{2,1,0:T(8,128)(2,1)S(1)}, u32[]{:S(2)}, u32[]{:S(2)}) async-start(bf16[8,32,640]{2,1,0:T(8,128)(2,1)} %bitcast.20), calls=%async_computation.6 | async-start | bytes 655360 | tf_op jit(solution)/shard_map/all_to_all | solution.py:567
  10.7 2.7 %collective-permute-start.12 = (bf16[512,384]{1,0:T(8,128)(2,1)S(1)}, bf16[512,384]{1,0:T(8,128)(2,1)S(1)}, u32[]{:S(2)}, u32[]{:S(2)}) collective-permute-start(bf16[512,384]{1,0:T(8,128)(2,1)S(1)} %get-tuple-element.284), channel_id=1, source_target_pairs={{24,16},{25,17},{26,18},{27,19},{28,20},{29,21},{30,22},{31,23}} | collective-permute-start | bytes 1179656 | tf_op jit(solution)/shard_map/ppermute | solution.py:586
  11.4 10.3 %collective-permute-start.11 = (bf16[512,384]{1,0:T(8,128)(2,1)S(1)}, bf16[512,384]{1,0:T(8,128)(2,1)S(1)}, u32[]{:S(2)}, u32[]{:S(2)}) collective-permute-start(bf16[512,384]{1,0:T(8,128)(2,1)S(1)} %get-tuple-element.284), channel_id=1, source_target_pairs={{24,8},{25,9},{26,10},{27,11},{28,12},{29,13},{30,14},{31,15}} | collective-permute-start | bytes 1179656 | tf_op jit(solution)/shard_map/ppermute | solution.py:586
  12.7 9.0 %collective-permute-start.10 = (bf16[512,384]{1,0:T(8,128)(2,1)S(1)}, bf16[512,384]{1,0:T(8,128)(2,1)S(1)}, u32[]{:S(2)}, u32[]{:S(2)}) collective-permute-start(bf16[512,384]{1,0:T(8,128)(2,1)S(1)} %get-tuple-element.284), channel_id=1, source_target_pairs={{24,0},{25,1},{26,2},{27,3},{28,4},{29,5},{30,6},{31,7}} | collective-permute-start | bytes 1179656 | tf_op jit(solution)/shard_map/ppermute | solution.py:586
  21.8 20.0 %copy-start.2 = (f32[1,3,512,128]{3,2,1,0:T(8,128)S(1)}, f32[1,3,512,128]{3,2,1,0:T(8,128)}, u32[]{:S(2)}) copy-start(f32[1,3,512,128]{3,2,1,0:T(8,128)} %param.23) | copy-start | bytes 2359300
  21.8 20.0 %copy-start.3 = (f32[1,3,512,128]{3,2,1,0:T(8,128)S(1)}, f32[1,3,512,128]{3,2,1,0:T(8,128)}, u32[]{:S(2)}) copy-start(f32[1,3,512,128]{3,2,1,0:T(8,128)} %param.22) | copy-start | bytes 2359300
  22.8 23.1 %all-to-all-start.7 = ((bf16[8,32,512]{2,1,0:T(8,128)(2,1)}), bf16[8,32,512]{2,1,0:T(8,128)(2,1)}, u32[]{:S(2)}, u32[]{:S(2)}) async-start(bf16[8,32,512]{2,1,0:T(8,128)(2,1)} %bitcast.22), calls=%async_computation.7 | async-start | bytes 524288 | tf_op jit(solution)/shard_map/all_to_all | solution.py:567
  28.3 15.5 %collective-permute-start.17 = (bf16[256,640]{1,0:T(8,128)(2,1)S(1)}, bf16[256,640]{1,0:T(8,128)(2,1)}, u32[]{:S(2)}, u32[]{:S(2)}) collective-permute-start(bf16[256,640]{1,0:T(8,128)(2,1)S(1)} %bitcast.40), channel_id=1, source_target_pairs={{16,24},{17,25},{18,26},{19,27},{20,28},{21,29},{22,30},{23,31}} | collective-permute-start | bytes 983048 | tf_op jit(solution)/shard_map/ppermute | solution.py:605
  29.7 14.1 %collective-permute-start.16 = (bf16[256,640]{1,0:T(8,128)(2,1)S(1)}, bf16[256,640]{1,0:T(8,128)(2,1)}, u32[]{:S(2)}, u32[]{:S(2)}) collective-permute-start(bf16[256,640]{1,0:T(8,128)(2,1)S(1)} %bitcast.41), channel_id=1, source_target_pairs={{8,24},{9,25},{10,26},{11,27},{12,28},{13,29},{14,30},{15,31}} | collective-permute-start | bytes 983048 | tf_op jit(solution)/shard_map/ppermute | solution.py:605
  35.0 8.7 %collective-permute-start.15 = (bf16[256,640]{1,0:T(8,128)(2,1)S(1)}, bf16[256,640]{1,0:T(8,128)(2,1)}, u32[]{:S(2)}, u32[]{:S(2)}) collective-permute-start(bf16[256,640]{1,0:T(8,128)(2,1)S(1)} %bitcast.42), channel_id=1, source_target_pairs={{0,24},{1,25},{2,26},{3,27},{4,28},{5,29},{6,30},{7,31}} | collective-permute-start | bytes 983048 | tf_op jit(solution)/shard_map/ppermute | solution.py:605
  36.4 7.4 %collective-permute-start.13 = (f32[200,128]{1,0:T(8,128)S(1)}, f32[200,128]{1,0:T(8,128)}, u32[]{:S(2)}, u32[]{:S(2)}) collective-permute-start(f32[200,128]{1,0:T(8,128)S(1)} %get-tuple-element.288), channel_id=1, source_target_pairs={{0,1},{1,2},{2,3},{3,4},{4,5},{5,6},{6,7},{8,9},{9,10},{10,11},{11... | collective-permute-start | bytes 307208 | tf_op jit(solution)/shard_map/ppermute | solution.py:562
  40.4 5.5 %collective-permute-start.14 = (f32[200,128]{1,0:T(8,128)S(1)}, f32[200,128]{1,0:T(8,128)}, u32[]{:S(2)}, u32[]{:S(2)}) collective-permute-start(f32[200,128]{1,0:T(8,128)S(1)} %get-tuple-element.289), channel_id=1, source_target_pairs={{1,0},{2,1},{3,2},{4,3},{5,4},{6,5},{7,6},{9,8},{10,9},{11,10},{12... | collective-permute-start | bytes 307208 | tf_op jit(solution)/shard_map/ppermute | solution.py:563
  45.9 0.9 copy-start.4
  50.9 12.0 %all-to-all-start.1 = ((bf16[8,32,512]{2,1,0:T(8,128)(2,1)}), bf16[8,32,512]{2,1,0:T(8,128)(2,1)}, u32[]{:S(2)}, u32[]{:S(2)}) async-start(bf16[8,32,512]{2,1,0:T(8,128)(2,1)} %bitcast.3), calls=%async_computation.1 | async-start | bytes 524288 | tf_op jit(solution)/shard_map/cond/branch_1_fun/all_to_all | solution.py:567
  62.9 11.2 %collective-permute-start.18 = (bf16[256,512]{1,0:T(8,128)(2,1)}, bf16[256,512]{1,0:T(8,128)(2,1)}, u32[]{:S(2)}, u32[]{:S(2)}) collective-permute-start(bf16[256,512]{1,0:T(8,128)(2,1)} %get-tuple-element.295), channel_id=1, source_target_pairs={{0,24},{1,25},{2,26},{3,27},{4,28},{5,29},{6,30},{7,31},{24,0},{25... | collective-permute-start | bytes 786440 | tf_op jit(solution)/shard_map/ppermute | solution.py:664
  64.3 13.4 %collective-permute-start.19 = (bf16[256,512]{1,0:T(8,128)(2,1)}, bf16[256,512]{1,0:T(8,128)(2,1)}, u32[]{:S(2)}, u32[]{:S(2)}) collective-permute-start(bf16[256,512]{1,0:T(8,128)(2,1)} %get-tuple-element.298), channel_id=1, source_target_pairs={{8,24},{9,25},{10,26},{11,27},{12,28},{13,29},{14,30},{15,31},{24,... | collective-permute-start | bytes 786440 | tf_op jit(solution)/shard_map/ppermute | solution.py:664
  72.7 4.9 %collective-permute-start.20 = (bf16[256,512]{1,0:T(8,128)(2,1)}, bf16[256,512]{1,0:T(8,128)(2,1)}, u32[]{:S(2)}, u32[]{:S(2)}) collective-permute-start(bf16[256,512]{1,0:T(8,128)(2,1)} %get-tuple-element.299), channel_id=1, source_target_pairs={{16,24},{17,25},{18,26},{19,27},{20,28},{21,29},{22,30},{23,31},{2... | collective-permute-start | bytes 786440 | tf_op jit(solution)/shard_map/ppermute | solution.py:664
  77.7 13.9 %copy-start.6 = (f32[1536,128]{1,0:T(8,128)S(1)}, f32[1536,128]{1,0:T(8,128)}, u32[]{:S(2)}) copy-start(f32[1536,128]{1,0:T(8,128)} %get-tuple-element.232.base) | copy-start | bytes 2359300 | tf_op jit(solution)/shard_map/cond
  77.7 4.2 %copy-start.7 = (f32[192,128]{1,0:T(8,128)S(1)}, f32[192,128]{1,0:T(8,128)}, u32[]{:S(2)}) copy-start(f32[192,128]{1,0:T(8,128)} %get-tuple-element.224) | copy-start | bytes 294916 | tf_op jit(solution)/shard_map/cond/branch_0_fun/cond
  77.7 8.1 %copy-start.9 = (f32[192,128]{1,0:T(8,128)S(1)}, f32[192,128]{1,0:T(8,128)}, u32[]{:S(2)}) copy-start(f32[192,128]{1,0:T(8,128)} %get-tuple-element.225) | copy-start | bytes 294916 | tf_op jit(solution)/shard_map/cond/branch_0_fun/cond
  77.7 13.8 %all-to-all-start.4 = ((bf16[8,32,512]{2,1,0:T(8,128)(2,1)}), bf16[8,32,512]{2,1,0:T(8,128)(2,1)}, u32[]{:S(2)}, u32[]{:S(2)}) async-start(bf16[8,32,512]{2,1,0:T(8,128)(2,1)} %bitcast.9), calls=%async_computation.4 | async-start | bytes 524288 | tf_op jit(solution)/shard_map/cond/branch_0_fun/cond/branch_1_fun/all_to_all | solution.py:567
  81.9 5.8 %collective-permute-start.4 = (f32[192,128]{1,0:T(8,128)S(1)}, f32[192,128]{1,0:T(8,128)}, u32[]{:S(2)}, u32[]{:S(2)}) collective-permute-start(f32[192,128]{1,0:T(8,128)S(1)} %copy-done.7), channel_id=1, source_target_pairs={{8,9},{9,10},{10,11},{11,12},{12,13},{13,14},{14,15}} | collective-permute-start | bytes 294920 | tf_op jit(solution)/shard_map/cond/branch_0_fun/cond/branch_1_fun/ppermute | solution.py:562
  85.8 5.8 %collective-permute-start.5 = (f32[192,128]{1,0:T(8,128)S(1)}, f32[192,128]{1,0:T(8,128)}, u32[]{:S(2)}, u32[]{:S(2)}) collective-permute-start(f32[192,128]{1,0:T(8,128)S(1)} %copy-done.9), channel_id=1, source_target_pairs={{9,8},{10,9},{11,10},{12,11},{13,12},{14,13},{15,14}} | collective-permute-start | bytes 294920 | tf_op jit(solution)/shard_map/cond/branch_0_fun/cond/branch_1_fun/ppermute | solution.py:563
  (2 other events, 1.3 us)

commit v4 on v3

--- a/solution.py
+++ b/solution.py
@@ -20,7 +20,7 @@
 F32, BF16 = jnp.float32, jnp.bfloat16
 VMEM = pl.BlockSpec(memory_space=pltpu.VMEM)
 SMEM = pl.BlockSpec(memory_space=pltpu.SMEM)
-ANY = pl.BlockSpec(memory_space=pl.ANY)
+ANY = pl.BlockSpec(memory_space=pltpu.HBM)
 
 
 def shape_of(shape, dtype=F32):
@@ -244,7 +244,7 @@
         out[layer_rows(x), :] = layer_to_octants(chunk, scale, tables, tiles)
         return carry
 
-    lax.fori_loop(0, 16, layer, 0)
+    lax.fori_loop(0, 16, layer, 0, unroll=2)
 
 
 def layer_from_octants(layer, tables, tiles):
@@ -268,117 +268,142 @@
     )
 
 
-def sweep(below, here, above, kap, masks):
-    inner, outer, last, first = masks
-    halves = [v.reshape(2, 8, 8, LANES) for v in (below, here, above, kap)]
-    out = []
-    for o in range(2):
-        low, c, high, rate = (v[o] for v in halves)
-        twin = halves[1][1 - o]
-        if o == 0:
-            y_above = jnp.concatenate([c[1:], twin[0:1]], axis=0)
-            y_below = jnp.concatenate([c[0:1], c[:-1]], axis=0)
-        else:
-            y_above = jnp.concatenate([c[1:], c[7:8]], axis=0)
-            y_below = jnp.concatenate([twin[7:8], c[:-1]], axis=0)
-        r = pltpu.roll(c, 7, 1)
-        z_above = jnp.where(inner, r, jnp.where(last, c, pltpu.roll(r, LANES - 1, 2)))
-        r = pltpu.roll(c, 1, 1)
-        z_below = jnp.where(outer, r, jnp.where(first, c, pltpu.roll(r, 1, 2)))
-        base = 1.0 + c * c
-        inflow = None
-        for n in (high, low, y_above, y_below, z_above, z_below):
-            part = (base + n * n) * (n - c)
-            inflow = part if inflow is None else inflow + part
-        out.append((c + rate * inflow).reshape(64, LANES))
-    return jnp.concatenate(out, axis=0)
+def weight(c):
+    return 0.5 + c * c
+
+
+def flux(c, s, other, other_s):
+    return (s + other_s) * (other - c)
+
+
+def inside(c, s, masks):
+    inner, last, outer = masks
+    fy = flux(c[:-1], s[:-1], c[1:], s[1:])
+    r = pltpu.roll(c, 7, 1)
+    up = jnp.where(inner, r, jnp.where(last, c, pltpu.roll(r, LANES - 1, 2)))
+    fz = flux(c, s, up, weight(up))
+    r = pltpu.roll(fz, 1, 1)
+    total = fz - jnp.where(outer, r, pltpu.roll(r, 1, 2))
+    return jnp.concatenate([total[:1] + fy[:1], total[1:-1] + (fy[1:] - fy[:-1]), total[-1:] - fy[-1:]], axis=0)
 
 
 def sweep_masks(q_count):
-    k, lane = iota((8, 8, LANES), 1), iota((8, 8, LANES), 2)
-    return k < 7, k > 0, lane == q_count - 1, lane == 0
-
-
-def inner_sweeps(phi, kap, middle, edges, put, q_count):
+    k, lane = iota((16, 8, LANES), 1), iota((16, 8, LANES), 2)
+    return k < 7, lane >= q_count - 1, k > 0
+
+
+def load(ref, x):
+    return ref[layer_rows(x), :].reshape(16, 8, LANES)
+
+
+def sweep_range(ref, kap, start, stop, put, weights, fluxes, masks):
+    c, s = load(ref, start), None
+    before = load(ref, start - 1)
+    s = weight(c)
+    weights[...] = s
+    fluxes[...] = flux(before, weight(before), c, s)
+
+    def step(x, carry):
+        c, up = load(ref, x), load(ref, x + 1)
+        s, up_s = weights[...], weight(up)
+        weights[...] = up_s
+        fx = flux(c, s, up, up_s)
+        total = (fx - fluxes[...]) + inside(c, s, masks)
+        fluxes[...] = fx
+        put(x, (c + load(kap, x) * total).reshape(LANES, LANES))
+        return carry
+
+    lax.fori_loop(start, stop, step, 0, unroll=2)
+
+
+def inner_sweeps(phi, kap, middle, edges, put, weights, fluxes, q_count):
     masks = sweep_masks(q_count)
 
-    def around(ref, x):
-        return ref[layer_rows(x - 1), :], ref[layer_rows(x), :], ref[layer_rows(x + 1), :]
-
-    def first(x, carry):
-        middle[layer_rows(x), :] = sweep(*around(phi, x), kap[layer_rows(x), :], masks)
-        return carry
-
-    def second(x, carry):
-        put(x, sweep(*around(middle, x), kap[layer_rows(x), :], masks))
-        return carry
-
-    lax.fori_loop(1, 15, first, 0)
+    def keep(x, layer):
+        middle[layer_rows(x), :] = layer
+
+    sweep_range(phi, kap, 1, 15, keep, weights, fluxes, masks)
     for n, x in enumerate((1, 2, 13, 14)):
         edges[layer_rows(n), :] = middle[layer_rows(x), :]
-    lax.fori_loop(2, 14, second, 0)
+    sweep_range(middle, kap, 2, 14, put, weights, fluxes, masks)
+
+
+def sweep_chain(layers, kaps, masks):
+    weights = [weight(c) for c in layers]
+    fx = [
+        flux(layers[n], weights[n], layers[n + 1], weights[n + 1]) for n in range(len(layers) - 1)
+    ]
+    return [
+        layers[n] + kaps[n - 1] * ((fx[n] - fx[n - 1]) + inside(layers[n], weights[n], masks))
+        for n in range(1, len(layers) - 1)
+    ]
 
 
 def edge_sweeps(top, bottom, low, high, kap_edge, kap_low, kap_high, middle, q_count):
     masks = sweep_masks(q_count)
-
-    def of(ref, n):
-        return ref[LANES * n : LANES * (n + 1), :]
-
-    k = [of(kap_edge, n) for n in range(4)]
-    far_low, near_low, a, b = of(low, 0), of(low, 1), of(bottom, 0), of(bottom, 1)
-    c, d, near_high, far_high = of(top, 0), of(top, 1), of(high, 0), of(high, 1)
-    m = [of(middle, n) for n in range(4)]
-    before = sweep(far_low, near_low, a, of(kap_low, 2), masks)
-    zero = sweep(near_low, a, b, k[0], masks)
-    last = sweep(c, d, near_high, k[3], masks)
-    after = sweep(d, near_high, far_high, of(kap_high, 2), masks)
-    return [
-        sweep(before, zero, m[0], k[0], masks),
-        sweep(zero, m[0], m[1], k[1], masks),
-        sweep(m[2], m[3], last, k[2], masks),
-        sweep(m[3], last, after, k[3], masks),
-    ]
+    k = [load(kap_edge, n) for n in range(4)]
+    m = [load(middle, n) for n in range(4)]
+    first = [load(low, 0), load(low, 1), load(bottom, 0), load(bottom, 1)]
+    first = sweep_chain(first, [load(kap_low, 2), k[0]], masks)
+    first = sweep_chain([*first, m[0], m[1]], k[:2], masks)
+    last = [load(top, 0), load(top, 1), load(high, 0), load(high, 1)]
+    last = sweep_chain(last, [k[3], load(kap_high, 2)], masks)
+    last = sweep_chain([m[2], m[3], *last], k[2:], masks)
+    return [layer.reshape(LANES, LANES) for layer in first + last]
 
 
 def prepare(n_blk, cap, tiles, solvent):
-    def body(grp, state, occ, col, octant, send, sel, field, phi, up, down, dil):
+    def body(grp, state, occ, col, octant, send, sel, filled, field, phi, up, down, *scratch):
+        dil, ints, layers, int_sems, sem = scratch
         e = state.shape[-1]
         quarter = 16 * tiles
 
         @pl.when(grp[0] != solvent)
         def _():
-            filled = occ[...].reshape(1, 1, e)
-            dilate(state, filled, dil)
-            hits = jnp.where(col[...] == iota((n_blk, e), 0), 1.0, 0.0)
+            copies = [
+                pltpu.make_async_copy(ref, ints.at[n], int_sems.at[n])
+                for n, ref in enumerate((occ, col, octant))
+            ]
+            for copy in copies:
+                copy.start()
+            dilate(state, 1.0, dil)
+            for copy in copies:
+                copy.wait()
+            full, column, o = ints[0].astype(F32), ints[1], ints[2]
+            hits = jnp.where(column == iota((n_blk, e), 0), 1.0, 0.0)
             earlier = jnp.where(iota((e, e), 0) < iota((e, e), 1), 1.0, 0.0).astype(BF16)
             rank = dot(hits.astype(BF16), earlier, ((1,), (0,)))
             rank = jnp.sum(rank * hits, axis=0, keepdims=True).astype(jnp.int32)
-            slot = col[...] * cap + rank
-            chosen = jnp.where(iota((n_blk * cap, e), 0) == slot, 1.0, 0.0).astype(BF16)
+            slot = column * cap + rank
+            chosen = jnp.where(iota((n_blk * cap, e), 0) == slot, 1.0, 0.0)
+            held = (chosen * full).astype(BF16)
+            chosen = chosen.astype(BF16)
             sel[...] = chosen
-            send[:, pl.ds(0, 512)] = dot(chosen, dil[...], ((1,), (1,))).astype(BF16)
-            o = octant[...]
+            send[:, pl.ds(0, 512)] = dot(held, dil[...], ((1,), (1,))).astype(BF16)
             block = sum((jnp.where(o >= n * quarter, 1, 0) for n in range(1, 4)))
             spot = o - quarter * block
             tile = jnp.where(iota((LANES, e), 0) == spot, (block + 1).astype(F32), 0.0)
             tile = dot(chosen, tile.astype(BF16), ((1,), (1,)))
             send[:, pl.ds(512, LANES)] = tile.astype(BF16)
             put_faces(state, up, down)
-            up[pl.ds(192, 8), :] = jnp.broadcast_to(occ[...], (8, e))
-            down[pl.ds(192, 8), :] = jnp.broadcast_to(occ[...], (8, e))
+            filled[...] = jnp.broadcast_to(full, (8, e))
+            up[pl.ds(192, 8), :] = jnp.broadcast_to(full, (8, e))
+            down[pl.ds(192, 8), :] = jnp.broadcast_to(full, (8, e))
 
         @pl.when(grp[0] == solvent)
         def _():
             tables = tables_in()
-            to_octants(state, phi, 1.0, tables, tiles)
+            to_octants(state, layers, 1.0, tables, tiles)
+            copy = pltpu.make_async_copy(layers, phi, sem.at[0])
+            copy.start()
             for i in range(8):
                 parts = []
                 for ox in range(2):
                     for oy in range(2):
-                        p = pressures(phi[pl.ds(LANES * (8 * ox + i) + 64 * oy, 64), :])
+                        p = pressures(layers[pl.ds(LANES * (8 * ox + i) + 64 * oy, 64), :])
                         parts.append(p[:, :quarter])
                 field[pl.ds(64 * i, 64), :] = jnp.concatenate(parts, axis=1)
+            copy.wait()
 
     return body
 
@@ -401,7 +426,7 @@
 
 
 def elastic_forces(state, mat, occ, out, *scratch):
-    elastic(state, mat, occ[...].reshape(1, 1, occ.shape[-1]), out, *scratch[-2:])
+    elastic(state, mat, occ[pl.ds(0, 1), :].reshape(1, 1, occ.shape[-1]), out, *scratch[-2:])
 
 
 def idle(*refs):
@@ -409,7 +434,7 @@
 
 
 def first_step(state, mat, occ, base, sel, recv, low, high, out, send, up, down, *scratch):
-    filled = occ[...].reshape(1, 1, occ.shape[-1])
+    filled = occ[pl.ds(0, 1), :].reshape(1, 1, occ.shape[-1])
     fills = (low[pl.ds(192, 1), :], high[pl.ds(192, 1), :])
     advance(state, mat, filled, base, recv, sel, low, high, fills, out, *scratch[:3])
     dil = scratch[3]
@@ -419,7 +444,7 @@
 
 
 def last_step(state, mat, occ, base, sel, recv, low, high, fill_low, fill_high, out, *scratch):
-    filled = occ[...].reshape(1, 1, occ.shape[-1])
+    filled = occ[pl.ds(0, 1), :].reshape(1, 1, occ.shape[-1])
     fills = (fill_low[pl.ds(192, 1), :], fill_high[pl.ds(192, 1), :])
     advance(state, mat, filled, base, recv, sel, low, high, fills, out, *scratch)
 
@@ -464,11 +489,11 @@
 
 
 def inner_first(q_count):
-    def body(phi, kap, out, edges, middle):
+    def body(phi, kap, out, edges, *scratch):
         def put(x, layer):
             out[layer_rows(x), :] = layer
 
-        inner_sweeps(phi, kap, middle, edges, put, q_count)
+        inner_sweeps(phi, kap, scratch[0], edges, put, *scratch[1:], q_count)
 
     return body
 
@@ -493,7 +518,7 @@
 
 
 def inner_last(q_count, tiles):
-    def body(phi, kap, out, edges, middle):
+    def body(phi, kap, out, edges, *scratch):
         tables = tables_out()
         rows = 16 * tiles
 
@@ -501,7 +526,7 @@
             spot = pl.ds(pl.multiple_of(x * rows, 8), rows)
             out[spot, :] = layer_from_octants(layer, tables, tiles)
 
-        inner_sweeps(phi, kap, middle, edges, put, q_count)
+        inner_sweeps(phi, kap, scratch[0], edges, put, *scratch[1:], q_count)
 
     return body
 
@@ -540,7 +565,6 @@
     grp_at = grp.reshape(1)
     current = state.reshape(1536, e)
     mat = material.reshape(1536, e)
-    occ = occupied.astype(F32).reshape(1, e)
     col = brick_column.reshape(1, e)
     octant = brick_octant.reshape(1, e)
     layers, ends, halo = shape_of((2048, LANES)), shape_of((512, LANES)), shape_of((256, LANES))
@@ -566,19 +590,28 @@
     def swap(block):
         return lax.all_to_all(block, "blk", split_axis=0, concat_axis=0, tiled=True)
 
-    send, sel, field, phi, up, down = call(
+    send, sel, occ, field, phi, up, down = call(
         prepare(n_blk, cap, tiles, solvent),
-        (grp_at, current, occ, col, octant),
+        (grp_at, current, occupied.reshape(1, e), col, octant),
         (
             shape_of((slots, 512 + LANES), BF16),
             shape_of((slots, e), BF16),
+            shape_of((8, e)),
             shape_of((512, 4 * q_count), BF16),
             layers,
             side,
             side,
         ),
-        [pltpu.VMEM((512, e), BF16)],
+        [
+            pltpu.VMEM((512, e), BF16),
+            pltpu.VMEM((3, 1, e), jnp.int32),
+            pltpu.VMEM(layers.shape, F32),
+            pltpu.SemaphoreType.DMA((3,)),
+            pltpu.SemaphoreType.DMA((1,)),
+        ],
         smem=1,
+        away=(2, 3, 4),
+        unused=(4,),
     )
     recv = swap(send)
     fields = []
@@ -586,7 +619,7 @@
         fields.append(lax.ppermute(field, axes, pairs(True, g)))
     side_low, side_high = both_ways(up, down, groups)
     work = [pltpu.VMEM((512, e), F32), pltpu.VMEM((1536, e), F32), pltpu.VMEM((1536, e), F32)]
-    middle = pltpu.VMEM(layers.shape, F32)
+    sweeping = [pltpu.VMEM(layers.shape, F32)] + [pltpu.VMEM((16, 8, LANES), F32)] * 2
 
     def gathered(g):
         def run():
@@ -633,7 +666,7 @@
             deposit(False), (phi, kap_edge, *arrived), (layers, wide, wide, tile, flat), unused=(4,)
         )
         low, high = both_ways(top, bottom, [solvent])
-        inner, mid = call(inner_first(q_count), (added, kap), (layers, ends), [middle])
+        inner, mid = call(inner_first(q_count), (added, kap), (layers, ends), sweeping)
         edge, s0, s1, s2 = call(
             outer_first(q_count),
             (top, bottom, low, high, kap_edge, low, high, mid, inner, hot),
@@ -668,7 +701,7 @@
     def solvent_last():
         added, top, bottom = call(deposit(True), (inner, edge, *back, hot), (layers, halo, halo))
         low, high = both_ways(top, bottom, [solvent])
-        out, mid = call(inner_last(q_count, tiles), (added, kap), (flat, ends), [middle])
+        out, mid = call(inner_last(q_count, tiles), (added, kap), (flat, ends), sweeping)
         (out,) = call(
             outer_last(q_count, tiles),
             (top, bottom, low, high, kap_edge, far_low, far_high, mid, out),

time: 95.8 us -> 94.7 us (0.989)
  no operation moved by 1% of the time
where the time goes in v4:
time: 94.7 us; the launch traced here: 93.9 us
  starting transfers between devices  53.1 us (56%)
  waiting for transfers between devices  22.8 us (24%)
  Pallas kernels  16.2 us (17%)
  local copies, waits for them, and re-layouts  1.58 us (2%)
    all_to_all x4, starting transfers between devices, swap(): return lax.all_to_all(block, 'blk', split_axis=0, concat_axis=0, tiled=True)  20.7 us
    pallas_call x6, Pallas kernels, call(): pl.pallas_call(body, out_shape=outs, in_specs=[ANY if n in away else spec...  16.2 us
    ppermute x3, starting transfers between devices, shards(): lax.ppermute(block, axes, pairs(False, g) + pairs(True, g))  11.2 us
    all_to_all x4, waiting for transfers between devices, swap(): return lax.all_to_all(block, 'blk', split_axis=0, concat_axis=0, tiled=True)  10 us
    ppermute x3, starting transfers between devices, shards(): arrived.append(lax.ppermute(recv, axes, pairs(False, g)))  8.15 us
    ppermute x2, starting transfers between devices, both_ways(): lax.ppermute(up, axes, planes(True, which))  7.86 us
    ppermute x2, waiting for transfers between devices, both_ways(): lax.ppermute(down, axes, planes(False, which))  6.01 us
    ppermute x3, waiting for transfers between devices, shards(): lax.ppermute(block, axes, pairs(False, g) + pairs(True, g))  3.56 us
  transfers between devices with their start and end apart: 17, of which 7 were waited for; matrix products, arithmetic and copies ran while one was open for 0% of the time, Pallas kernels for 5%

profile of v4, /device:TPU:1, one launch (start us, length us, event | category | flops | bytes accessed | tf_op | source)
XLA Modules:
  0.0 93.9 jit_solution(15452060360256403737)
XLA Ops:
  0.7 2.8 %shard_map.57 = (bf16[256,640]{1,0:T(8,128)(2,1)}, bf16[256,128]{1,0:T(8,128)(2,1)S(1)}, f32[8,128]{1,0:T(8,128)S(1)}, bf16[512,384]{1,0:T(8,128)(2,1)S(1)}, f32...) custom-call(s32[1]{0:T(128)} %bitcast.15.grp, f32[1536,128]{1,0:T(8,128)} %bitcast.34, ...), custom_call_target="tpu_custom_call" | custom-call | tf_op jit(solution)/shard_map/pallas_call | solution.py:32
  3.5 6.4 %all-to-all-start.6 = ((bf16[8,32,640]{2,1,0:T(8,128)(2,1)}), bf16[8,32,640]{2,1,0:T(8,128)(2,1)S(1)}, u32[]{:S(2)}, u32[]{:S(2)}) async-start(bf16[8,32,640]{2,1,0:T(8,128)(2,1)} %bitcast.20), calls=%async_computation.6 | async-start | bytes 655360 | tf_op jit(solution)/shard_map/all_to_all | solution.py:591
  12.6 5.6 %all-to-all-done.6 = bf16[8,32,640]{2,1,0:T(8,128)(2,1)S(1)} async-done(((bf16[8,32,640]{2,1,0:T(8,128)(2,1)}), bf16[8,32,640]{2,1,0:T(8,128)(2,1)S(1)}, u32[]{:S(2)}, u32[]{:S(2)}) %all-to-all-start.6) | async-done | bytes 327712 | tf_op jit(solution)/shard_map/all_to_all | solution.py:591
  18.2 2.6 %collective-permute-done.11 = bf16[512,384]{1,0:T(8,128)(2,1)S(1)} collective-permute-done((bf16[512,384]{1,0:T(8,128)(2,1)S(1)}, bf16[512,384]{1,0:T(8,128)(2,1)S(1)}, u32[]{:S(2)}, u32[]{:S(2)}) %collective-permute-start.11) | collective-permute-done | bytes 393248 | tf_op jit(solution)/shard_map/ppermute | solution.py:619
  21.8 5.4 %all-to-all-start.7 = ((bf16[8,32,512]{2,1,0:T(8,128)(2,1)}), bf16[8,32,512]{2,1,0:T(8,128)(2,1)}, u32[]{:S(2)}, u32[]{:S(2)}) async-start(bf16[8,32,512]{2,1,0:T(8,128)(2,1)} %bitcast.22), calls=%async_computation.7 | async-start | bytes 524288 | tf_op jit(solution)/shard_map/all_to_all | solution.py:591
  28.6 5.4 %collective-permute-start.16 = (bf16[256,640]{1,0:T(8,128)(2,1)S(1)}, bf16[256,640]{1,0:T(8,128)(2,1)}, u32[]{:S(2)}, u32[]{:S(2)}) collective-permute-start(bf16[256,640]{1,0:T(8,128)(2,1)S(1)} %bitcast.41), channel_id=1, source_target_pairs={{8,24},{9,25},{10,26},{11,27},{12,28},{13,29},{14,30},{15,31}} | collective-permute-start | bytes 983048 | tf_op jit(solution)/shard_map/ppermute | solution.py:638
  35.4 4.0 %collective-permute-start.13 = (f32[200,128]{1,0:T(8,128)S(1)}, f32[200,128]{1,0:T(8,128)}, u32[]{:S(2)}, u32[]{:S(2)}) collective-permute-start(f32[200,128]{1,0:T(8,128)S(1)} %get-tuple-element.290), channel_id=1, source_target_pairs={{0,1},{1,2},{2,3},{3,4},{4,5},{5,6},{6,7},{8,9},{9,10},{10,11},{11... | collective-permute-start | bytes 307208 | tf_op jit(solution)/shard_map/ppermute | solution.py:586
  40.7 2.0 %conditional.7 = ((f32[2048,128]{1,0:T(8,128)S(1)}, f32[512,128]{1,0:T(8,128)S(1)})) conditional(s32[]{:T(128)} %convert_element_type.2, (f32[1536,128]{1,0:T(8,128)S(1)}, f32[1536,128]{1,0:T(8,128)S(1)}, f32[8,128]{1,0:T(8,128)S(1)}) %tuple.107, f32[1536,128]{1,0:T(8,128)S(1)} %bitcast.27), branch_computations={%region_0.0_spmd, %region_1.0_spmd} | conditional | bytes 8 | solution.py:659
  40.7 2.0 %branch_0_fun.5 = (f32[2048,128]{1,0:T(8,128)S(1)}, f32[512,128]{1,0:T(8,128)S(1)}) custom-call(f32[1536,128]{1,0:T(8,128)S(1)} %get-tuple-element.150.state, f32[1536,128]{1,0:T(8,128)S(1)} %get-tuple-element.151.mat, f32[8,128]{1,0:T(8,128)S(1)} %get-tuple-element.152.occ), custom_call_target="tpu_custom_call" | custom-call | tf_op jit(solution)/shard_map/cond/branch_0_fun/pallas_call | solution.py:32
  42.7 2.1 %collective-permute-done.14 = f32[200,128]{1,0:T(8,128)} collective-permute-done((f32[200,128]{1,0:T(8,128)S(1)}, f32[200,128]{1,0:T(8,128)}, u32[]{:S(2)}, u32[]{:S(2)}) %collective-permute-start.14) | collective-permute-done | bytes 102432 | tf_op jit(solution)/shard_map/ppermute | solution.py:587
  44.9 5.0 %conditional.8 = ((f32[2048,128]{1,0:T(8,128)S(1)}, bf16[256,512]{1,0:T(8,128)(2,1)}, f32[192,128]{1,0:T(8,128)}, f32[192,128]{1,0:T(8,128)})) conditional(s32[]{:T(128)} %convert_element_type.2, (bf16[8,32,512]{2,1,0:T(8,128)(2,1)}, f32[1536,128]{1,0:T(8,128)S(1)}, f32[1536,128]{1,0:T(8,128)S(1)}, f32[8,128]{1,0:T(8,128)S(1)}, ...), branch_computations={%region_6.0_spmd, %region_7.0_spmd} | conditional | bytes 3145764 | solution.py:662
  45.8 4.1 %branch_0_fun.7 = (f32[2048,128]{1,0:T(8,128)S(1)}, bf16[256,512]{1,0:T(8,128)(2,1)}, f32[192,128]{1,0:T(8,128)}, f32[192,128]{1,0:T(8,128)}) custom-call(f32[1536,128]{1,0:T(8,128)} %copy-done.5, f32[1536,128]{1,0:T(8,128)S(1)} %get-tuple-element.160.mat, f32[8,128]{1,0:T(8,128)S(1)} %get-tuple-element.161.occ, f32[2048,128]{1,0:T(8,128)S(1)} %get-tuple-element.162.base, ...), custom_call_target="tpu_custom_call" | custom-call | tf_op jit(solution)/shard_map/cond/branch_0_fun/pallas_call | solution.py:32
  49.9 12.0 %conditional.9 = (f32[2048,128]{1,0:T(8,128)}, f32[512,128]{1,0:T(8,128)S(1)}, bf16[768,128]{1,0:T(8,128)(2,1)}, f32[1536,128]{1,0:T(8,128)}, f32[384,128]{1,0:T...) conditional(s32[]{:T(128)} %clamp.7, ...), branch_computations={%region_8.0_spmd, %region_9.0_spmd, %region_10.0_spmd, %region_11.... | conditional | bytes 5767348 | solution.py:695
  49.9 4.7 %all-to-all-start.1 = ((bf16[8,32,512]{2,1,0:T(8,128)(2,1)}), bf16[8,32,512]{2,1,0:T(8,128)(2,1)}, u32[]{:S(2)}, u32[]{:S(2)}) async-start(bf16[8,32,512]{2,1,0:T(8,128)(2,1)} %bitcast.3), calls=%async_computation.1 | async-start | bytes 524288 | tf_op jit(solution)/shard_map/cond/branch_1_fun/all_to_all | solution.py:591
  54.6 2.8 %branch_1_fun.10 = (f32[1536,128]{1,0:T(8,128)}, f32[2048,128]{1,0:T(8,128)}, f32[512,128]{1,0:T(8,128)S(1)}, bf16[768,128]{1,0:T(8,128)(2,1)}, f32[384,128]{1,0...) custom-call(f32[2048,128]{1,0:T(8,128)S(1)} %get-tuple-element.179.state, ...), custom_call_target="tpu_custom_call" | custom-call | tf_op jit(solution)/shard_map/cond/branch_1_fun/pallas_call | solution.py:32
  57.4 4.4 %all-to-all-done.1 = bf16[8,32,512]{2,1,0:T(8,128)(2,1)} async-done(((bf16[8,32,512]{2,1,0:T(8,128)(2,1)}), bf16[8,32,512]{2,1,0:T(8,128)(2,1)}, u32[]{:S(2)}, u32[]{:S(2)}) %all-to-all-start.1) | async-done | bytes 262176 | tf_op jit(solution)/shard_map/cond/branch_1_fun/all_to_all | solution.py:591
  63.2 8.4 %collective-permute-start.19 = (bf16[256,512]{1,0:T(8,128)(2,1)}, bf16[256,512]{1,0:T(8,128)(2,1)}, u32[]{:S(2)}, u32[]{:S(2)}) collective-permute-start(bf16[256,512]{1,0:T(8,128)(2,1)} %get-tuple-element.300), channel_id=1, source_target_pairs={{8,24},{9,25},{10,26},{11,27},{12,28},{13,29},{14,30},{15,31},{24,... | collective-permute-start | bytes 786440 | tf_op jit(solution)/shard_map/ppermute | solution.py:697
  73.1 3.6 %collective-permute-done.19 = bf16[256,512]{1,0:T(8,128)(2,1)} collective-permute-done((bf16[256,512]{1,0:T(8,128)(2,1)}, bf16[256,512]{1,0:T(8,128)(2,1)}, u32[]{:S(2)}, u32[]{:S(2)}) %collective-permute-start.19) | collective-permute-done | bytes 262176 | tf_op jit(solution)/shard_map/ppermute | solution.py:697
  76.6 17.3 %conditional.10 = (f32[1,3,512,128]{3,2,1,0:T(8,128)}) conditional(s32[]{:T(128)} %convert_element_type.2, (s32[]{:T(128)}, bf16[256,512]{1,0:T(8,128)(2,1)}, f32[192,128]{1,0:T(8,128)}, f32[192,128]{1,0:T(8,128)}, bf16[256,512]{1,0:T(8,128)(2,1)}, /*index=5*/bf16[256,512]{1,0:T(8,128)(2,1)}, f32[2048,128]{1,0:T(8,128)S(1)}, ...), branch_computations={%region_12.0_spmd, %region_16.0_spmd} | conditional | flops 1 | bytes 5505340 | solution.py:729
  76.6 13.9 %conditional = (bf16[256,512]{1,0:T(8,128)(2,1)}, f32[192,128]{1,0:T(8,128)}, f32[192,128]{1,0:T(8,128)}) conditional(s32[]{:T(128)} %clamp.1, (bf16[256,512]{1,0:T(8,128)(2,1)}, f32[192,128]{1,0:T(8,128)}, f32[192,128]{1,0:T(8,128)}) %tuple.49, (bf16[256,512]{1,0:T(8,128)(2,1)}, f32[192,128]{1,0:T(8,128)}, ...), branch_computations={%region_13.0_spmd, %region_14.0_spmd, %region_15.0_spmd} | conditional | bytes 2359488 | solution.py:720
  76.7 4.2 %all-to-all-start.4 = ((bf16[8,32,512]{2,1,0:T(8,128)(2,1)}), bf16[8,32,512]{2,1,0:T(8,128)(2,1)}, u32[]{:S(2)}, u32[]{:S(2)}) async-start(bf16[8,32,512]{2,1,0:T(8,128)(2,1)} %bitcast.9), calls=%async_computation.4 | async-start | bytes 524288 | tf_op jit(solution)/shard_map/cond/branch_0_fun/cond/branch_1_fun/all_to_all | solution.py:591
  80.9 3.9 %collective-permute-start.4 = (f32[192,128]{1,0:T(8,128)S(1)}, f32[192,128]{1,0:T(8,128)}, u32[]{:S(2)}, u32[]{:S(2)}) collective-permute-start(f32[192,128]{1,0:T(8,128)S(1)} %copy-done.8), channel_id=1, source_target_pairs={{8,9},{9,10},{10,11},{11,12},{12,13},{13,14},{14,15}} | collective-permute-start | bytes 294920 | tf_op jit(solution)/shard_map/cond/branch_0_fun/cond/branch_1_fun/ppermute | solution.py:586
  86.6 3.9 %collective-permute-done.5 = f32[192,128]{1,0:T(8,128)} collective-permute-done((f32[192,128]{1,0:T(8,128)S(1)}, f32[192,128]{1,0:T(8,128)}, u32[]{:S(2)}, u32[]{:S(2)}) %collective-permute-start.5) | collective-permute-done | bytes 98336 | tf_op jit(solution)/shard_map/cond/branch_0_fun/cond/branch_1_fun/ppermute | solution.py:587
  90.5 3.4 %branch_0_fun.9 = f32[1536,128]{1,0:T(8,128)} custom-call(f32[2048,128]{1,0:T(8,128)S(1)} %get-tuple-element.229.state, f32[1536,128]{1,0:T(8,128)S(1)} %get-tuple-element.230.mat, f32[8,128]{1,0:T(8,128)S(1)} %get-tuple-element.231.occ, f32[1536,128]{1,0:T(8,128)S(1)} %copy-done.7, bf16[256,128]{1,0:T(8,128)(2,1)S(1)} %get-tuple-element.233.sel, ...), custom_call_target="tpu_custom_call" | custom-call | tf_op jit(solution)/shard_map/cond/branch_0_fun/pallas_call | solution.py:32
  (40 shorter events, 15.1 us)
Async XLA Ops:
  0.0 0.7 copy-start.2
  3.5 14.6 %all-to-all-start.6 = ((bf16[8,32,640]{2,1,0:T(8,128)(2,1)}), bf16[8,32,640]{2,1,0:T(8,128)(2,1)S(1)}, u32[]{:S(2)}, u32[]{:S(2)}) async-start(bf16[8,32,640]{2,1,0:T(8,128)(2,1)} %bitcast.20), calls=%async_computation.6 | async-start | bytes 655360 | tf_op jit(solution)/shard_map/all_to_all | solution.py:591
  9.9 2.7 %collective-permute-start.12 = (bf16[512,384]{1,0:T(8,128)(2,1)S(1)}, bf16[512,384]{1,0:T(8,128)(2,1)S(1)}, u32[]{:S(2)}, u32[]{:S(2)}) collective-permute-start(bf16[512,384]{1,0:T(8,128)(2,1)S(1)} %get-tuple-element.285), channel_id=1, source_target_pairs={{24,16},{25,17},{26,18},{27,19},{28,20},{29,21},{30,22},{31,23}} | collective-permute-start | bytes 1179656 | tf_op jit(solution)/shard_map/ppermute | solution.py:619
  10.5 10.2 %collective-permute-start.11 = (bf16[512,384]{1,0:T(8,128)(2,1)S(1)}, bf16[512,384]{1,0:T(8,128)(2,1)S(1)}, u32[]{:S(2)}, u32[]{:S(2)}) collective-permute-start(bf16[512,384]{1,0:T(8,128)(2,1)S(1)} %get-tuple-element.285), channel_id=1, source_target_pairs={{24,8},{25,9},{26,10},{27,11},{28,12},{29,13},{30,14},{31,15}} | collective-permute-start | bytes 1179656 | tf_op jit(solution)/shard_map/ppermute | solution.py:619
  11.8 8.9 %collective-permute-start.10 = (bf16[512,384]{1,0:T(8,128)(2,1)S(1)}, bf16[512,384]{1,0:T(8,128)(2,1)S(1)}, u32[]{:S(2)}, u32[]{:S(2)}) collective-permute-start(bf16[512,384]{1,0:T(8,128)(2,1)S(1)} %get-tuple-element.285), channel_id=1, source_target_pairs={{24,0},{25,1},{26,2},{27,3},{28,4},{29,5},{30,6},{31,7}} | collective-permute-start | bytes 1179656 | tf_op jit(solution)/shard_map/ppermute | solution.py:619
  20.7 19.9 %copy-start.3 = (f32[1,3,512,128]{3,2,1,0:T(8,128)S(1)}, f32[1,3,512,128]{3,2,1,0:T(8,128)}, u32[]{:S(2)}) copy-start(f32[1,3,512,128]{3,2,1,0:T(8,128)} %param.23) | copy-start | bytes 2359300
  20.7 19.9 %copy-start.4 = (f32[1,3,512,128]{3,2,1,0:T(8,128)S(1)}, f32[1,3,512,128]{3,2,1,0:T(8,128)}, u32[]{:S(2)}) copy-start(f32[1,3,512,128]{3,2,1,0:T(8,128)} %param.22) | copy-start | bytes 2359300
  21.8 23.1 %all-to-all-start.7 = ((bf16[8,32,512]{2,1,0:T(8,128)(2,1)}), bf16[8,32,512]{2,1,0:T(8,128)(2,1)}, u32[]{:S(2)}, u32[]{:S(2)}) async-start(bf16[8,32,512]{2,1,0:T(8,128)(2,1)} %bitcast.22), calls=%async_computation.7 | async-start | bytes 524288 | tf_op jit(solution)/shard_map/all_to_all | solution.py:591
  27.2 15.5 %collective-permute-start.17 = (bf16[256,640]{1,0:T(8,128)(2,1)S(1)}, bf16[256,640]{1,0:T(8,128)(2,1)}, u32[]{:S(2)}, u32[]{:S(2)}) collective-permute-start(bf16[256,640]{1,0:T(8,128)(2,1)S(1)} %bitcast.40), channel_id=1, source_target_pairs={{16,24},{17,25},{18,26},{19,27},{20,28},{21,29},{22,30},{23,31}} | collective-permute-start | bytes 983048 | tf_op jit(solution)/shard_map/ppermute | solution.py:638
  28.6 14.1 %collective-permute-start.16 = (bf16[256,640]{1,0:T(8,128)(2,1)S(1)}, bf16[256,640]{1,0:T(8,128)(2,1)}, u32[]{:S(2)}, u32[]{:S(2)}) collective-permute-start(bf16[256,640]{1,0:T(8,128)(2,1)S(1)} %bitcast.41), channel_id=1, source_target_pairs={{8,24},{9,25},{10,26},{11,27},{12,28},{13,29},{14,30},{15,31}} | collective-permute-start | bytes 983048 | tf_op jit(solution)/shard_map/ppermute | solution.py:638
  34.0 8.7 %collective-permute-start.15 = (bf16[256,640]{1,0:T(8,128)(2,1)S(1)}, bf16[256,640]{1,0:T(8,128)(2,1)}, u32[]{:S(2)}, u32[]{:S(2)}) collective-permute-start(bf16[256,640]{1,0:T(8,128)(2,1)S(1)} %bitcast.42), channel_id=1, source_target_pairs={{0,24},{1,25},{2,26},{3,27},{4,28},{5,29},{6,30},{7,31}} | collective-permute-start | bytes 983048 | tf_op jit(solution)/shard_map/ppermute | solution.py:638
  35.4 7.4 %collective-permute-start.13 = (f32[200,128]{1,0:T(8,128)S(1)}, f32[200,128]{1,0:T(8,128)}, u32[]{:S(2)}, u32[]{:S(2)}) collective-permute-start(f32[200,128]{1,0:T(8,128)S(1)} %get-tuple-element.290), channel_id=1, source_target_pairs={{0,1},{1,2},{2,3},{3,4},{4,5},{5,6},{6,7},{8,9},{9,10},{10,11},{11... | collective-permute-start | bytes 307208 | tf_op jit(solution)/shard_map/ppermute | solution.py:586
  39.4 5.5 %collective-permute-start.14 = (f32[200,128]{1,0:T(8,128)S(1)}, f32[200,128]{1,0:T(8,128)}, u32[]{:S(2)}, u32[]{:S(2)}) collective-permute-start(f32[200,128]{1,0:T(8,128)S(1)} %get-tuple-element.291), channel_id=1, source_target_pairs={{1,0},{2,1},{3,2},{4,3},{5,4},{6,5},{7,6},{9,8},{10,9},{11,10},{12... | collective-permute-start | bytes 307208 | tf_op jit(solution)/shard_map/ppermute | solution.py:587
  44.9 0.9 copy-start.5
  49.9 12.0 %all-to-all-start.1 = ((bf16[8,32,512]{2,1,0:T(8,128)(2,1)}), bf16[8,32,512]{2,1,0:T(8,128)(2,1)}, u32[]{:S(2)}, u32[]{:S(2)}) async-start(bf16[8,32,512]{2,1,0:T(8,128)(2,1)} %bitcast.3), calls=%async_computation.1 | async-start | bytes 524288 | tf_op jit(solution)/shard_map/cond/branch_1_fun/all_to_all | solution.py:591
  61.9 11.2 %collective-permute-start.18 = (bf16[256,512]{1,0:T(8,128)(2,1)}, bf16[256,512]{1,0:T(8,128)(2,1)}, u32[]{:S(2)}, u32[]{:S(2)}) collective-permute-start(bf16[256,512]{1,0:T(8,128)(2,1)} %get-tuple-element.297), channel_id=1, source_target_pairs={{0,24},{1,25},{2,26},{3,27},{4,28},{5,29},{6,30},{7,31},{24,0},{25... | collective-permute-start | bytes 786440 | tf_op jit(solution)/shard_map/ppermute | solution.py:697
  63.2 13.4 %collective-permute-start.19 = (bf16[256,512]{1,0:T(8,128)(2,1)}, bf16[256,512]{1,0:T(8,128)(2,1)}, u32[]{:S(2)}, u32[]{:S(2)}) collective-permute-start(bf16[256,512]{1,0:T(8,128)(2,1)} %get-tuple-element.300), channel_id=1, source_target_pairs={{8,24},{9,25},{10,26},{11,27},{12,28},{13,29},{14,30},{15,31},{24,... | collective-permute-start | bytes 786440 | tf_op jit(solution)/shard_map/ppermute | solution.py:697
  71.7 4.9 %collective-permute-start.20 = (bf16[256,512]{1,0:T(8,128)(2,1)}, bf16[256,512]{1,0:T(8,128)(2,1)}, u32[]{:S(2)}, u32[]{:S(2)}) collective-permute-start(bf16[256,512]{1,0:T(8,128)(2,1)} %get-tuple-element.301), channel_id=1, source_target_pairs={{16,24},{17,25},{18,26},{19,27},{20,28},{21,29},{22,30},{23,31},{2... | collective-permute-start | bytes 786440 | tf_op jit(solution)/shard_map/ppermute | solution.py:697
  76.6 13.9 %copy-start.7 = (f32[1536,128]{1,0:T(8,128)S(1)}, f32[1536,128]{1,0:T(8,128)}, u32[]{:S(2)}) copy-start(f32[1536,128]{1,0:T(8,128)} %get-tuple-element.232.base) | copy-start | bytes 2359300 | tf_op jit(solution)/shard_map/cond
  76.6 4.2 %copy-start.8 = (f32[192,128]{1,0:T(8,128)S(1)}, f32[192,128]{1,0:T(8,128)}, u32[]{:S(2)}) copy-start(f32[192,128]{1,0:T(8,128)} %get-tuple-element.224) | copy-start | bytes 294916 | tf_op jit(solution)/shard_map/cond/branch_0_fun/cond
  76.6 8.1 %copy-start.10 = (f32[192,128]{1,0:T(8,128)S(1)}, f32[192,128]{1,0:T(8,128)}, u32[]{:S(2)}) copy-start(f32[192,128]{1,0:T(8,128)} %get-tuple-element.225) | copy-start | bytes 294916 | tf_op jit(solution)/shard_map/cond/branch_0_fun/cond
  76.7 13.8 %all-to-all-start.4 = ((bf16[8,32,512]{2,1,0:T(8,128)(2,1)}), bf16[8,32,512]{2,1,0:T(8,128)(2,1)}, u32[]{:S(2)}, u32[]{:S(2)}) async-start(bf16[8,32,512]{2,1,0:T(8,128)(2,1)} %bitcast.9), calls=%async_computation.4 | async-start | bytes 524288 | tf_op jit(solution)/shard_map/cond/branch_0_fun/cond/branch_1_fun/all_to_all | solution.py:591
  80.9 5.8 %collective-permute-start.4 = (f32[192,128]{1,0:T(8,128)S(1)}, f32[192,128]{1,0:T(8,128)}, u32[]{:S(2)}, u32[]{:S(2)}) collective-permute-start(f32[192,128]{1,0:T(8,128)S(1)} %copy-done.8), channel_id=1, source_target_pairs={{8,9},{9,10},{10,11},{11,12},{12,13},{13,14},{14,15}} | collective-permute-start | bytes 294920 | tf_op jit(solution)/shard_map/cond/branch_0_fun/cond/branch_1_fun/ppermute | solution.py:586
  84.7 5.8 %collective-permute-start.5 = (f32[192,128]{1,0:T(8,128)S(1)}, f32[192,128]{1,0:T(8,128)}, u32[]{:S(2)}, u32[]{:S(2)}) collective-permute-start(f32[192,128]{1,0:T(8,128)S(1)} %copy-done.10), channel_id=1, source_target_pairs={{9,8},{10,9},{11,10},{12,11},{13,12},{14,13},{15,14}} | collective-permute-start | bytes 294920 | tf_op jit(solution)/shard_map/cond/branch_0_fun/cond/branch_1_fun/ppermute | solution.py:587
  (2 other events, 1.3 us)

commit v5 on v4

--- a/solution.py
+++ b/solution.py
@@ -68,12 +68,16 @@
 
 
 def slab(ref, c, i):
-    rows = ref[pl.ds(c * 512 + 64 * i, 64), :]
+    rows = ref[c, pl.ds(64 * i, 64), :] if len(ref.shape) == 3 else ref[pl.ds(c * 512 + 64 * i, 64), :]
     return rows.reshape(8, 8, rows.shape[-1])
 
 
 def put_slab(ref, c, i, value):
-    ref[pl.ds(c * 512 + 64 * i, 64), :] = value.reshape(64, value.shape[-1])
+    value = value.reshape(64, value.shape[-1])
+    if len(ref.shape) == 3:
+        ref[c, pl.ds(64 * i, 64), :] = value
+    else:
+        ref[pl.ds(c * 512 + 64 * i, 64), :] = value
 
 
 def gradients(ref, i):
@@ -124,8 +128,8 @@
 
 def put_faces(ref, up, down):
     for c in range(3):
-        up[pl.ds(64 * c, 64), :] = ref[pl.ds(c * 512 + 448, 64), :]
-        down[pl.ds(64 * c, 64), :] = ref[pl.ds(c * 512, 64), :]
+        up[pl.ds(64 * c, 64), :] = slab(ref, c, 7).reshape(64, ref.shape[-1])
+        down[pl.ds(64 * c, 64), :] = slab(ref, c, 0).reshape(64, ref.shape[-1])
 
 
 def elastic(ref, mat, filled, out, stress, partial):
@@ -169,22 +173,53 @@
             put_slab(out, a, i, force)
 
 
-def advance(ref, mat, filled, base, recv, sel, low, high, fills, out, pressure, stress, partial):
+CHUNKS = 4
+
+
+class Stream:
+    def __init__(self, state, base, mat, out, held, forces, mobility, result, sems):
+        part = 512 // CHUNKS
+        self.state, self.base, self.out, self.mob = [], [], [], []
+        for n in range(CHUNKS):
+            rows = pl.ds(part * n, part)
+            whole = (pl.ds(0, 3), rows)
+            copy = pltpu.make_async_copy
+            self.state.append(copy(state.at[whole], held.at[whole], sems.at[0, n]))
+            self.base.append(copy(base.at[whole], forces.at[whole], sems.at[1, n]))
+            self.mob.append(copy(mat.at[2, rows], mobility.at[0, rows], sems.at[2, n]))
+            self.out.append(copy(result.at[whole], out.at[whole], sems.at[3, n]))
+        for n in range(CHUNKS):
+            self.state[n].start()
+            self.base[n].start()
+        for n in range(CHUNKS):
+            self.mob[n].start()
+
+
+def advance(stream, held, forces, mobility, result, filled, recv, sel, low, high, fills, *scratch):
+    pressure, stress, partial = scratch
     e = filled.shape[-1]
+    per = 8 // CHUNKS
     pressure[...] = dot(recv[...], sel[...], ((0,), (0,))) * PRESSURE_SCALE
+    stream.state[0].wait()
     for i in range(8):
-        cof = cofactors(gradients(ref, i))
+        if i % per == per - 1 and i < 7:
+            stream.state[i // per + 1].wait()
+        if i % per == 0:
+            stream.base[i // per].wait()
+        cof = cofactors(gradients(held, i))
         p = pressure[pl.ds(64 * i, 64), :].reshape(8, 8, e)
         for a in range(3):
             first = [p * cof[a][b] for b in range(3)]
             put_slab(stress, a, i, first[0])
-            put_slab(partial, a, i, slab(base, a, i) - (diff_j(first[1]) + diff_k(first[2])))
+            put_slab(partial, a, i, slab(forces, a, i) - (diff_j(first[1]) + diff_k(first[2])))
     penalty = PENALTY * UNIT_LENGTH
     fill_low, fill_high = fills[0].reshape(1, 1, e), fills[1].reshape(1, 1, e)
     for i in range(8):
-        rate = (TIME_STEP / UNIT_LENGTH) * slab(mat, 2, i) * filled
+        if i % per == 0:
+            stream.mob[i // per].wait()
+        rate = (TIME_STEP / UNIT_LENGTH) * slab(mobility, 0, i) * filled
         for a in range(3):
-            here = slab(ref, a, i)
+            here = slab(held, a, i)
             force = slab(partial, a, i) - diff_i(
                 slab(stress, a, i - 1) if i > 0 else None,
                 slab(stress, a, i),
@@ -196,7 +231,9 @@
             if i == 7:
                 other = high[pl.ds(64 * a, 64), :].reshape(8, 8, e)
                 force = force + penalty * fill_high * (other - here)
-            put_slab(out, a, i, here + rate * force)
+            put_slab(result, a, i, here + rate * force)
+        if i % per == per - 1:
+            stream.out[i // per].start()
 
 
 def permute_in(x, tables):
@@ -344,10 +381,10 @@
     k = [load(kap_edge, n) for n in range(4)]
     m = [load(middle, n) for n in range(4)]
     first = [load(low, 0), load(low, 1), load(bottom, 0), load(bottom, 1)]
-    first = sweep_chain(first, [load(kap_low, 2), k[0]], masks)
+    first = sweep_chain(first, [load(kap_low, 0), k[0]], masks)
     first = sweep_chain([*first, m[0], m[1]], k[:2], masks)
     last = [load(top, 0), load(top, 1), load(high, 0), load(high, 1)]
-    last = sweep_chain(last, [k[3], load(kap_high, 2)], masks)
+    last = sweep_chain(last, [k[3], load(kap_high, 0)], masks)
     last = sweep_chain([m[2], m[3], *last], k[2:], masks)
     return [layer.reshape(LANES, LANES) for layer in first + last]
 
@@ -409,8 +446,10 @@
 
 
 def rates(tiles):
-    def body(mat, kap, edge):
+    def body(mat, kap, edge, up, down):
         to_octants(mat, kap, 0.5 * SWEEP_STEP, tables_in(), tiles)
+        up[...] = kap[layer_rows(15), :]
+        down[...] = kap[layer_rows(0), :]
         for n, x in enumerate((0, 1, 14, 15)):
             edge[layer_rows(n), :] = kap[layer_rows(x), :]
 
@@ -433,20 +472,27 @@
     pass
 
 
-def first_step(state, mat, occ, base, sel, recv, low, high, out, send, up, down, *scratch):
+def first_step(state, base, mat, occ, sel, recv, low, high, out, send, up, down, *scratch):
+    *work, dil, held, forces, mobility, result, sems = scratch
+    stream = Stream(state, base, mat, out, held, forces, mobility, result, sems)
     filled = occ[pl.ds(0, 1), :].reshape(1, 1, occ.shape[-1])
     fills = (low[pl.ds(192, 1), :], high[pl.ds(192, 1), :])
-    advance(state, mat, filled, base, recv, sel, low, high, fills, out, *scratch[:3])
-    dil = scratch[3]
-    dilate(out, filled, dil)
+    advance(stream, held, forces, mobility, result, filled, recv, sel, low, high, fills, *work)
+    dilate(result, filled, dil)
     send[...] = dot(sel[...], dil[...], ((1,), (1,))).astype(BF16)
-    put_faces(out, up, down)
-
-
-def last_step(state, mat, occ, base, sel, recv, low, high, fill_low, fill_high, out, *scratch):
+    put_faces(result, up, down)
+    for copy in stream.out:
+        copy.wait()
+
+
+def last_step(state, base, mat, occ, sel, recv, low, high, fill_low, fill_high, out, *scratch):
+    *work, held, forces, mobility, result, sems = scratch
+    stream = Stream(state, base, mat, out, held, forces, mobility, result, sems)
     filled = occ[pl.ds(0, 1), :].reshape(1, 1, occ.shape[-1])
     fills = (fill_low[pl.ds(192, 1), :], fill_high[pl.ds(192, 1), :])
-    advance(state, mat, filled, base, recv, sel, low, high, fills, out, *scratch)
+    advance(stream, held, forces, mobility, result, filled, recv, sel, low, high, fills, *work)
+    for copy in stream.out:
+        copy.wait()
 
 
 def deposit(edged):
@@ -454,9 +500,7 @@
         if edged:
             edge, v0, v1, v2, tile, out, up, down = refs
         else:
-            border, v0, v1, v2, out, up, down, tile, _ = refs
-            down[layer_rows(2), :] = border[layer_rows(0), :]
-            up[layer_rows(2), :] = border[layer_rows(3), :]
+            v0, v1, v2, out, up, down, tile, *_ = refs
         total = None
         for n, v in enumerate((v0, v1, v2)):
             spot = pl.ds(n * v.shape[0], v.shape[0])
@@ -569,7 +613,7 @@
     octant = brick_octant.reshape(1, e)
     layers, ends, halo = shape_of((2048, LANES)), shape_of((512, LANES)), shape_of((256, LANES))
     rows, flat = shape_of((slots, 512), BF16), shape_of((1536, e))
-    face, side, wide = shape_of((192, e)), shape_of((200, e)), shape_of((384, e))
+    face, side, one = shape_of((192, e)), shape_of((200, e)), shape_of((LANES, LANES))
     tile = shape_of((slots * (n_grp - 1), LANES), BF16)
 
     def pairs(back, g):
@@ -619,6 +663,13 @@
         fields.append(lax.ppermute(field, axes, pairs(True, g)))
     side_low, side_high = both_ways(up, down, groups)
     work = [pltpu.VMEM((512, e), F32), pltpu.VMEM((1536, e), F32), pltpu.VMEM((1536, e), F32)]
+    streaming = [
+        pltpu.VMEM((3, 512, e), F32),
+        pltpu.VMEM((3, 512, e), F32),
+        pltpu.VMEM((1, 512, e), F32),
+        pltpu.VMEM((3, 512, e), F32),
+        pltpu.SemaphoreType.DMA((4, CHUNKS)),
+    ]
     sweeping = [pltpu.VMEM(layers.shape, F32)] + [pltpu.VMEM((16, 8, LANES), F32)] * 2
 
     def gathered(g):
@@ -638,61 +689,77 @@
         arrived.append(lax.ppermute(recv, axes, pairs(False, g)))
 
     def solvent_rates():
-        return tuple(call(rates(tiles), (mat,), (layers, ends)))
+        kap, edge, up, down = call(rates(tiles), (mat,), (layers, ends, one, one))
+        return kap, edge, *both_ways(up, down, [solvent])
 
     def mech_elastic():
-        return tuple(
-            call(elastic_forces, (current, mat, occ), (layers, ends), work[1:], unused=(1,))
-        )
+        outs = (layers, ends, one, one)
+        args = (current, mat, occ)
+        return tuple(call(elastic_forces, args, outs, work[1:], unused=(1, 2, 3)))
 
     def mech_first():
         return tuple(
             call(
                 first_step,
-                (current, mat, occ, base, sel, mine, side_low, side_high),
-                (layers, rows, face, face),
-                work + [pltpu.VMEM((512, e), BF16)],
+                (
+                    current.reshape(3, 512, e),
+                    base.reshape(4, 512, e),
+                    mat.reshape(3, 512, e),
+                    occ,
+                    sel,
+                    mine,
+                    side_low,
+                    side_high,
+                ),
+                (shape_of((4, 512, e)), rows, face, face),
+                work + [pltpu.VMEM((512, e), BF16)] + streaming,
+                away=(0, 1, 2),
+                unused=(0,),
             )
         )
 
     is_solvent = grp == solvent
-    base, kap_edge = lax.cond(is_solvent, solvent_rates, mech_elastic)
+    base, kap_edge, far_low, far_high = lax.cond(is_solvent, solvent_rates, mech_elastic)
     kap = base
-    idle_first = lambda: tuple(nothing(layers, rows, face, face)())
+    idle_first = lambda: tuple(nothing(shape_of((4, 512, e)), rows, face, face)())
     moved, send, fore, aft = lax.cond(is_solvent, idle_first, mech_first)
 
     def solvent_first():
-        added, top, bottom, hot, spare = call(
-            deposit(False), (phi, kap_edge, *arrived), (layers, wide, wide, tile, flat), unused=(4,)
+        added, top, bottom, hot, *spare = call(
+            deposit(False),
+            (phi, *arrived),
+            (layers, halo, halo, tile, flat, face, face),
+            unused=(4, 5, 6),
         )
         low, high = both_ways(top, bottom, [solvent])
         inner, mid = call(inner_first(q_count), (added, kap), (layers, ends), sweeping)
         edge, s0, s1, s2 = call(
             outer_first(q_count),
-            (top, bottom, low, high, kap_edge, low, high, mid, inner, hot),
+            (top, bottom, low, high, kap_edge, far_low, far_high, mid, inner, hot),
             (ends, rows, rows, rows),
             [pltpu.VMEM((512, 4 * LANES), BF16)],
         )
-        return inner, edge, hot, spare, low, high, s0, s1, s2
+        return inner, edge, hot, *spare, s0, s1, s2
 
     def mech_turn(g):
         def run():
             mine = swap(send)
+            low, high = both_ways(fore, aft, [g])
             force, *spare = call(
                 elastic_forces,
-                (moved, mat, occ),
-                (flat, layers, ends, tile, wide, wide, rows, rows),
+                (moved.reshape(2048, e), mat, occ),
+                (flat, layers, ends, tile, rows, rows),
                 work[1:],
-                unused=range(1, 8),
+                unused=range(1, 6),
             )
-            blocks = list(spare[5:])
+            blocks = list(spare[3:])
             blocks.insert(g, mine)
-            return *spare[:3], force, *spare[3:5], *blocks
+            return *spare[:3], force, low, high, *blocks
 
         return run
 
     turns = [mech_turn(g) for g in groups] + [solvent_first]
-    inner, edge, hot, force, far_low, far_high, *blocks = lax.switch(grp, turns)
+    inner, edge, hot, force, face_low, face_high, *blocks = lax.switch(grp, turns)
     back = [
         lax.ppermute(block, axes, pairs(False, g) + pairs(True, g))
         for g, block in zip(groups, blocks)
@@ -714,17 +781,30 @@
         return out
 
     def swapped(g):
-        return lambda: (swap(back[g]), *both_ways(fore, aft, [g]))
+        return lambda: swap(back[g])
 
     def mech_last():
-        mine, low, high = lax.switch(grp, [swapped(g) for g in groups])
+        mine = lax.switch(grp, [swapped(g) for g in groups])
         (out,) = call(
             last_step,
-            (moved, mat, occ, force, sel, mine, low, high, side_low, side_high),
-            (flat,),
-            work,
+            (
+                moved,
+                force.reshape(3, 512, e),
+                mat.reshape(3, 512, e),
+                occ,
+                sel,
+                mine,
+                face_low,
+                face_high,
+                side_low,
+                side_high,
+            ),
+            (shape_of((3, 512, e)),),
+            work + streaming,
+            away=(0, 1, 2),
+            unused=(0,),
         )
-        return out
+        return out.reshape(1536, e)
 
     return lax.cond(is_solvent, solvent_last, mech_last).reshape(state.shape)
 

time: 94.7 us -> 102 us (1.077)
  blocking collectives: 0 us -> 12.3 us
  waiting for transfers between devices: 22.8 us -> 18.1 us
  starting transfers between devices: 53.1 us -> 50 us
  Pallas kernels: 16.2 us -> 18.4 us
    all_to_all x0 -> x1, blocking collectives: none -> 12.3 us  [swap(): return lax.all_to_all(block, 'blk', split_axis=0, concat_axis=0, tiled=True)]
    all_to_all x4 -> x3, waiting for transfers between devices: 10 us -> 5.6 us  [swap(): return lax.all_to_all(block, 'blk', split_axis=0, concat_axis=0, tiled=True)]
    all_to_all x4 -> x3, starting transfers between devices: 20.7 us -> 16.6 us  [swap(): return lax.all_to_all(block, 'blk', split_axis=0, concat_axis=0, tiled=True)]
    pallas_call x6, Pallas kernels: 16.2 us -> 18.4 us  [call(): pl.pallas_call(body, out_shape=outs, in_specs=[ANY if n in away else spec...]
  transfers between devices with their start and end apart: 17 -> 16, of which waited for: 7 -> 5; matrix products, arithmetic and copies ran while one was open for 0% -> 0% of each run, Pallas kernels for 5% -> 5%
where the time goes in v5:
time: 102 us; the launch traced here: 101 us
  starting transfers between devices  50 us (49%)
  Pallas kernels  18.4 us (18%)
  waiting for transfers between devices  18.1 us (18%)
  blocking collectives  12.3 us (12%)
  local copies, waits for them, and re-layouts  1.46 us (1%)
    pallas_call x6, Pallas kernels, call(): pl.pallas_call(body, out_shape=outs, in_specs=[ANY if n in away else spec...  18.4 us
    all_to_all x3, starting transfers between devices, swap(): return lax.all_to_all(block, 'blk', split_axis=0, concat_axis=0, tiled=True)  16.6 us
    all_to_all x1, blocking collectives, swap(): return lax.all_to_all(block, 'blk', split_axis=0, concat_axis=0, tiled=True)  12.3 us
    ppermute x3, starting transfers between devices, shards(): lax.ppermute(block, axes, pairs(False, g) + pairs(True, g))  12.1 us
    ppermute x3, starting transfers between devices, shards(): arrived.append(lax.ppermute(recv, axes, pairs(False, g)))  8.16 us
    ppermute x2, starting transfers between devices, both_ways(): lax.ppermute(up, axes, planes(True, which))  8 us
    ppermute x2, waiting for transfers between devices, both_ways(): lax.ppermute(down, axes, planes(False, which))  6.47 us
    all_to_all x3, waiting for transfers between devices, swap(): return lax.all_to_all(block, 'blk', split_axis=0, concat_axis=0, tiled=True)  5.6 us
  transfers between devices with their start and end apart: 16, of which 5 were waited for; matrix products, arithmetic and copies ran while one was open for 0% of the time, Pallas kernels for 5%

profile of v5, /device:TPU:1, one launch (start us, length us, event | category | flops | bytes accessed | tf_op | source)
XLA Modules:
  0.0 100.7 jit_solution(17453311826019897664)
XLA Ops:
  0.7 2.8 %shard_map.57 = (bf16[256,640]{1,0:T(8,128)(2,1)}, bf16[256,128]{1,0:T(8,128)(2,1)S(1)}, f32[8,128]{1,0:T(8,128)S(1)}, bf16[512,384]{1,0:T(8,128)(2,1)S(1)}, f32...) custom-call(s32[1]{0:T(128)} %bitcast.25.grp, f32[1536,128]{1,0:T(8,128)} %bitcast.46, ...), custom_call_target="tpu_custom_call" | custom-call | tf_op jit(solution)/shard_map/pallas_call | solution.py:32
  3.5 6.4 %all-to-all-start.6 = ((bf16[8,32,640]{2,1,0:T(8,128)(2,1)}), bf16[8,32,640]{2,1,0:T(8,128)(2,1)S(1)}, u32[]{:S(2)}, u32[]{:S(2)}) async-start(bf16[8,32,640]{2,1,0:T(8,128)(2,1)} %bitcast.29), calls=%async_computation.6 | async-start | bytes 655360 | tf_op jit(solution)/shard_map/all_to_all | solution.py:635
  12.6 5.6 %all-to-all-done.6 = bf16[8,32,640]{2,1,0:T(8,128)(2,1)S(1)} async-done(((bf16[8,32,640]{2,1,0:T(8,128)(2,1)}), bf16[8,32,640]{2,1,0:T(8,128)(2,1)S(1)}, u32[]{:S(2)}, u32[]{:S(2)}) %all-to-all-start.6) | async-done | bytes 327712 | tf_op jit(solution)/shard_map/all_to_all | solution.py:635
  18.2 2.6 %collective-permute-done.13 = bf16[512,384]{1,0:T(8,128)(2,1)S(1)} collective-permute-done((bf16[512,384]{1,0:T(8,128)(2,1)S(1)}, bf16[512,384]{1,0:T(8,128)(2,1)S(1)}, u32[]{:S(2)}, u32[]{:S(2)}) %collective-permute-start.13) | collective-permute-done | bytes 393248 | tf_op jit(solution)/shard_map/ppermute | solution.py:663
  22.5 5.4 %all-to-all-start.7 = ((bf16[8,32,512]{2,1,0:T(8,128)(2,1)}), bf16[8,32,512]{2,1,0:T(8,128)(2,1)S(1)}, u32[]{:S(2)}, u32[]{:S(2)}) async-start(bf16[8,32,512]{2,1,0:T(8,128)(2,1)} %bitcast.31), calls=%async_computation.7 | async-start | bytes 524288 | tf_op jit(solution)/shard_map/all_to_all | solution.py:635
  28.0 1.4 %collective-permute-start.19 = (bf16[256,640]{1,0:T(8,128)(2,1)S(1)}, bf16[256,640]{1,0:T(8,128)(2,1)}, u32[]{:S(2)}, u32[]{:S(2)}) collective-permute-start(bf16[256,640]{1,0:T(8,128)(2,1)S(1)} %bitcast.52), channel_id=1, source_target_pairs={{16,24},{17,25},{18,26},{19,27},{20,28},{21,29},{22,30},{23,31}} | collective-permute-start | bytes 983048 | tf_op jit(solution)/shard_map/ppermute | solution.py:689
  29.4 5.4 %collective-permute-start.18 = (bf16[256,640]{1,0:T(8,128)(2,1)S(1)}, bf16[256,640]{1,0:T(8,128)(2,1)}, u32[]{:S(2)}, u32[]{:S(2)}) collective-permute-start(bf16[256,640]{1,0:T(8,128)(2,1)S(1)} %bitcast.53), channel_id=1, source_target_pairs={{8,24},{9,25},{10,26},{11,27},{12,28},{13,29},{14,30},{15,31}} | collective-permute-start | bytes 983048 | tf_op jit(solution)/shard_map/ppermute | solution.py:689
  36.1 2.0 %conditional.6 = ((f32[2048,128]{1,0:T(8,128)S(1)}, f32[512,128]{1,0:T(8,128)}, f32[128,128]{1,0:T(8,128)}, f32[128,128]{1,0:T(8,128)})) conditional(s32[]{:T(128)} %convert_element_type.2, (f32[1536,128]{1,0:T(8,128)S(1)}, f32[1536,128]{1,0:T(8,128)S(1)}, f32[8,128]{1,0:T(8,128)S(1)}) %tuple.105, f32[1536,128]{1,0:T(8,128)S(1)} %bitcast.35), branch_computations={%region_0.0_spmd, %region_1.0_spmd} | conditional | bytes 1048752 | solution.py:722
  36.1 2.0 %branch_0_fun.5 = (f32[2048,128]{1,0:T(8,128)S(1)}, f32[512,128]{1,0:T(8,128)}, f32[128,128]{1,0:T(8,128)}, f32[128,128]{1,0:T(8,128)}) custom-call(f32[1536,128]{1,0:T(8,128)S(1)} %get-tuple-element.154.state, f32[1536,128]{1,0:T(8,128)S(1)} %get-tuple-element.155.mat, f32[8,128]{1,0:T(8,128)S(1)} %get-tuple-element.156.occ), custom_call_target="tpu_custom_call" | custom-call | tf_op jit(solution)/shard_map/cond/branch_0_fun/pallas_call | solution.py:32
  38.1 4.0 %collective-permute-start.15 = (f32[200,128]{1,0:T(8,128)S(1)}, f32[200,128]{1,0:T(8,128)}, u32[]{:S(2)}, u32[]{:S(2)}) collective-permute-start(f32[200,128]{1,0:T(8,128)S(1)} %get-tuple-element.292), channel_id=1, source_target_pairs={{0,1},{1,2},{2,3},{3,4},{4,5},{5,6},{6,7},{8,9},{9,10},{10,11},{11... | collective-permute-start | bytes 307208 | tf_op jit(solution)/shard_map/ppermute | solution.py:630
  43.5 4.2 %collective-permute-done.16 = f32[200,128]{1,0:T(8,128)} collective-permute-done((f32[200,128]{1,0:T(8,128)S(1)}, f32[200,128]{1,0:T(8,128)}, u32[]{:S(2)}, u32[]{:S(2)}) %collective-permute-start.16) | collective-permute-done | bytes 102432 | tf_op jit(solution)/shard_map/ppermute | solution.py:631
  47.6 5.2 %conditional.8 = ((f32[4,512,128]{2,1,0:T(8,128)S(1)}, bf16[256,512]{1,0:T(8,128)(2,1)}, f32[192,128]{1,0:T(8,128)}, f32[192,128]{1,0:T(8,128)})) conditional(s32[]{:T(128)} %convert_element_type.2, (f32[1,3,512,128]{3,2,1,0:T(8,128)}, f32[2048,128]{1,0:T(8,128)S(1)}, f32[1,3,512,128]{3,2,1,0:T(8,128)S(1)}, f32[8,128]{1,0:T(8,128)S(1)}, ...), branch_computations={%region_6.0_spmd, %region_7.0_spmd} | conditional | bytes 8 | solution.py:725
  47.7 5.2 %branch_0_fun.7 = (f32[4,512,128]{2,1,0:T(8,128)S(1)}, bf16[256,512]{1,0:T(8,128)(2,1)}, f32[192,128]{1,0:T(8,128)}, f32[192,128]{1,0:T(8,128)}) custom-call(f32[3,512,128]{2,1,0:T(8,128)} %bitcast.48, f32[4,512,128]{2,1,0:T(8,128)S(1)} %bitcast.45, f32[3,512,128]{2,1,0:T(8,128)S(1)} %bitcast.40, f32[8,128]{1,0:T(8,128)S(1)} %get-tuple-element.170.occ, ...), custom_call_target="tpu_custom_call" | custom-call | tf_op jit(solution)/shard_map/cond/branch_0_fun/pallas_call | solution.py:32
  52.9 15.3 %conditional.9 = (f32[2048,128]{1,0:T(8,128)}, f32[512,128]{1,0:T(8,128)}, bf16[768,128]{1,0:T(8,128)(2,1)}, f32[1536,128]{1,0:T(8,128)}, f32[192,128]{1,0:T(8,1...) conditional(s32[]{:T(128)} %clamp.7, ...), branch_computations={%region_8.0_spmd, %region_9.0_spmd, %region_10.0_spmd, %region_11.... | conditional | bytes 5505232 | solution.py:762
  52.9 4.8 %all-to-all-start.1 = ((bf16[8,32,512]{2,1,0:T(8,128)(2,1)}), bf16[8,32,512]{2,1,0:T(8,128)(2,1)}, u32[]{:S(2)}, u32[]{:S(2)}) async-start(bf16[8,32,512]{2,1,0:T(8,128)(2,1)} %bitcast.8), calls=%async_computation.1 | async-start | bytes 524288 | tf_op jit(solution)/shard_map/cond/branch_1_fun/all_to_all | solution.py:635
  57.7 4.0 %collective-permute-start.4 = (f32[192,128]{1,0:T(8,128)S(1)}, f32[192,128]{1,0:T(8,128)}, u32[]{:S(2)}, u32[]{:S(2)}) collective-permute-start(f32[192,128]{1,0:T(8,128)S(1)} %copy-done.17), channel_id=1, source_target_pairs={{8,9},{9,10},{10,11},{11,12},{12,13},{13,14},{14,15}} | collective-permute-start | bytes 294920 | tf_op jit(solution)/shard_map/cond/branch_1_fun/ppermute | solution.py:630
  63.0 2.8 %branch_1_fun.10 = (f32[1536,128]{1,0:T(8,128)}, f32[2048,128]{1,0:T(8,128)}, f32[512,128]{1,0:T(8,128)}, bf16[768,128]{1,0:T(8,128)(2,1)}, bf16[256,512]{1,0:T(8,128)(2,1)}, /*index=5*/bf16[256,512]{1,0:T(8,128)(2,1)}) custom-call(f32[2048,128]{1,0:T(8,128)S(1)} %bitcast.43, f32[1536,128]{1,0:T(8,128)S(1)} %get-tuple-element.188.mat, ...), custom_call_target="tpu_custom_call" | custom-call | tf_op jit(solution)/shard_map/cond/branch_1_fun/pallas_call | solution.py:32
  65.8 2.3 %collective-permute-done.5 = f32[192,128]{1,0:T(8,128)} collective-permute-done((f32[192,128]{1,0:T(8,128)S(1)}, f32[192,128]{1,0:T(8,128)}, u32[]{:S(2)}, u32[]{:S(2)}) %collective-permute-start.5) | collective-permute-done | bytes 98336 | tf_op jit(solution)/shard_map/cond/branch_1_fun/ppermute | solution.py:631
  68.8 10.0 %collective-permute-start.21 = (bf16[256,512]{1,0:T(8,128)(2,1)}, bf16[256,512]{1,0:T(8,128)(2,1)S(1)}, u32[]{:S(2)}, u32[]{:S(2)}) collective-permute-start(bf16[256,512]{1,0:T(8,128)(2,1)} %get-tuple-element.305), channel_id=1, source_target_pairs={{8,24},{9,25},{10,26},{11,27},{12,28},{13,29},{14,30},{15,31},{24,... | collective-permute-start | bytes 786440 | tf_op jit(solution)/shard_map/ppermute | solution.py:764
  80.2 3.4 %collective-permute-done.21 = bf16[256,512]{1,0:T(8,128)(2,1)S(1)} collective-permute-done((bf16[256,512]{1,0:T(8,128)(2,1)}, bf16[256,512]{1,0:T(8,128)(2,1)S(1)}, u32[]{:S(2)}, u32[]{:S(2)}) %collective-permute-start.21) | collective-permute-done | bytes 262176 | tf_op jit(solution)/shard_map/ppermute | solution.py:764
  83.7 16.9 %conditional.10 = (f32[1,3,512,128]{3,2,1,0:T(8,128)}) conditional(s32[]{:T(128)} %convert_element_type.2, (f32[1536,128]{1,0:T(8,128)}, f32[1,3,512,128]{3,2,1,0:T(8,128)S(1)}, s32[]{:T(128)}, bf16[256,512]{1,0:T(8,128)(2,1)S(1)}, bf16[256,512]{1,0:T(8,128)(2,1)S(1)}, /*index=5*/bf16[256,512]{1,0:T(8,128)(2,1)}, f32[4,512,128]{2,1,0:T(8,128)S(1)}, ...), branch_computations={%region_12.0_spmd, %region_16.0_spmd} | conditional | flops 1 | bytes 3670076 | solution.py:809
  83.7 12.3 %conditional = (bf16[256,512]{1,0:T(8,128)(2,1)S(1)}) conditional(s32[]{:T(128)} %clamp.1, bf16[256,512]{1,0:T(8,128)(2,1)S(1)} %get-tuple-element.238, bf16[256,512]{1,0:T(8,128)(2,1)S(1)} %get-tuple-element.239, bf16[256,512]{1,0:T(8,128)(2,1)} %get-tuple-element.240), branch_computations={%region_13.0_spmd, %region_14.0_spmd, %region_15.0_spmd} | conditional | bytes 524296 | solution.py:787
  83.7 12.3 %all_to_all.80 = bf16[8,32,512]{2,1,0:T(8,128)(2,1)S(1)} all-to-all(bf16[8,32,512]{2,1,0:T(8,128)(2,1)S(1)} %bitcast.57), channel_id=1, replica_groups=mesh['grp'=4,'blk'=8] {'blk'}, dimensions={0} | all-to-all | bytes 524288 | tf_op jit(solution)/shard_map/cond/branch_0_fun/cond/branch_1_fun/all_to_all | solution.py:635
  96.0 4.5 %branch_0_fun.9 = f32[3,512,128]{2,1,0:T(8,128)} custom-call(f32[4,512,128]{2,1,0:T(8,128)S(1)} %get-tuple-element.232.state, f32[3,512,128]{2,1,0:T(8,128)S(1)} %bitcast.61, f32[3,512,128]{2,1,0:T(8,128)S(1)} %bitcast.41, f32[8,128]{1,0:T(8,128)S(1)} %get-tuple-element.235.occ, bf16[256,128]{1,0:T(8,128)(2,1)S(1)} %get-tuple-element.236.sel, ...), custom_call_target="tpu_custom_call" | custom-call | tf_op jit(solution)/shard_map/cond/branch_0_fun/pallas_call | solution.py:32
  (45 shorter events, 12.2 us)
Async XLA Ops:
  3.5 14.6 %all-to-all-start.6 = ((bf16[8,32,640]{2,1,0:T(8,128)(2,1)}), bf16[8,32,640]{2,1,0:T(8,128)(2,1)S(1)}, u32[]{:S(2)}, u32[]{:S(2)}) async-start(bf16[8,32,640]{2,1,0:T(8,128)(2,1)} %bitcast.29), calls=%async_computation.6 | async-start | bytes 655360 | tf_op jit(solution)/shard_map/all_to_all | solution.py:635
  9.9 2.7 %collective-permute-start.14 = (bf16[512,384]{1,0:T(8,128)(2,1)S(1)}, bf16[512,384]{1,0:T(8,128)(2,1)S(1)}, u32[]{:S(2)}, u32[]{:S(2)}) collective-permute-start(bf16[512,384]{1,0:T(8,128)(2,1)S(1)} %get-tuple-element.290), channel_id=1, source_target_pairs={{24,16},{25,17},{26,18},{27,19},{28,20},{29,21},{30,22},{31,23}} | collective-permute-start | bytes 1179656 | tf_op jit(solution)/shard_map/ppermute | solution.py:663
  10.5 10.2 %collective-permute-start.13 = (bf16[512,384]{1,0:T(8,128)(2,1)S(1)}, bf16[512,384]{1,0:T(8,128)(2,1)S(1)}, u32[]{:S(2)}, u32[]{:S(2)}) collective-permute-start(bf16[512,384]{1,0:T(8,128)(2,1)S(1)} %get-tuple-element.290), channel_id=1, source_target_pairs={{24,8},{25,9},{26,10},{27,11},{28,12},{29,13},{30,14},{31,15}} | collective-permute-start | bytes 1179656 | tf_op jit(solution)/shard_map/ppermute | solution.py:663
  11.8 8.9 %collective-permute-start.12 = (bf16[512,384]{1,0:T(8,128)(2,1)S(1)}, bf16[512,384]{1,0:T(8,128)(2,1)S(1)}, u32[]{:S(2)}, u32[]{:S(2)}) collective-permute-start(bf16[512,384]{1,0:T(8,128)(2,1)S(1)} %get-tuple-element.290), channel_id=1, source_target_pairs={{24,0},{25,1},{26,2},{27,3},{28,4},{29,5},{30,6},{31,7}} | collective-permute-start | bytes 1179656 | tf_op jit(solution)/shard_map/ppermute | solution.py:663
  21.5 14.6 %copy-start.3 = (f32[1,3,512,128]{3,2,1,0:T(8,128)S(1)}, f32[1,3,512,128]{3,2,1,0:T(8,128)}, u32[]{:S(2)}) copy-start(f32[1,3,512,128]{3,2,1,0:T(8,128)} %param.23) | copy-start | bytes 2359300
  21.5 14.6 %copy-start.4 = (f32[1,3,512,128]{3,2,1,0:T(8,128)S(1)}, f32[1,3,512,128]{3,2,1,0:T(8,128)}, u32[]{:S(2)}) copy-start(f32[1,3,512,128]{3,2,1,0:T(8,128)} %param.22) | copy-start | bytes 2359300
  22.5 25.1 %all-to-all-start.7 = ((bf16[8,32,512]{2,1,0:T(8,128)(2,1)}), bf16[8,32,512]{2,1,0:T(8,128)(2,1)S(1)}, u32[]{:S(2)}, u32[]{:S(2)}) async-start(bf16[8,32,512]{2,1,0:T(8,128)(2,1)} %bitcast.31), calls=%async_computation.7 | async-start | bytes 524288 | tf_op jit(solution)/shard_map/all_to_all | solution.py:635
  28.0 15.5 %collective-permute-start.19 = (bf16[256,640]{1,0:T(8,128)(2,1)S(1)}, bf16[256,640]{1,0:T(8,128)(2,1)}, u32[]{:S(2)}, u32[]{:S(2)}) collective-permute-start(bf16[256,640]{1,0:T(8,128)(2,1)S(1)} %bitcast.52), channel_id=1, source_target_pairs={{16,24},{17,25},{18,26},{19,27},{20,28},{21,29},{22,30},{23,31}} | collective-permute-start | bytes 983048 | tf_op jit(solution)/shard_map/ppermute | solution.py:689
  29.4 14.1 %collective-permute-start.18 = (bf16[256,640]{1,0:T(8,128)(2,1)S(1)}, bf16[256,640]{1,0:T(8,128)(2,1)}, u32[]{:S(2)}, u32[]{:S(2)}) collective-permute-start(bf16[256,640]{1,0:T(8,128)(2,1)S(1)} %bitcast.53), channel_id=1, source_target_pairs={{8,24},{9,25},{10,26},{11,27},{12,28},{13,29},{14,30},{15,31}} | collective-permute-start | bytes 983048 | tf_op jit(solution)/shard_map/ppermute | solution.py:689
  34.7 8.7 %collective-permute-start.17 = (bf16[256,640]{1,0:T(8,128)(2,1)S(1)}, bf16[256,640]{1,0:T(8,128)(2,1)}, u32[]{:S(2)}, u32[]{:S(2)}) collective-permute-start(bf16[256,640]{1,0:T(8,128)(2,1)S(1)} %bitcast.54), channel_id=1, source_target_pairs={{0,24},{1,25},{2,26},{3,27},{4,28},{5,29},{6,30},{7,31}} | collective-permute-start | bytes 983048 | tf_op jit(solution)/shard_map/ppermute | solution.py:689
  38.1 5.3 %collective-permute-start.15 = (f32[200,128]{1,0:T(8,128)S(1)}, f32[200,128]{1,0:T(8,128)}, u32[]{:S(2)}, u32[]{:S(2)}) collective-permute-start(f32[200,128]{1,0:T(8,128)S(1)} %get-tuple-element.292), channel_id=1, source_target_pairs={{0,1},{1,2},{2,3},{3,4},{4,5},{5,6},{6,7},{8,9},{9,10},{10,11},{11... | collective-permute-start | bytes 307208 | tf_op jit(solution)/shard_map/ppermute | solution.py:630
  42.1 5.5 %collective-permute-start.16 = (f32[200,128]{1,0:T(8,128)S(1)}, f32[200,128]{1,0:T(8,128)}, u32[]{:S(2)}, u32[]{:S(2)}) collective-permute-start(f32[200,128]{1,0:T(8,128)S(1)} %get-tuple-element.293), channel_id=1, source_target_pairs={{1,0},{2,1},{3,2},{4,3},{5,4},{6,5},{7,6},{9,8},{10,9},{11,10},{12... | collective-permute-start | bytes 307208 | tf_op jit(solution)/shard_map/ppermute | solution.py:631
  47.6 5.2 %copy-start.6 = (f32[512,128]{1,0:T(8,128)S(1)}, f32[512,128]{1,0:T(8,128)}, u32[]{:S(2)}) copy-start(f32[512,128]{1,0:T(8,128)} %get-tuple-element.300) | copy-start | bytes 786436
  47.6 5.2 %copy-start.11 = (f32[128,128]{1,0:T(8,128)S(1)}, f32[128,128]{1,0:T(8,128)}, u32[]{:S(2)}) copy-start(f32[128,128]{1,0:T(8,128)} %get-tuple-element.301) | copy-start | bytes 196612
  52.9 30.8 %copy-start.12 = (f32[128,128]{1,0:T(8,128)S(1)}, f32[128,128]{1,0:T(8,128)}, u32[]{:S(2)}) copy-start(f32[128,128]{1,0:T(8,128)} %get-tuple-element.301) | copy-start | bytes 196612
  52.9 4.8 %copy-start.17 = (f32[192,128]{1,0:T(8,128)S(1)}, f32[192,128]{1,0:T(8,128)}, u32[]{:S(2)}) copy-start(f32[192,128]{1,0:T(8,128)} %get-tuple-element.194) | copy-start | bytes 294916 | tf_op jit(solution)/shard_map/cond
  52.9 8.8 %copy-start.20 = (f32[192,128]{1,0:T(8,128)S(1)}, f32[192,128]{1,0:T(8,128)}, u32[]{:S(2)}) copy-start(f32[192,128]{1,0:T(8,128)} %get-tuple-element.195) | copy-start | bytes 294916 | tf_op jit(solution)/shard_map/cond
  52.9 15.2 %all-to-all-start.1 = ((bf16[8,32,512]{2,1,0:T(8,128)(2,1)}), bf16[8,32,512]{2,1,0:T(8,128)(2,1)}, u32[]{:S(2)}, u32[]{:S(2)}) async-start(bf16[8,32,512]{2,1,0:T(8,128)(2,1)} %bitcast.8), calls=%async_computation.1 | async-start | bytes 524288 | tf_op jit(solution)/shard_map/cond/branch_1_fun/all_to_all | solution.py:635
  57.7 8.1 %collective-permute-start.4 = (f32[192,128]{1,0:T(8,128)S(1)}, f32[192,128]{1,0:T(8,128)}, u32[]{:S(2)}, u32[]{:S(2)}) collective-permute-start(f32[192,128]{1,0:T(8,128)S(1)} %copy-done.17), channel_id=1, source_target_pairs={{8,9},{9,10},{10,11},{11,12},{12,13},{13,14},{14,15}} | collective-permute-start | bytes 294920 | tf_op jit(solution)/shard_map/cond/branch_1_fun/ppermute | solution.py:630
  61.7 6.4 %collective-permute-start.5 = (f32[192,128]{1,0:T(8,128)S(1)}, f32[192,128]{1,0:T(8,128)}, u32[]{:S(2)}, u32[]{:S(2)}) collective-permute-start(f32[192,128]{1,0:T(8,128)S(1)} %copy-done.20), channel_id=1, source_target_pairs={{9,8},{10,9},{11,10},{12,11},{13,12},{14,13},{15,14}} | collective-permute-start | bytes 294920 | tf_op jit(solution)/shard_map/cond/branch_1_fun/ppermute | solution.py:631
  68.1 12.1 %collective-permute-start.20 = (bf16[256,512]{1,0:T(8,128)(2,1)}, bf16[256,512]{1,0:T(8,128)(2,1)S(1)}, u32[]{:S(2)}, u32[]{:S(2)}) collective-permute-start(bf16[256,512]{1,0:T(8,128)(2,1)} %get-tuple-element.304), channel_id=1, source_target_pairs={{0,24},{1,25},{2,26},{3,27},{4,28},{5,29},{6,30},{7,31},{24,0},{25... | collective-permute-start | bytes 786440 | tf_op jit(solution)/shard_map/ppermute | solution.py:764
  68.8 14.9 %collective-permute-start.21 = (bf16[256,512]{1,0:T(8,128)(2,1)}, bf16[256,512]{1,0:T(8,128)(2,1)S(1)}, u32[]{:S(2)}, u32[]{:S(2)}) collective-permute-start(bf16[256,512]{1,0:T(8,128)(2,1)} %get-tuple-element.305), channel_id=1, source_target_pairs={{8,24},{9,25},{10,26},{11,27},{12,28},{13,29},{14,30},{15,31},{24,... | collective-permute-start | bytes 786440 | tf_op jit(solution)/shard_map/ppermute | solution.py:764
  78.8 4.8 %collective-permute-start.22 = (bf16[256,512]{1,0:T(8,128)(2,1)}, bf16[256,512]{1,0:T(8,128)(2,1)}, u32[]{:S(2)}, u32[]{:S(2)}) collective-permute-start(bf16[256,512]{1,0:T(8,128)(2,1)} %get-tuple-element.306), channel_id=1, source_target_pairs={{16,24},{17,25},{18,26},{19,27},{20,28},{21,29},{22,30},{23,31},{2... | collective-permute-start | bytes 786440 | tf_op jit(solution)/shard_map/ppermute | solution.py:764
  83.7 12.3 %copy-start.8 = (f32[1536,128]{1,0:T(8,128)S(1)}, f32[1536,128]{1,0:T(8,128)}, u32[]{:S(2)}) copy-start(f32[1536,128]{1,0:T(8,128)} %get-tuple-element.233) | copy-start | bytes 2359300 | tf_op jit(solution)/shard_map/cond
  (4 other events, 2.8 us)

commit v6 on v4

--- a/solution.py
+++ b/solution.py
@@ -124,8 +124,8 @@
 
 def put_faces(ref, up, down):
     for c in range(3):
-        up[pl.ds(64 * c, 64), :] = ref[pl.ds(c * 512 + 448, 64), :]
-        down[pl.ds(64 * c, 64), :] = ref[pl.ds(c * 512, 64), :]
+        up[pl.ds(64 * c, 64), :] = ref[pl.ds(c * 512 + 448, 64), :].astype(BF16)
+        down[pl.ds(64 * c, 64), :] = ref[pl.ds(c * 512, 64), :].astype(BF16)
 
 
 def elastic(ref, mat, filled, out, stress, partial):
@@ -191,10 +191,10 @@
                 slab(stress, a, i + 1) if i < 7 else None,
             )
             if i == 0:
-                other = low[pl.ds(64 * a, 64), :].reshape(8, 8, e)
+                other = low[pl.ds(64 * a, 64), :].astype(F32).reshape(8, 8, e)
                 force = force + penalty * fill_low * (other - here)
             if i == 7:
-                other = high[pl.ds(64 * a, 64), :].reshape(8, 8, e)
+                other = high[pl.ds(64 * a, 64), :].astype(F32).reshape(8, 8, e)
                 force = force + penalty * fill_high * (other - here)
             put_slab(out, a, i, here + rate * force)
 
@@ -293,7 +293,7 @@
 
 
 def load(ref, x):
-    return ref[layer_rows(x), :].reshape(16, 8, LANES)
+    return ref[layer_rows(x), :].astype(F32).reshape(16, 8, LANES)
 
 
 def sweep_range(ref, kap, start, stop, put, weights, fluxes, masks):
@@ -325,6 +325,8 @@
     sweep_range(phi, kap, 1, 15, keep, weights, fluxes, masks)
     for n, x in enumerate((1, 2, 13, 14)):
         edges[layer_rows(n), :] = middle[layer_rows(x), :]
+    for n, x in enumerate((0, 1, 14, 15)):
+        edges[layer_rows(4 + n), :] = phi[layer_rows(x), :]
     sweep_range(middle, kap, 2, 14, put, weights, fluxes, masks)
 
 
@@ -339,14 +341,14 @@
     ]
 
 
-def edge_sweeps(top, bottom, low, high, kap_edge, kap_low, kap_high, middle, q_count):
+def edge_sweeps(low, high, kap_edge, kap_low, kap_high, middle, q_count):
     masks = sweep_masks(q_count)
     k = [load(kap_edge, n) for n in range(4)]
-    m = [load(middle, n) for n in range(4)]
-    first = [load(low, 0), load(low, 1), load(bottom, 0), load(bottom, 1)]
+    m = [load(middle, n) for n in range(8)]
+    first = [load(low, 0), load(low, 1), m[4], m[5]]
     first = sweep_chain(first, [load(kap_low, 2), k[0]], masks)
     first = sweep_chain([*first, m[0], m[1]], k[:2], masks)
-    last = [load(top, 0), load(top, 1), load(high, 0), load(high, 1)]
+    last = [m[6], m[7], load(high, 0), load(high, 1)]
     last = sweep_chain(last, [k[3], load(kap_high, 2)], masks)
     last = sweep_chain([m[2], m[3], *last], k[2:], masks)
     return [layer.reshape(LANES, LANES) for layer in first + last]
@@ -387,8 +389,8 @@
             send[:, pl.ds(512, LANES)] = tile.astype(BF16)
             put_faces(state, up, down)
             filled[...] = jnp.broadcast_to(full, (8, e))
-            up[pl.ds(192, 8), :] = jnp.broadcast_to(full, (8, e))
-            down[pl.ds(192, 8), :] = jnp.broadcast_to(full, (8, e))
+            up[pl.ds(192, 8), :] = jnp.broadcast_to(full, (8, e)).astype(BF16)
+            down[pl.ds(192, 8), :] = jnp.broadcast_to(full, (8, e)).astype(BF16)
 
         @pl.when(grp[0] == solvent)
         def _():
@@ -435,7 +437,7 @@
 
 def first_step(state, mat, occ, base, sel, recv, low, high, out, send, up, down, *scratch):
     filled = occ[pl.ds(0, 1), :].reshape(1, 1, occ.shape[-1])
-    fills = (low[pl.ds(192, 1), :], high[pl.ds(192, 1), :])
+    fills = [ref[pl.ds(192, 8), :].astype(F32)[:1] for ref in (low, high)]
     advance(state, mat, filled, base, recv, sel, low, high, fills, out, *scratch[:3])
     dil = scratch[3]
     dilate(out, filled, dil)
@@ -445,7 +447,7 @@
 
 def last_step(state, mat, occ, base, sel, recv, low, high, fill_low, fill_high, out, *scratch):
     filled = occ[pl.ds(0, 1), :].reshape(1, 1, occ.shape[-1])
-    fills = (fill_low[pl.ds(192, 1), :], fill_high[pl.ds(192, 1), :])
+    fills = [ref[pl.ds(192, 8), :].astype(F32)[:1] for ref in (fill_low, fill_high)]
     advance(state, mat, filled, base, recv, sel, low, high, fills, out, *scratch)
 
 
@@ -455,8 +457,8 @@
             edge, v0, v1, v2, tile, out, up, down = refs
         else:
             border, v0, v1, v2, out, up, down, tile, _ = refs
-            down[layer_rows(2), :] = border[layer_rows(0), :]
-            up[layer_rows(2), :] = border[layer_rows(3), :]
+            down[layer_rows(2), :] = border[layer_rows(0), :].astype(BF16)
+            up[layer_rows(2), :] = border[layer_rows(3), :].astype(BF16)
         total = None
         for n, v in enumerate((v0, v1, v2)):
             spot = pl.ds(n * v.shape[0], v.shape[0])
@@ -481,9 +483,9 @@
             layer = layer + (SWEEP_STEP * SOURCE_RATE) * added
             out[layer_rows(x), :] = layer
             if x < 2:
-                down[layer_rows(x), :] = layer
+                down[layer_rows(x), :] = layer.astype(BF16)
             if x >= 14:
-                up[layer_rows(x - 14), :] = layer
+                up[layer_rows(x - 14), :] = layer.astype(BF16)
 
     return body
 
@@ -499,8 +501,8 @@
 
 
 def outer_first(q_count):
-    def body(up, down, low, high, kap_edge, kap_low, kap_high, mid, phi, tile, edge, s0, s1, s2, field):
-        final = edge_sweeps(up, down, low, high, kap_edge, kap_low, kap_high, mid, q_count)
+    def body(low, high, kap_edge, kap_low, kap_high, mid, phi, tile, edge, s0, s1, s2, field):
+        final = edge_sweeps(low, high, kap_edge, kap_low, kap_high, mid, q_count)
         for n in range(4):
             edge[layer_rows(n), :] = final[n]
         for x in range(16):
@@ -532,8 +534,8 @@
 
 
 def outer_last(q_count, tiles):
-    def body(up, down, low, high, kap_edge, kap_low, kap_high, mid, _, out, ends, sem):
-        final = edge_sweeps(up, down, low, high, kap_edge, kap_low, kap_high, mid, q_count)
+    def body(low, high, kap_edge, kap_low, kap_high, mid, _, out, ends, sem):
+        final = edge_sweeps(low, high, kap_edge, kap_low, kap_high, mid, q_count)
         tables = tables_out()
         rows = 16 * tiles
         for n in range(4):
@@ -567,9 +569,10 @@
     mat = material.reshape(1536, e)
     col = brick_column.reshape(1, e)
     octant = brick_octant.reshape(1, e)
-    layers, ends, halo = shape_of((2048, LANES)), shape_of((512, LANES)), shape_of((256, LANES))
+    layers, ends, halves = shape_of((2048, LANES)), shape_of((512, LANES)), shape_of((1024, LANES))
+    halo = shape_of((256, LANES), BF16)
     rows, flat = shape_of((slots, 512), BF16), shape_of((1536, e))
-    face, side, wide = shape_of((192, e)), shape_of((200, e)), shape_of((384, e))
+    face, side, wide = (shape_of((n, e), BF16) for n in (192, 200, 384))
     tile = shape_of((slots * (n_grp - 1), LANES), BF16)
 
     def pairs(back, g):
@@ -666,10 +669,10 @@
             deposit(False), (phi, kap_edge, *arrived), (layers, wide, wide, tile, flat), unused=(4,)
         )
         low, high = both_ways(top, bottom, [solvent])
-        inner, mid = call(inner_first(q_count), (added, kap), (layers, ends), sweeping)
+        inner, mid = call(inner_first(q_count), (added, kap), (layers, halves), sweeping)
         edge, s0, s1, s2 = call(
             outer_first(q_count),
-            (top, bottom, low, high, kap_edge, low, high, mid, inner, hot),
+            (low, high, kap_edge, low, high, mid, inner, hot),
             (ends, rows, rows, rows),
             [pltpu.VMEM((512, 4 * LANES), BF16)],
         )
@@ -701,15 +704,15 @@
     def solvent_last():
         added, top, bottom = call(deposit(True), (inner, edge, *back, hot), (layers, halo, halo))
         low, high = both_ways(top, bottom, [solvent])
-        out, mid = call(inner_last(q_count, tiles), (added, kap), (flat, ends), sweeping)
+        out, mid = call(inner_last(q_count, tiles), (added, kap), (flat, halves), sweeping)
         (out,) = call(
             outer_last(q_count, tiles),
-            (top, bottom, low, high, kap_edge, far_low, far_high, mid, out),
+            (low, high, kap_edge, far_low, far_high, mid, out),
             (flat,),
             [pltpu.VMEM((4 * 16 * tiles, LANES), F32), pltpu.SemaphoreType.DMA((2,))],
-            away=(8,),
+            away=(6,),
             unused=(0,),
-            alias={8: 0},
+            alias={6: 0},
         )
         return out
 

time: 94.7 us -> 93.2 us (0.984)
  waiting for transfers between devices: 22.8 us -> 21.3 us
  transfers between devices with their start and end apart: 17 -> 17, of which waited for: 7 -> 6; matrix products, arithmetic and copies ran while one was open for 0% -> 0% of each run, Pallas kernels for 5% -> 5%
where the time goes in v6:
time: 93.2 us; the launch traced here: 92.3 us
  starting transfers between devices  53.2 us (57%)
  waiting for transfers between devices  21.3 us (23%)
  Pallas kernels  16.1 us (17%)
  local copies, waits for them, and re-layouts  1.58 us (2%)
    all_to_all x4, starting transfers between devices, swap(): return lax.all_to_all(block, 'blk', split_axis=0, concat_axis=0, tiled=True)  20.5 us
    pallas_call x6, Pallas kernels, call(): pl.pallas_call(body, out_shape=outs, in_specs=[ANY if n in away else spec...  16.1 us
    ppermute x3, starting transfers between devices, shards(): lax.ppermute(block, axes, pairs(False, g) + pairs(True, g))  11.5 us
    all_to_all x4, waiting for transfers between devices, swap(): return lax.all_to_all(block, 'blk', split_axis=0, concat_axis=0, tiled=True)  9.97 us
    ppermute x3, starting transfers between devices, shards(): arrived.append(lax.ppermute(recv, axes, pairs(False, g)))  8.15 us
    ppermute x2, starting transfers between devices, both_ways(): lax.ppermute(up, axes, planes(True, which))  7.8 us
    ppermute x2, waiting for transfers between devices, both_ways(): lax.ppermute(down, axes, planes(False, which))  5.21 us
    ppermute x3, waiting for transfers between devices, shards(): lax.ppermute(block, axes, pairs(False, g) + pairs(True, g))  3.57 us
  transfers between devices with their start and end apart: 17, of which 6 were waited for; matrix products, arithmetic and copies ran while one was open for 0% of the time, Pallas kernels for 5%

profile of v6, /device:TPU:1, one launch (start us, length us, event | category | flops | bytes accessed | tf_op | source)
XLA Modules:
  0.0 92.3 jit_solution(16436326064834728411)
XLA Ops:
  0.7 2.8 %shard_map.57 = (bf16[256,640]{1,0:T(8,128)(2,1)}, bf16[256,128]{1,0:T(8,128)(2,1)S(1)}, f32[8,128]{1,0:T(8,128)S(1)}, bf16[512,384]{1,0:T(8,128)(2,1)S(1)}, f32...) custom-call(s32[1]{0:T(128)} %bitcast.15.grp, f32[1536,128]{1,0:T(8,128)} %bitcast.34, ...), custom_call_target="tpu_custom_call" | custom-call | tf_op jit(solution)/shard_map/pallas_call | solution.py:32
  3.5 6.4 %all-to-all-start.6 = ((bf16[8,32,640]{2,1,0:T(8,128)(2,1)}), bf16[8,32,640]{2,1,0:T(8,128)(2,1)S(1)}, u32[]{:S(2)}, u32[]{:S(2)}) async-start(bf16[8,32,640]{2,1,0:T(8,128)(2,1)} %bitcast.20), calls=%async_computation.6 | async-start | bytes 655360 | tf_op jit(solution)/shard_map/all_to_all | solution.py:594
  12.6 5.6 %all-to-all-done.6 = bf16[8,32,640]{2,1,0:T(8,128)(2,1)S(1)} async-done(((bf16[8,32,640]{2,1,0:T(8,128)(2,1)}), bf16[8,32,640]{2,1,0:T(8,128)(2,1)S(1)}, u32[]{:S(2)}, u32[]{:S(2)}) %all-to-all-start.6) | async-done | bytes 327712 | tf_op jit(solution)/shard_map/all_to_all | solution.py:594
  18.2 2.6 %collective-permute-done.11 = bf16[512,384]{1,0:T(8,128)(2,1)S(1)} collective-permute-done((bf16[512,384]{1,0:T(8,128)(2,1)S(1)}, bf16[512,384]{1,0:T(8,128)(2,1)S(1)}, u32[]{:S(2)}, u32[]{:S(2)}) %collective-permute-start.11) | collective-permute-done | bytes 393248 | tf_op jit(solution)/shard_map/ppermute | solution.py:622
  21.8 5.4 %all-to-all-start.7 = ((bf16[8,32,512]{2,1,0:T(8,128)(2,1)}), bf16[8,32,512]{2,1,0:T(8,128)(2,1)}, u32[]{:S(2)}, u32[]{:S(2)}) async-start(bf16[8,32,512]{2,1,0:T(8,128)(2,1)} %bitcast.22), calls=%async_computation.7 | async-start | bytes 524288 | tf_op jit(solution)/shard_map/all_to_all | solution.py:594
  28.6 5.4 %collective-permute-start.16 = (bf16[256,640]{1,0:T(8,128)(2,1)S(1)}, bf16[256,640]{1,0:T(8,128)(2,1)}, u32[]{:S(2)}, u32[]{:S(2)}) collective-permute-start(bf16[256,640]{1,0:T(8,128)(2,1)S(1)} %bitcast.41), channel_id=1, source_target_pairs={{8,24},{9,25},{10,26},{11,27},{12,28},{13,29},{14,30},{15,31}} | collective-permute-start | bytes 983048 | tf_op jit(solution)/shard_map/ppermute | solution.py:641
  35.4 4.0 %collective-permute-start.13 = (bf16[200,128]{1,0:T(8,128)(2,1)S(1)}, bf16[200,128]{1,0:T(8,128)(2,1)}, u32[]{:S(2)}, u32[]{:S(2)}) collective-permute-start(bf16[200,128]{1,0:T(8,128)(2,1)S(1)} %get-tuple-element.290), channel_id=1, source_target_pairs={{0,1},{1,2},{2,3},{3,4},{4,5},{5,6},{6,7},{8,9},{9,10},{10,11},{11... | collective-permute-start | bytes 153608 | tf_op jit(solution)/shard_map/ppermute | solution.py:589
  40.6 2.0 %conditional.7 = ((f32[2048,128]{1,0:T(8,128)S(1)}, f32[512,128]{1,0:T(8,128)S(1)})) conditional(s32[]{:T(128)} %convert_element_type.2, (f32[1536,128]{1,0:T(8,128)S(1)}, f32[1536,128]{1,0:T(8,128)S(1)}, f32[8,128]{1,0:T(8,128)S(1)}) %tuple.107, f32[1536,128]{1,0:T(8,128)S(1)} %bitcast.27), branch_computations={%region_0.0_spmd, %region_1.0_spmd} | conditional | bytes 8 | solution.py:662
  40.7 2.0 %branch_0_fun.5 = (f32[2048,128]{1,0:T(8,128)S(1)}, f32[512,128]{1,0:T(8,128)S(1)}) custom-call(f32[1536,128]{1,0:T(8,128)S(1)} %get-tuple-element.150.state, f32[1536,128]{1,0:T(8,128)S(1)} %get-tuple-element.151.mat, f32[8,128]{1,0:T(8,128)S(1)} %get-tuple-element.152.occ), custom_call_target="tpu_custom_call" | custom-call | tf_op jit(solution)/shard_map/cond/branch_0_fun/pallas_call | solution.py:32
  42.7 1.6 %collective-permute-done.14 = bf16[200,128]{1,0:T(8,128)(2,1)} collective-permute-done((bf16[200,128]{1,0:T(8,128)(2,1)S(1)}, bf16[200,128]{1,0:T(8,128)(2,1)}, u32[]{:S(2)}, u32[]{:S(2)}) %collective-permute-start.14) | collective-permute-done | bytes 51232 | tf_op jit(solution)/shard_map/ppermute | solution.py:590
  44.3 5.0 %conditional.8 = ((f32[2048,128]{1,0:T(8,128)S(1)}, bf16[256,512]{1,0:T(8,128)(2,1)}, bf16[192,128]{1,0:T(8,128)(2,1)S(1)}, bf16[192,128]{1,0:T(8,128)(2,1)})) conditional(s32[]{:T(128)} %convert_element_type.2, (bf16[8,32,512]{2,1,0:T(8,128)(2,1)}, f32[1536,128]{1,0:T(8,128)S(1)}, f32[1536,128]{1,0:T(8,128)S(1)}, f32[8,128]{1,0:T(8,128)S(1)}, ...), branch_computations={%region_6.0_spmd, %region_7.0_spmd} | conditional | bytes 3145764 | solution.py:665
  45.2 4.1 %branch_0_fun.7 = (f32[2048,128]{1,0:T(8,128)S(1)}, bf16[256,512]{1,0:T(8,128)(2,1)}, bf16[192,128]{1,0:T(8,128)(2,1)S(1)}, bf16[192,128]{1,0:T(8,128)(2,1)}) custom-call(f32[1536,128]{1,0:T(8,128)} %copy-done.5, f32[1536,128]{1,0:T(8,128)S(1)} %get-tuple-element.160.mat, f32[8,128]{1,0:T(8,128)S(1)} %get-tuple-element.161.occ, ...), custom_call_target="tpu_custom_call" | custom-call | tf_op jit(solution)/shard_map/cond/branch_0_fun/pallas_call | solution.py:32
  49.3 11.8 %conditional.9 = (f32[2048,128]{1,0:T(8,128)}, f32[512,128]{1,0:T(8,128)S(1)}, bf16[768,128]{1,0:T(8,128)(2,1)}, f32[1536,128]{1,0:T(8,128)}, bf16[384,128]{1,0:...) conditional(s32[]{:T(128)} %clamp.7, ...), branch_computations={%region_8.0_spmd, %region_9.0_spmd, %region_10.0_spmd, %region_11.... | conditional | bytes 4980916 | solution.py:698
  49.3 4.6 %all-to-all-start.1 = ((bf16[8,32,512]{2,1,0:T(8,128)(2,1)}), bf16[8,32,512]{2,1,0:T(8,128)(2,1)}, u32[]{:S(2)}, u32[]{:S(2)}) async-start(bf16[8,32,512]{2,1,0:T(8,128)(2,1)} %bitcast.3), calls=%async_computation.1 | async-start | bytes 524288 | tf_op jit(solution)/shard_map/cond/branch_1_fun/all_to_all | solution.py:594
  53.8 2.8 %branch_1_fun.10 = (f32[1536,128]{1,0:T(8,128)}, f32[2048,128]{1,0:T(8,128)}, f32[512,128]{1,0:T(8,128)S(1)}, bf16[768,128]{1,0:T(8,128)(2,1)}, bf16[384,128]{1,...) custom-call(f32[2048,128]{1,0:T(8,128)S(1)} %get-tuple-element.179.state, ...), custom_call_target="tpu_custom_call" | custom-call | tf_op jit(solution)/shard_map/cond/branch_1_fun/pallas_call | solution.py:32
  56.7 4.4 %all-to-all-done.1 = bf16[8,32,512]{2,1,0:T(8,128)(2,1)} async-done(((bf16[8,32,512]{2,1,0:T(8,128)(2,1)}), bf16[8,32,512]{2,1,0:T(8,128)(2,1)}, u32[]{:S(2)}, u32[]{:S(2)}) %all-to-all-start.1) | async-done | bytes 262176 | tf_op jit(solution)/shard_map/cond/branch_1_fun/all_to_all | solution.py:594
  62.4 8.7 %collective-permute-start.19 = (bf16[256,512]{1,0:T(8,128)(2,1)}, bf16[256,512]{1,0:T(8,128)(2,1)}, u32[]{:S(2)}, u32[]{:S(2)}) collective-permute-start(bf16[256,512]{1,0:T(8,128)(2,1)} %get-tuple-element.300), channel_id=1, source_target_pairs={{8,24},{9,25},{10,26},{11,27},{12,28},{13,29},{14,30},{15,31},{24,... | collective-permute-start | bytes 786440 | tf_op jit(solution)/shard_map/ppermute | solution.py:700
  72.5 3.6 %collective-permute-done.19 = bf16[256,512]{1,0:T(8,128)(2,1)} collective-permute-done((bf16[256,512]{1,0:T(8,128)(2,1)}, bf16[256,512]{1,0:T(8,128)(2,1)}, u32[]{:S(2)}, u32[]{:S(2)}) %collective-permute-start.19) | collective-permute-done | bytes 262176 | tf_op jit(solution)/shard_map/ppermute | solution.py:700
  76.1 16.3 %conditional.10 = (f32[1,3,512,128]{3,2,1,0:T(8,128)}) conditional(s32[]{:T(128)} %convert_element_type.2, (s32[]{:T(128)}, bf16[256,512]{1,0:T(8,128)(2,1)}, bf16[192,128]{1,0:T(8,128)(2,1)S(1)}, bf16[192,128]{1,0:T(8,128)(2,1)}, bf16[256,512]{1,0:T(8,128)(2,1)}, /*index=5*/bf16[256,512]{1,0:T(8,128)(2,1)}, f32[2048,128]{1,0:T(8,128)S(1)}, ...), branch_computations={%region_12.0_spmd, %region_16.0_spmd} | conditional | flops 1 | bytes 4522272 | solution.py:732
  76.1 13.0 %conditional = (bf16[256,512]{1,0:T(8,128)(2,1)}, bf16[192,128]{1,0:T(8,128)(2,1)}, bf16[192,128]{1,0:T(8,128)(2,1)}) conditional(s32[]{:T(128)} %clamp.1, (bf16[256,512]{1,0:T(8,128)(2,1)}, bf16[192,128]{1,0:T(8,128)(2,1)S(1)}, bf16[192,128]{1,0:T(8,128)(2,1)}) %tuple.49, (bf16[256,512]{1,0:T(8,128)(2,1)}, ...), branch_computations={%region_13.0_spmd, %region_14.0_spmd, %region_15.0_spmd} | conditional | bytes 1376420 | solution.py:723
  76.1 4.2 %all-to-all-start.4 = ((bf16[8,32,512]{2,1,0:T(8,128)(2,1)}), bf16[8,32,512]{2,1,0:T(8,128)(2,1)}, u32[]{:S(2)}, u32[]{:S(2)}) async-start(bf16[8,32,512]{2,1,0:T(8,128)(2,1)} %bitcast.9), calls=%async_computation.4 | async-start | bytes 524288 | tf_op jit(solution)/shard_map/cond/branch_0_fun/cond/branch_1_fun/all_to_all | solution.py:594
  80.3 3.8 %collective-permute-start.4 = (bf16[192,128]{1,0:T(8,128)(2,1)S(1)}, bf16[192,128]{1,0:T(8,128)(2,1)}, u32[]{:S(2)}, u32[]{:S(2)}) collective-permute-start(bf16[192,128]{1,0:T(8,128)(2,1)S(1)} %get-tuple-element.224), channel_id=1, source_target_pairs={{8,9},{9,10},{10,11},{11,12},{12,13},{13,14},{14,15}} | collective-permute-start | bytes 147464 | tf_op jit(solution)/shard_map/cond/branch_0_fun/cond/branch_1_fun/ppermute | solution.py:589
  85.4 3.6 %collective-permute-done.5 = bf16[192,128]{1,0:T(8,128)(2,1)} collective-permute-done((bf16[192,128]{1,0:T(8,128)(2,1)S(1)}, bf16[192,128]{1,0:T(8,128)(2,1)}, u32[]{:S(2)}, u32[]{:S(2)}) %collective-permute-start.5) | collective-permute-done | bytes 49184 | tf_op jit(solution)/shard_map/cond/branch_0_fun/cond/branch_1_fun/ppermute | solution.py:590
  89.0 3.3 %branch_0_fun.9 = f32[1536,128]{1,0:T(8,128)} custom-call(f32[2048,128]{1,0:T(8,128)S(1)} %get-tuple-element.229.state, f32[1536,128]{1,0:T(8,128)S(1)} %get-tuple-element.230.mat, f32[8,128]{1,0:T(8,128)S(1)} %get-tuple-element.231.occ, f32[1536,128]{1,0:T(8,128)S(1)} %copy-done.7, bf16[256,128]{1,0:T(8,128)(2,1)S(1)} %get-tuple-element.233.sel, ...), custom_call_target="tpu_custom_call" | custom-call | tf_op jit(solution)/shard_map/cond/branch_0_fun/pallas_call | solution.py:32
  (38 shorter events, 14.4 us)
Async XLA Ops:
  0.0 0.7 copy-start.1
  0.0 0.7 copy-start.2
  3.5 14.7 %all-to-all-start.6 = ((bf16[8,32,640]{2,1,0:T(8,128)(2,1)}), bf16[8,32,640]{2,1,0:T(8,128)(2,1)S(1)}, u32[]{:S(2)}, u32[]{:S(2)}) async-start(bf16[8,32,640]{2,1,0:T(8,128)(2,1)} %bitcast.20), calls=%async_computation.6 | async-start | bytes 655360 | tf_op jit(solution)/shard_map/all_to_all | solution.py:594
  9.9 2.7 %collective-permute-start.12 = (bf16[512,384]{1,0:T(8,128)(2,1)S(1)}, bf16[512,384]{1,0:T(8,128)(2,1)S(1)}, u32[]{:S(2)}, u32[]{:S(2)}) collective-permute-start(bf16[512,384]{1,0:T(8,128)(2,1)S(1)} %get-tuple-element.285), channel_id=1, source_target_pairs={{24,16},{25,17},{26,18},{27,19},{28,20},{29,21},{30,22},{31,23}} | collective-permute-start | bytes 1179656 | tf_op jit(solution)/shard_map/ppermute | solution.py:622
  10.6 10.2 %collective-permute-start.11 = (bf16[512,384]{1,0:T(8,128)(2,1)S(1)}, bf16[512,384]{1,0:T(8,128)(2,1)S(1)}, u32[]{:S(2)}, u32[]{:S(2)}) collective-permute-start(bf16[512,384]{1,0:T(8,128)(2,1)S(1)} %get-tuple-element.285), channel_id=1, source_target_pairs={{24,8},{25,9},{26,10},{27,11},{28,12},{29,13},{30,14},{31,15}} | collective-permute-start | bytes 1179656 | tf_op jit(solution)/shard_map/ppermute | solution.py:622
  11.9 8.9 %collective-permute-start.10 = (bf16[512,384]{1,0:T(8,128)(2,1)S(1)}, bf16[512,384]{1,0:T(8,128)(2,1)S(1)}, u32[]{:S(2)}, u32[]{:S(2)}) collective-permute-start(bf16[512,384]{1,0:T(8,128)(2,1)S(1)} %get-tuple-element.285), channel_id=1, source_target_pairs={{24,0},{25,1},{26,2},{27,3},{28,4},{29,5},{30,6},{31,7}} | collective-permute-start | bytes 1179656 | tf_op jit(solution)/shard_map/ppermute | solution.py:622
  20.7 19.9 %copy-start.3 = (f32[1,3,512,128]{3,2,1,0:T(8,128)S(1)}, f32[1,3,512,128]{3,2,1,0:T(8,128)}, u32[]{:S(2)}) copy-start(f32[1,3,512,128]{3,2,1,0:T(8,128)} %param.23) | copy-start | bytes 2359300
  20.7 19.9 %copy-start.4 = (f32[1,3,512,128]{3,2,1,0:T(8,128)S(1)}, f32[1,3,512,128]{3,2,1,0:T(8,128)}, u32[]{:S(2)}) copy-start(f32[1,3,512,128]{3,2,1,0:T(8,128)} %param.22) | copy-start | bytes 2359300
  21.8 22.5 %all-to-all-start.7 = ((bf16[8,32,512]{2,1,0:T(8,128)(2,1)}), bf16[8,32,512]{2,1,0:T(8,128)(2,1)}, u32[]{:S(2)}, u32[]{:S(2)}) async-start(bf16[8,32,512]{2,1,0:T(8,128)(2,1)} %bitcast.22), calls=%async_computation.7 | async-start | bytes 524288 | tf_op jit(solution)/shard_map/all_to_all | solution.py:594
  27.2 15.5 %collective-permute-start.17 = (bf16[256,640]{1,0:T(8,128)(2,1)S(1)}, bf16[256,640]{1,0:T(8,128)(2,1)}, u32[]{:S(2)}, u32[]{:S(2)}) collective-permute-start(bf16[256,640]{1,0:T(8,128)(2,1)S(1)} %bitcast.40), channel_id=1, source_target_pairs={{16,24},{17,25},{18,26},{19,27},{20,28},{21,29},{22,30},{23,31}} | collective-permute-start | bytes 983048 | tf_op jit(solution)/shard_map/ppermute | solution.py:641
  28.6 14.1 %collective-permute-start.16 = (bf16[256,640]{1,0:T(8,128)(2,1)S(1)}, bf16[256,640]{1,0:T(8,128)(2,1)}, u32[]{:S(2)}, u32[]{:S(2)}) collective-permute-start(bf16[256,640]{1,0:T(8,128)(2,1)S(1)} %bitcast.41), channel_id=1, source_target_pairs={{8,24},{9,25},{10,26},{11,27},{12,28},{13,29},{14,30},{15,31}} | collective-permute-start | bytes 983048 | tf_op jit(solution)/shard_map/ppermute | solution.py:641
  34.0 8.7 %collective-permute-start.15 = (bf16[256,640]{1,0:T(8,128)(2,1)S(1)}, bf16[256,640]{1,0:T(8,128)(2,1)}, u32[]{:S(2)}, u32[]{:S(2)}) collective-permute-start(bf16[256,640]{1,0:T(8,128)(2,1)S(1)} %bitcast.42), channel_id=1, source_target_pairs={{0,24},{1,25},{2,26},{3,27},{4,28},{5,29},{6,30},{7,31}} | collective-permute-start | bytes 983048 | tf_op jit(solution)/shard_map/ppermute | solution.py:641
  35.4 7.3 %collective-permute-start.13 = (bf16[200,128]{1,0:T(8,128)(2,1)S(1)}, bf16[200,128]{1,0:T(8,128)(2,1)}, u32[]{:S(2)}, u32[]{:S(2)}) collective-permute-start(bf16[200,128]{1,0:T(8,128)(2,1)S(1)} %get-tuple-element.290), channel_id=1, source_target_pairs={{0,1},{1,2},{2,3},{3,4},{4,5},{5,6},{6,7},{8,9},{9,10},{10,11},{11... | collective-permute-start | bytes 153608 | tf_op jit(solution)/shard_map/ppermute | solution.py:589
  39.3 5.0 %collective-permute-start.14 = (bf16[200,128]{1,0:T(8,128)(2,1)S(1)}, bf16[200,128]{1,0:T(8,128)(2,1)}, u32[]{:S(2)}, u32[]{:S(2)}) collective-permute-start(bf16[200,128]{1,0:T(8,128)(2,1)S(1)} %get-tuple-element.291), channel_id=1, source_target_pairs={{1,0},{2,1},{3,2},{4,3},{5,4},{6,5},{7,6},{9,8},{10,9},{11,10},{12... | collective-permute-start | bytes 153608 | tf_op jit(solution)/shard_map/ppermute | solution.py:590
  44.3 0.9 copy-start.5
  49.3 11.8 %all-to-all-start.1 = ((bf16[8,32,512]{2,1,0:T(8,128)(2,1)}), bf16[8,32,512]{2,1,0:T(8,128)(2,1)}, u32[]{:S(2)}, u32[]{:S(2)}) async-start(bf16[8,32,512]{2,1,0:T(8,128)(2,1)} %bitcast.3), calls=%async_computation.1 | async-start | bytes 524288 | tf_op jit(solution)/shard_map/cond/branch_1_fun/all_to_all | solution.py:594
  61.0 11.5 %collective-permute-start.18 = (bf16[256,512]{1,0:T(8,128)(2,1)}, bf16[256,512]{1,0:T(8,128)(2,1)}, u32[]{:S(2)}, u32[]{:S(2)}) collective-permute-start(bf16[256,512]{1,0:T(8,128)(2,1)} %get-tuple-element.297), channel_id=1, source_target_pairs={{0,24},{1,25},{2,26},{3,27},{4,28},{5,29},{6,30},{7,31},{24,0},{25... | collective-permute-start | bytes 786440 | tf_op jit(solution)/shard_map/ppermute | solution.py:700
  62.4 13.7 %collective-permute-start.19 = (bf16[256,512]{1,0:T(8,128)(2,1)}, bf16[256,512]{1,0:T(8,128)(2,1)}, u32[]{:S(2)}, u32[]{:S(2)}) collective-permute-start(bf16[256,512]{1,0:T(8,128)(2,1)} %get-tuple-element.300), channel_id=1, source_target_pairs={{8,24},{9,25},{10,26},{11,27},{12,28},{13,29},{14,30},{15,31},{24,... | collective-permute-start | bytes 786440 | tf_op jit(solution)/shard_map/ppermute | solution.py:700
  71.1 4.9 %collective-permute-start.20 = (bf16[256,512]{1,0:T(8,128)(2,1)}, bf16[256,512]{1,0:T(8,128)(2,1)}, u32[]{:S(2)}, u32[]{:S(2)}) collective-permute-start(bf16[256,512]{1,0:T(8,128)(2,1)} %get-tuple-element.301), channel_id=1, source_target_pairs={{16,24},{17,25},{18,26},{19,27},{20,28},{21,29},{22,30},{23,31},{2... | collective-permute-start | bytes 786440 | tf_op jit(solution)/shard_map/ppermute | solution.py:700
  76.1 13.0 %copy-start.7 = (f32[1536,128]{1,0:T(8,128)S(1)}, f32[1536,128]{1,0:T(8,128)}, u32[]{:S(2)}) copy-start(f32[1536,128]{1,0:T(8,128)} %get-tuple-element.232.base) | copy-start | bytes 2359300 | tf_op jit(solution)/shard_map/cond
  76.1 8.0 %copy-start.8 = (bf16[192,128]{1,0:T(8,128)(2,1)S(1)}, bf16[192,128]{1,0:T(8,128)(2,1)}, u32[]{:S(2)}) copy-start(bf16[192,128]{1,0:T(8,128)(2,1)} %get-tuple-element.225) | copy-start | bytes 147460 | tf_op jit(solution)/shard_map/cond/branch_0_fun/cond
  76.1 13.0 %all-to-all-start.4 = ((bf16[8,32,512]{2,1,0:T(8,128)(2,1)}), bf16[8,32,512]{2,1,0:T(8,128)(2,1)}, u32[]{:S(2)}, u32[]{:S(2)}) async-start(bf16[8,32,512]{2,1,0:T(8,128)(2,1)} %bitcast.9), calls=%async_computation.4 | async-start | bytes 524288 | tf_op jit(solution)/shard_map/cond/branch_0_fun/cond/branch_1_fun/all_to_all | solution.py:594
  80.3 5.1 %collective-permute-start.4 = (bf16[192,128]{1,0:T(8,128)(2,1)S(1)}, bf16[192,128]{1,0:T(8,128)(2,1)}, u32[]{:S(2)}, u32[]{:S(2)}) collective-permute-start(bf16[192,128]{1,0:T(8,128)(2,1)S(1)} %get-tuple-element.224), channel_id=1, source_target_pairs={{8,9},{9,10},{10,11},{11,12},{12,13},{13,14},{14,15}} | collective-permute-start | bytes 147464 | tf_op jit(solution)/shard_map/cond/branch_0_fun/cond/branch_1_fun/ppermute | solution.py:589
  84.1 4.9 %collective-permute-start.5 = (bf16[192,128]{1,0:T(8,128)(2,1)S(1)}, bf16[192,128]{1,0:T(8,128)(2,1)}, u32[]{:S(2)}, u32[]{:S(2)}) collective-permute-start(bf16[192,128]{1,0:T(8,128)(2,1)S(1)} %copy-done.8), channel_id=1, source_target_pairs={{9,8},{10,9},{11,10},{12,11},{13,12},{14,13},{15,14}} | collective-permute-start | bytes 147464 | tf_op jit(solution)/shard_map/cond/branch_0_fun/cond/branch_1_fun/ppermute | solution.py:590
  (1 other events, 0.7 us)

commit v7 on v6

--- a/solution.py
+++ b/solution.py
@@ -169,7 +169,7 @@
             put_slab(out, a, i, force)
 
 
-def advance(ref, mat, filled, base, recv, sel, low, high, fills, out, pressure, stress, partial):
+def advance(ref, rates, filled, base, recv, sel, low, high, fills, out, pressure, stress, partial):
     e = filled.shape[-1]
     pressure[...] = dot(recv[...], sel[...], ((0,), (0,))) * PRESSURE_SCALE
     for i in range(8):
@@ -182,7 +182,7 @@
     penalty = PENALTY * UNIT_LENGTH
     fill_low, fill_high = fills[0].reshape(1, 1, e), fills[1].reshape(1, 1, e)
     for i in range(8):
-        rate = (TIME_STEP / UNIT_LENGTH) * slab(mat, 2, i) * filled
+        rate = slab(rates, 0, i)
         for a in range(3):
             here = slab(ref, a, i)
             force = slab(partial, a, i) - diff_i(
@@ -355,7 +355,7 @@
 
 
 def prepare(n_blk, cap, tiles, solvent):
-    def body(grp, state, occ, col, octant, send, sel, filled, field, phi, up, down, *scratch):
+    def body(grp, state, occ, col, octant, send, sel, filled, near, far, phi, up, down, *scratch):
         dil, ints, layers, int_sems, sem = scratch
         e = state.shape[-1]
         quarter = 16 * tiles
@@ -404,7 +404,8 @@
                     for oy in range(2):
                         p = pressures(layers[pl.ds(LANES * (8 * ox + i) + 64 * oy, 64), :])
                         parts.append(p[:, :quarter])
-                field[pl.ds(64 * i, 64), :] = jnp.concatenate(parts, axis=1)
+                half = near if i < 4 else far
+                half[pl.ds(64 * (i % 4), 64), :] = jnp.concatenate(parts, axis=1)
             copy.wait()
 
     return body
@@ -420,11 +421,19 @@
 
 
 def gather_field(quarter):
-    def body(recv, field, out):
+    def body(recv, near, far, out):
         hot = one_hot(recv[:, pl.ds(512, LANES)].astype(F32), quarter)
-        out[...] = dot(hot, field[...], ((1,), (1,))).astype(BF16)
+        for n, half in enumerate((near, far)):
+            out[:, pl.ds(256 * n, 256)] = dot(hot, half[...], ((1,), (1,))).astype(BF16)
 
     return body
+
+
+def elastic_and_rate(state, mat, occ, out, rate, *scratch):
+    filled = occ[pl.ds(0, 1), :].reshape(1, 1, occ.shape[-1])
+    for i in range(8):
+        put_slab(rate, 0, i, (TIME_STEP / UNIT_LENGTH) * slab(mat, 2, i) * filled)
+    elastic(state, mat, filled, out, *scratch)
 
 
 def elastic_forces(state, mat, occ, out, *scratch):
@@ -435,20 +444,20 @@
     pass
 
 
-def first_step(state, mat, occ, base, sel, recv, low, high, out, send, up, down, *scratch):
+def first_step(state, rates, occ, base, sel, recv, low, high, out, send, up, down, *scratch):
     filled = occ[pl.ds(0, 1), :].reshape(1, 1, occ.shape[-1])
     fills = [ref[pl.ds(192, 8), :].astype(F32)[:1] for ref in (low, high)]
-    advance(state, mat, filled, base, recv, sel, low, high, fills, out, *scratch[:3])
+    advance(state, rates, filled, base, recv, sel, low, high, fills, out, *scratch[:3])
     dil = scratch[3]
     dilate(out, filled, dil)
     send[...] = dot(sel[...], dil[...], ((1,), (1,))).astype(BF16)
     put_faces(out, up, down)
 
 
-def last_step(state, mat, occ, base, sel, recv, low, high, fill_low, fill_high, out, *scratch):
+def last_step(state, rates, occ, base, sel, recv, low, high, fill_low, fill_high, out, *scratch):
     filled = occ[pl.ds(0, 1), :].reshape(1, 1, occ.shape[-1])
     fills = [ref[pl.ds(192, 8), :].astype(F32)[:1] for ref in (fill_low, fill_high)]
-    advance(state, mat, filled, base, recv, sel, low, high, fills, out, *scratch)
+    advance(state, rates, filled, base, recv, sel, low, high, fills, out, *scratch)
 
 
 def deposit(edged):
@@ -593,14 +602,15 @@
     def swap(block):
         return lax.all_to_all(block, "blk", split_axis=0, concat_axis=0, tiled=True)
 
-    send, sel, occ, field, phi, up, down = call(
+    send, sel, occ, near, far, phi, up, down = call(
         prepare(n_blk, cap, tiles, solvent),
         (grp_at, current, occupied.reshape(1, e), col, octant),
         (
             shape_of((slots, 512 + LANES), BF16),
             shape_of((slots, e), BF16),
             shape_of((8, e)),
-            shape_of((512, 4 * q_count), BF16),
+            shape_of((256, 4 * q_count), BF16),
+            shape_of((256, 4 * q_count), BF16),
             layers,
             side,
             side,
@@ -614,19 +624,29 @@
         ],
         smem=1,
         away=(2, 3, 4),
-        unused=(4,),
+        unused=(5,),
     )
     recv = swap(send)
-    fields = []
-    for g in groups:
-        fields.append(lax.ppermute(field, axes, pairs(True, g)))
+
+    def field_to(half, route):
+        return lax.ppermute(half, axes, route)
+
+    def across(i, j):
+        return [(i * n_blk + b, j * n_blk + b) for b in range(n_blk)]
+
+    near0 = field_to(near, pairs(True, 0))
+    far1 = field_to(far, pairs(True, 1))
+    fields = [(near0, field_to(far1, across(1, 0)))]
+    fields.append((field_to(near0, across(0, 1)), far1))
+    for g in groups[2:]:
+        fields.append(tuple(field_to(half, pairs(True, g)) for half in (near, far)))
     side_low, side_high = both_ways(up, down, groups)
     work = [pltpu.VMEM((512, e), F32), pltpu.VMEM((1536, e), F32), pltpu.VMEM((1536, e), F32)]
     sweeping = [pltpu.VMEM(layers.shape, F32)] + [pltpu.VMEM((16, 8, LANES), F32)] * 2
 
     def gathered(g):
         def run():
-            return call(gather_field(q_count), (recv, fields[g]), (rows,))[0]
+            return call(gather_field(q_count), (recv, *fields[g]), (rows,))[0]
 
         return run
 
@@ -644,15 +664,13 @@
         return tuple(call(rates(tiles), (mat,), (layers, ends)))
 
     def mech_elastic():
-        return tuple(
-            call(elastic_forces, (current, mat, occ), (layers, ends), work[1:], unused=(1,))
-        )
+        return tuple(call(elastic_and_rate, (current, mat, occ), (layers, ends), work[1:]))
 
     def mech_first():
         return tuple(
             call(
                 first_step,
-                (current, mat, occ, base, sel, mine, side_low, side_high),
+                (current, kap_edge, occ, base, sel, mine, side_low, side_high),
                 (layers, rows, face, face),
                 work + [pltpu.VMEM((512, e), BF16)],
             )
@@ -723,7 +741,7 @@
         mine, low, high = lax.switch(grp, [swapped(g) for g in groups])
         (out,) = call(
             last_step,
-            (moved, mat, occ, force, sel, mine, low, high, side_low, side_high),
+            (moved, kap_edge, occ, force, sel, mine, low, high, side_low, side_high),
             (flat,),
             work,
         )

time: 93.2 us -> 91.7 us (0.984)
  waiting for transfers between devices: 21.3 us -> 19.5 us
  local copies, waits for them, and re-layouts: 1.58 us -> 2.91 us
  starting transfers between devices: 53.2 us -> 52.1 us
    all_to_all x4, waiting for transfers between devices: 9.97 us -> 4.36 us  [swap(): return lax.all_to_all(block, 'blk', split_axis=0, concat_axis=0, tiled=True)]
    ppermute x3 -> x6, waiting for transfers between devices: 2.56 us -> 6.4 us  [field_to(): return lax.ppermute(half, axes, route)]
    ppermute x3 -> x6, starting transfers between devices: 2.65 us -> 6.1 us  [field_to(): return lax.ppermute(half, axes, route)]
    ppermute x3, starting transfers between devices: 8.15 us -> 4.83 us  [shards(): arrived.append(lax.ppermute(recv, axes, pairs(False, g)))]
    ppermute x3, starting transfers between devices: 11.5 us -> 9.95 us  [shards(): lax.ppermute(block, axes, pairs(False, g) + pairs(True, g))]
    unnamed x10 -> x14, local copies, waits for them, and re-layouts: 0.69 us -> 2.02 us
  transfers between devices with their start and end apart: 17 -> 20, of which waited for: 6 -> 5; matrix products, arithmetic and copies ran while one was open for 0% -> 0% of each run, Pallas kernels for 5% -> 5%
where the time goes in v7:
time: 91.7 us; the launch traced here: 90.8 us
  starting transfers between devices  52.1 us (57%)
  waiting for transfers between devices  19.5 us (21%)
  Pallas kernels  16.1 us (18%)
  local copies, waits for them, and re-layouts  2.91 us (3%)
    all_to_all x4, starting transfers between devices, swap(): return lax.all_to_all(block, 'blk', split_axis=0, concat_axis=0, tiled=True)  20.8 us
    pallas_call x6, Pallas kernels, call(): pl.pallas_call(body, out_shape=outs, in_specs=[ANY if n in away else spec...  16.1 us
    ppermute x3, starting transfers between devices, shards(): lax.ppermute(block, axes, pairs(False, g) + pairs(True, g))  9.95 us
    ppermute x2, starting transfers between devices, both_ways(): lax.ppermute(up, axes, planes(True, which))  7.81 us
    ppermute x6, waiting for transfers between devices, field_to(): return lax.ppermute(half, axes, route)  6.4 us
    ppermute x6, starting transfers between devices, field_to(): return lax.ppermute(half, axes, route)  6.1 us
    ppermute x2, waiting for transfers between devices, both_ways(): lax.ppermute(down, axes, planes(False, which))  5.19 us
    ppermute x3, starting transfers between devices, shards(): arrived.append(lax.ppermute(recv, axes, pairs(False, g)))  4.83 us
  transfers between devices with their start and end apart: 20, of which 5 were waited for; matrix products, arithmetic and copies ran while one was open for 0% of the time, Pallas kernels for 5%

profile of v7, /device:TPU:1, one launch (start us, length us, event | category | flops | bytes accessed | tf_op | source)
XLA Modules:
  0.0 90.8 jit_solution(5900021316925149527)
XLA Ops:
  0.7 2.8 %shard_map.57 = (bf16[256,640]{1,0:T(8,128)(2,1)}, bf16[256,128]{1,0:T(8,128)(2,1)S(1)}, f32[8,128]{1,0:T(8,128)S(1)}, bf16[256,384]{1,0:T(8,128)(2,1)S(1)}, bf1...) custom-call(s32[1]{0:T(128)} %bitcast.15.grp, ...), custom_call_target="tpu_custom_call" | custom-call | tf_op jit(solution)/shard_map/pallas_call | solution.py:32
  3.5 6.4 %all-to-all-start.6 = ((bf16[8,32,640]{2,1,0:T(8,128)(2,1)}), bf16[8,32,640]{2,1,0:T(8,128)(2,1)S(1)}, u32[]{:S(2)}, u32[]{:S(2)}) async-start(bf16[8,32,640]{2,1,0:T(8,128)(2,1)} %bitcast.20), calls=%async_computation.6 | async-start | bytes 655360 | tf_op jit(solution)/shard_map/all_to_all | solution.py:603
  13.1 6.4 %collective-permute-done.11 = bf16[256,384]{1,0:T(8,128)(2,1)S(1)} collective-permute-done((bf16[256,384]{1,0:T(8,128)(2,1)S(1)}, bf16[256,384]{1,0:T(8,128)(2,1)S(1)}, u32[]{:S(2)}, u32[]{:S(2)}) %collective-permute-start.11) | collective-permute-done | bytes 196640 | tf_op jit(solution)/shard_map/ppermute | solution.py:632
  19.5 1.5 %collective-permute-start.12 = (bf16[256,384]{1,0:T(8,128)(2,1)S(1)}, bf16[256,384]{1,0:T(8,128)(2,1)S(1)}, u32[]{:S(2)}, u32[]{:S(2)}) collective-permute-start(bf16[256,384]{1,0:T(8,128)(2,1)S(1)} %collective-permute-done.11), channel_id=1, source_target_pairs={{8,0},{9,1},{10,2},{11,3},{12,4},{13,5},{14,6},{15,7}} | collective-permute-start | bytes 589832 | tf_op jit(solution)/shard_map/ppermute | solution.py:632
  24.9 5.7 %all-to-all-start.7 = ((bf16[8,32,512]{2,1,0:T(8,128)(2,1)}), bf16[8,32,512]{2,1,0:T(8,128)(2,1)}, u32[]{:S(2)}, u32[]{:S(2)}) async-start(bf16[8,32,512]{2,1,0:T(8,128)(2,1)} %bitcast.22), calls=%async_computation.7 | async-start | bytes 524288 | tf_op jit(solution)/shard_map/all_to_all | solution.py:603
  32.0 2.0 %collective-permute-start.19 = (bf16[256,640]{1,0:T(8,128)(2,1)S(1)}, bf16[256,640]{1,0:T(8,128)(2,1)}, u32[]{:S(2)}, u32[]{:S(2)}) collective-permute-start(bf16[256,640]{1,0:T(8,128)(2,1)S(1)} %bitcast.39), channel_id=1, source_target_pairs={{8,24},{9,25},{10,26},{11,27},{12,28},{13,29},{14,30},{15,31}} | collective-permute-start | bytes 983048 | tf_op jit(solution)/shard_map/ppermute | solution.py:661
  35.4 4.0 %collective-permute-start.16 = (bf16[200,128]{1,0:T(8,128)(2,1)S(1)}, bf16[200,128]{1,0:T(8,128)(2,1)}, u32[]{:S(2)}, u32[]{:S(2)}) collective-permute-start(bf16[200,128]{1,0:T(8,128)(2,1)S(1)} %get-tuple-element.302), channel_id=1, source_target_pairs={{0,1},{1,2},{2,3},{3,4},{4,5},{5,6},{6,7},{8,9},{9,10},{10,11},{11... | collective-permute-start | bytes 153608 | tf_op jit(solution)/shard_map/ppermute | solution.py:598
  40.7 2.0 %conditional.7 = ((f32[2048,128]{1,0:T(8,128)S(1)}, f32[512,128]{1,0:T(8,128)S(1)})) conditional(s32[]{:T(128)} %convert_element_type.2, (f32[1536,128]{1,0:T(8,128)S(1)}, f32[1536,128]{1,0:T(8,128)S(1)}, f32[8,128]{1,0:T(8,128)S(1)}) %tuple.105, f32[1536,128]{1,0:T(8,128)S(1)} %bitcast.27), branch_computations={%region_0.0_spmd, %region_1.0_spmd} | conditional | bytes 8 | solution.py:680
  40.7 2.0 %branch_0_fun.5 = (f32[2048,128]{1,0:T(8,128)S(1)}, f32[512,128]{1,0:T(8,128)S(1)}) custom-call(f32[1536,128]{1,0:T(8,128)S(1)} %get-tuple-element.156.state, f32[1536,128]{1,0:T(8,128)S(1)} %get-tuple-element.157.mat, f32[8,128]{1,0:T(8,128)S(1)} %get-tuple-element.158.occ), custom_call_target="tpu_custom_call" | custom-call | tf_op jit(solution)/shard_map/cond/branch_0_fun/pallas_call | solution.py:32
  42.8 1.6 %collective-permute-done.17 = bf16[200,128]{1,0:T(8,128)(2,1)} collective-permute-done((bf16[200,128]{1,0:T(8,128)(2,1)S(1)}, bf16[200,128]{1,0:T(8,128)(2,1)}, u32[]{:S(2)}, u32[]{:S(2)}) %collective-permute-start.17) | collective-permute-done | bytes 51232 | tf_op jit(solution)/shard_map/ppermute | solution.py:599
  44.3 5.0 %conditional.8 = ((f32[2048,128]{1,0:T(8,128)S(1)}, bf16[256,512]{1,0:T(8,128)(2,1)}, bf16[192,128]{1,0:T(8,128)(2,1)S(1)}, bf16[192,128]{1,0:T(8,128)(2,1)})) conditional(s32[]{:T(128)} %convert_element_type.2, (bf16[8,32,512]{2,1,0:T(8,128)(2,1)}, f32[1536,128]{1,0:T(8,128)S(1)}, f32[512,128]{1,0:T(8,128)S(1)}, f32[8,128]{1,0:T(8,128)S(1)}, ...), branch_computations={%region_6.0_spmd, %region_7.0_spmd} | conditional | bytes 3145764 | solution.py:683
  45.2 4.1 %branch_0_fun.7 = (f32[2048,128]{1,0:T(8,128)S(1)}, bf16[256,512]{1,0:T(8,128)(2,1)}, bf16[192,128]{1,0:T(8,128)(2,1)S(1)}, bf16[192,128]{1,0:T(8,128)(2,1)}) custom-call(f32[1536,128]{1,0:T(8,128)} %copy-done.5, f32[512,128]{1,0:T(8,128)S(1)} %get-tuple-element.169.rates, f32[8,128]{1,0:T(8,128)S(1)} %get-tuple-element.170.occ, ...), custom_call_target="tpu_custom_call" | custom-call | tf_op jit(solution)/shard_map/cond/branch_0_fun/pallas_call | solution.py:32
  49.3 11.7 %conditional.9 = (f32[2048,128]{1,0:T(8,128)}, f32[512,128]{1,0:T(8,128)S(1)}, bf16[768,128]{1,0:T(8,128)(2,1)}, f32[1536,128]{1,0:T(8,128)}, bf16[384,128]{1,0:...) conditional(s32[]{:T(128)} %clamp.7, ...), branch_computations={%region_8.0_spmd, %region_9.0_spmd, %region_10.0_spmd, %region_11.... | conditional | bytes 4980916 | solution.py:716
  49.3 4.6 %all-to-all-start.1 = ((bf16[8,32,512]{2,1,0:T(8,128)(2,1)}), bf16[8,32,512]{2,1,0:T(8,128)(2,1)}, u32[]{:S(2)}, u32[]{:S(2)}) async-start(bf16[8,32,512]{2,1,0:T(8,128)(2,1)} %bitcast.3), calls=%async_computation.1 | async-start | bytes 524288 | tf_op jit(solution)/shard_map/cond/branch_1_fun/all_to_all | solution.py:603
  53.8 2.8 %branch_1_fun.10 = (f32[1536,128]{1,0:T(8,128)}, f32[2048,128]{1,0:T(8,128)}, f32[512,128]{1,0:T(8,128)S(1)}, bf16[768,128]{1,0:T(8,128)(2,1)}, bf16[384,128]{1,...) custom-call(f32[2048,128]{1,0:T(8,128)S(1)} %get-tuple-element.188.state, ...), custom_call_target="tpu_custom_call" | custom-call | tf_op jit(solution)/shard_map/cond/branch_1_fun/pallas_call | solution.py:32
  56.7 4.4 %all-to-all-done.1 = bf16[8,32,512]{2,1,0:T(8,128)(2,1)} async-done(((bf16[8,32,512]{2,1,0:T(8,128)(2,1)}), bf16[8,32,512]{2,1,0:T(8,128)(2,1)}, u32[]{:S(2)}, u32[]{:S(2)}) %all-to-all-start.1) | async-done | bytes 262176 | tf_op jit(solution)/shard_map/cond/branch_1_fun/all_to_all | solution.py:603
  62.4 7.2 %collective-permute-start.22 = (bf16[256,512]{1,0:T(8,128)(2,1)}, bf16[256,512]{1,0:T(8,128)(2,1)}, u32[]{:S(2)}, u32[]{:S(2)}) collective-permute-start(bf16[256,512]{1,0:T(8,128)(2,1)} %get-tuple-element.311), channel_id=1, source_target_pairs={{8,24},{9,25},{10,26},{11,27},{12,28},{13,29},{14,30},{15,31},{24,... | collective-permute-start | bytes 786440 | tf_op jit(solution)/shard_map/ppermute | solution.py:718
  71.0 3.6 %collective-permute-done.22 = bf16[256,512]{1,0:T(8,128)(2,1)} collective-permute-done((bf16[256,512]{1,0:T(8,128)(2,1)}, bf16[256,512]{1,0:T(8,128)(2,1)}, u32[]{:S(2)}, u32[]{:S(2)}) %collective-permute-start.22) | collective-permute-done | bytes 262176 | tf_op jit(solution)/shard_map/ppermute | solution.py:718
  74.6 16.3 %conditional.10 = (f32[1,3,512,128]{3,2,1,0:T(8,128)}) conditional(s32[]{:T(128)} %convert_element_type.2, (s32[]{:T(128)}, bf16[256,512]{1,0:T(8,128)(2,1)}, bf16[192,128]{1,0:T(8,128)(2,1)S(1)}, bf16[192,128]{1,0:T(8,128)(2,1)}, bf16[256,512]{1,0:T(8,128)(2,1)}, /*index=5*/bf16[256,512]{1,0:T(8,128)(2,1)}, f32[2048,128]{1,0:T(8,128)S(1)}, ...), branch_computations={%region_12.0_spmd, %region_16.0_spmd} | conditional | flops 1 | bytes 4522272 | solution.py:750
  74.6 13.0 %conditional = (bf16[256,512]{1,0:T(8,128)(2,1)}, bf16[192,128]{1,0:T(8,128)(2,1)}, bf16[192,128]{1,0:T(8,128)(2,1)}) conditional(s32[]{:T(128)} %clamp.1, (bf16[256,512]{1,0:T(8,128)(2,1)}, bf16[192,128]{1,0:T(8,128)(2,1)S(1)}, bf16[192,128]{1,0:T(8,128)(2,1)}) %tuple.49, (bf16[256,512]{1,0:T(8,128)(2,1)}, ...), branch_computations={%region_13.0_spmd, %region_14.0_spmd, %region_15.0_spmd} | conditional | bytes 1376420 | solution.py:741
  74.6 4.2 %all-to-all-start.4 = ((bf16[8,32,512]{2,1,0:T(8,128)(2,1)}), bf16[8,32,512]{2,1,0:T(8,128)(2,1)}, u32[]{:S(2)}, u32[]{:S(2)}) async-start(bf16[8,32,512]{2,1,0:T(8,128)(2,1)} %bitcast.9), calls=%async_computation.4 | async-start | bytes 524288 | tf_op jit(solution)/shard_map/cond/branch_0_fun/cond/branch_1_fun/all_to_all | solution.py:603
  78.8 3.8 %collective-permute-start.4 = (bf16[192,128]{1,0:T(8,128)(2,1)S(1)}, bf16[192,128]{1,0:T(8,128)(2,1)}, u32[]{:S(2)}, u32[]{:S(2)}) collective-permute-start(bf16[192,128]{1,0:T(8,128)(2,1)S(1)} %get-tuple-element.233), channel_id=1, source_target_pairs={{8,9},{9,10},{10,11},{11,12},{12,13},{13,14},{14,15}} | collective-permute-start | bytes 147464 | tf_op jit(solution)/shard_map/cond/branch_0_fun/cond/branch_1_fun/ppermute | solution.py:598
  83.9 3.6 %collective-permute-done.5 = bf16[192,128]{1,0:T(8,128)(2,1)} collective-permute-done((bf16[192,128]{1,0:T(8,128)(2,1)S(1)}, bf16[192,128]{1,0:T(8,128)(2,1)}, u32[]{:S(2)}, u32[]{:S(2)}) %collective-permute-start.5) | collective-permute-done | bytes 49184 | tf_op jit(solution)/shard_map/cond/branch_0_fun/cond/branch_1_fun/ppermute | solution.py:599
  87.5 3.3 %branch_0_fun.9 = f32[1536,128]{1,0:T(8,128)} custom-call(f32[2048,128]{1,0:T(8,128)S(1)} %get-tuple-element.238.state, f32[512,128]{1,0:T(8,128)S(1)} %get-tuple-element.239.rates, f32[8,128]{1,0:T(8,128)S(1)} %get-tuple-element.240.occ, f32[1536,128]{1,0:T(8,128)S(1)} %copy-done.7, bf16[256,128]{1,0:T(8,128)(2,1)S(1)} %get-tuple-element.242.sel, ...), custom_call_target="tpu_custom_call" | custom-call | tf_op jit(solution)/shard_map/cond/branch_0_fun/pallas_call | solution.py:32
  (48 shorter events, 17.7 us)
Async XLA Ops:
  3.5 18.9 %all-to-all-start.6 = ((bf16[8,32,640]{2,1,0:T(8,128)(2,1)}), bf16[8,32,640]{2,1,0:T(8,128)(2,1)S(1)}, u32[]{:S(2)}, u32[]{:S(2)}) async-start(bf16[8,32,640]{2,1,0:T(8,128)(2,1)} %bitcast.20), calls=%async_computation.6 | async-start | bytes 655360 | tf_op jit(solution)/shard_map/all_to_all | solution.py:603
  9.9 2.0 %collective-permute-start.10 = (bf16[256,384]{1,0:T(8,128)(2,1)S(1)}, bf16[256,384]{1,0:T(8,128)(2,1)S(1)}, u32[]{:S(2)}, u32[]{:S(2)}) collective-permute-start(bf16[256,384]{1,0:T(8,128)(2,1)S(1)} %get-tuple-element.295), channel_id=1, source_target_pairs={{24,0},{25,1},{26,2},{27,3},{28,4},{29,5},{30,6},{31,7}} | collective-permute-start | bytes 589832 | tf_op jit(solution)/shard_map/ppermute | solution.py:632
  10.5 9.0 %collective-permute-start.11 = (bf16[256,384]{1,0:T(8,128)(2,1)S(1)}, bf16[256,384]{1,0:T(8,128)(2,1)S(1)}, u32[]{:S(2)}, u32[]{:S(2)}) collective-permute-start(bf16[256,384]{1,0:T(8,128)(2,1)S(1)} %get-tuple-element.296), channel_id=1, source_target_pairs={{24,8},{25,9},{26,10},{27,11},{28,12},{29,13},{30,14},{31,15}} | collective-permute-start | bytes 589832 | tf_op jit(solution)/shard_map/ppermute | solution.py:632
  11.8 10.6 %collective-permute-start.13 = (bf16[256,384]{1,0:T(8,128)(2,1)S(1)}, bf16[256,384]{1,0:T(8,128)(2,1)S(1)}, u32[]{:S(2)}, u32[]{:S(2)}) collective-permute-start(bf16[256,384]{1,0:T(8,128)(2,1)S(1)} %collective-permute-done.10), channel_id=1, source_target_pairs={{0,8},{1,9},{2,10},{3,11},{4,12},{5,13},{6,14},{7,15}} | collective-permute-start | bytes 589832 | tf_op jit(solution)/shard_map/ppermute | solution.py:632
  19.5 2.9 %collective-permute-start.12 = (bf16[256,384]{1,0:T(8,128)(2,1)S(1)}, bf16[256,384]{1,0:T(8,128)(2,1)S(1)}, u32[]{:S(2)}, u32[]{:S(2)}) collective-permute-start(bf16[256,384]{1,0:T(8,128)(2,1)S(1)} %collective-permute-done.11), channel_id=1, source_target_pairs={{8,0},{9,1},{10,2},{11,3},{12,4},{13,5},{14,6},{15,7}} | collective-permute-start | bytes 589832 | tf_op jit(solution)/shard_map/ppermute | solution.py:632
  21.1 1.4 %collective-permute-start.14 = (bf16[256,384]{1,0:T(8,128)(2,1)S(1)}, bf16[256,384]{1,0:T(8,128)(2,1)S(1)}, u32[]{:S(2)}, u32[]{:S(2)}) collective-permute-start(bf16[256,384]{1,0:T(8,128)(2,1)S(1)} %get-tuple-element.295), channel_id=1, source_target_pairs={{24,16},{25,17},{26,18},{27,19},{28,20},{29,21},{30,22},{31,23}} | collective-permute-start | bytes 589832 | tf_op jit(solution)/shard_map/ppermute | solution.py:632
  21.7 0.7 collective-permute-start.15
  23.8 16.8 %copy-start.3 = (f32[1,3,512,128]{3,2,1,0:T(8,128)S(1)}, f32[1,3,512,128]{3,2,1,0:T(8,128)}, u32[]{:S(2)}) copy-start(f32[1,3,512,128]{3,2,1,0:T(8,128)} %param.23) | copy-start | bytes 2359300
  23.8 16.8 %copy-start.4 = (f32[1,3,512,128]{3,2,1,0:T(8,128)S(1)}, f32[1,3,512,128]{3,2,1,0:T(8,128)}, u32[]{:S(2)}) copy-start(f32[1,3,512,128]{3,2,1,0:T(8,128)} %param.22) | copy-start | bytes 2359300
  24.9 19.4 %all-to-all-start.7 = ((bf16[8,32,512]{2,1,0:T(8,128)(2,1)}), bf16[8,32,512]{2,1,0:T(8,128)(2,1)}, u32[]{:S(2)}, u32[]{:S(2)}) async-start(bf16[8,32,512]{2,1,0:T(8,128)(2,1)} %bitcast.22), calls=%async_computation.7 | async-start | bytes 524288 | tf_op jit(solution)/shard_map/all_to_all | solution.py:603
  30.6 12.2 %collective-permute-start.20 = (bf16[256,640]{1,0:T(8,128)(2,1)S(1)}, bf16[256,640]{1,0:T(8,128)(2,1)}, u32[]{:S(2)}, u32[]{:S(2)}) collective-permute-start(bf16[256,640]{1,0:T(8,128)(2,1)S(1)} %bitcast.38), channel_id=1, source_target_pairs={{16,24},{17,25},{18,26},{19,27},{20,28},{21,29},{22,30},{23,31}} | collective-permute-start | bytes 983048 | tf_op jit(solution)/shard_map/ppermute | solution.py:661
  32.0 10.8 %collective-permute-start.19 = (bf16[256,640]{1,0:T(8,128)(2,1)S(1)}, bf16[256,640]{1,0:T(8,128)(2,1)}, u32[]{:S(2)}, u32[]{:S(2)}) collective-permute-start(bf16[256,640]{1,0:T(8,128)(2,1)S(1)} %bitcast.39), channel_id=1, source_target_pairs={{8,24},{9,25},{10,26},{11,27},{12,28},{13,29},{14,30},{15,31}} | collective-permute-start | bytes 983048 | tf_op jit(solution)/shard_map/ppermute | solution.py:661
  34.0 8.7 %collective-permute-start.18 = (bf16[256,640]{1,0:T(8,128)(2,1)S(1)}, bf16[256,640]{1,0:T(8,128)(2,1)}, u32[]{:S(2)}, u32[]{:S(2)}) collective-permute-start(bf16[256,640]{1,0:T(8,128)(2,1)S(1)} %bitcast.40), channel_id=1, source_target_pairs={{0,24},{1,25},{2,26},{3,27},{4,28},{5,29},{6,30},{7,31}} | collective-permute-start | bytes 983048 | tf_op jit(solution)/shard_map/ppermute | solution.py:661
  35.4 7.4 %collective-permute-start.16 = (bf16[200,128]{1,0:T(8,128)(2,1)S(1)}, bf16[200,128]{1,0:T(8,128)(2,1)}, u32[]{:S(2)}, u32[]{:S(2)}) collective-permute-start(bf16[200,128]{1,0:T(8,128)(2,1)S(1)} %get-tuple-element.302), channel_id=1, source_target_pairs={{0,1},{1,2},{2,3},{3,4},{4,5},{5,6},{6,7},{8,9},{9,10},{10,11},{11... | collective-permute-start | bytes 153608 | tf_op jit(solution)/shard_map/ppermute | solution.py:598
  39.4 5.0 %collective-permute-start.17 = (bf16[200,128]{1,0:T(8,128)(2,1)S(1)}, bf16[200,128]{1,0:T(8,128)(2,1)}, u32[]{:S(2)}, u32[]{:S(2)}) collective-permute-start(bf16[200,128]{1,0:T(8,128)(2,1)S(1)} %get-tuple-element.303), channel_id=1, source_target_pairs={{1,0},{2,1},{3,2},{4,3},{5,4},{6,5},{7,6},{9,8},{10,9},{11,10},{12... | collective-permute-start | bytes 153608 | tf_op jit(solution)/shard_map/ppermute | solution.py:599
  49.3 11.7 %all-to-all-start.1 = ((bf16[8,32,512]{2,1,0:T(8,128)(2,1)}), bf16[8,32,512]{2,1,0:T(8,128)(2,1)}, u32[]{:S(2)}, u32[]{:S(2)}) async-start(bf16[8,32,512]{2,1,0:T(8,128)(2,1)} %bitcast.3), calls=%async_computation.1 | async-start | bytes 524288 | tf_op jit(solution)/shard_map/cond/branch_1_fun/all_to_all | solution.py:603
  61.0 10.0 %collective-permute-start.21 = (bf16[256,512]{1,0:T(8,128)(2,1)}, bf16[256,512]{1,0:T(8,128)(2,1)}, u32[]{:S(2)}, u32[]{:S(2)}) collective-permute-start(bf16[256,512]{1,0:T(8,128)(2,1)} %get-tuple-element.308), channel_id=1, source_target_pairs={{0,24},{1,25},{2,26},{3,27},{4,28},{5,29},{6,30},{7,31},{24,0},{25... | collective-permute-start | bytes 786440 | tf_op jit(solution)/shard_map/ppermute | solution.py:718
  62.4 12.2 %collective-permute-start.22 = (bf16[256,512]{1,0:T(8,128)(2,1)}, bf16[256,512]{1,0:T(8,128)(2,1)}, u32[]{:S(2)}, u32[]{:S(2)}) collective-permute-start(bf16[256,512]{1,0:T(8,128)(2,1)} %get-tuple-element.311), channel_id=1, source_target_pairs={{8,24},{9,25},{10,26},{11,27},{12,28},{13,29},{14,30},{15,31},{24,... | collective-permute-start | bytes 786440 | tf_op jit(solution)/shard_map/ppermute | solution.py:718
  69.6 4.9 %collective-permute-start.23 = (bf16[256,512]{1,0:T(8,128)(2,1)}, bf16[256,512]{1,0:T(8,128)(2,1)}, u32[]{:S(2)}, u32[]{:S(2)}) collective-permute-start(bf16[256,512]{1,0:T(8,128)(2,1)} %get-tuple-element.312), channel_id=1, source_target_pairs={{16,24},{17,25},{18,26},{19,27},{20,28},{21,29},{22,30},{23,31},{2... | collective-permute-start | bytes 786440 | tf_op jit(solution)/shard_map/ppermute | solution.py:718
  74.6 13.0 %copy-start.7 = (f32[1536,128]{1,0:T(8,128)S(1)}, f32[1536,128]{1,0:T(8,128)}, u32[]{:S(2)}) copy-start(f32[1536,128]{1,0:T(8,128)} %get-tuple-element.241.base) | copy-start | bytes 2359300 | tf_op jit(solution)/shard_map/cond
  74.6 8.0 %copy-start.10 = (bf16[192,128]{1,0:T(8,128)(2,1)S(1)}, bf16[192,128]{1,0:T(8,128)(2,1)}, u32[]{:S(2)}) copy-start(bf16[192,128]{1,0:T(8,128)(2,1)} %get-tuple-element.234) | copy-start | bytes 147460 | tf_op jit(solution)/shard_map/cond/branch_0_fun/cond
  74.6 13.0 %all-to-all-start.4 = ((bf16[8,32,512]{2,1,0:T(8,128)(2,1)}), bf16[8,32,512]{2,1,0:T(8,128)(2,1)}, u32[]{:S(2)}, u32[]{:S(2)}) async-start(bf16[8,32,512]{2,1,0:T(8,128)(2,1)} %bitcast.9), calls=%async_computation.4 | async-start | bytes 524288 | tf_op jit(solution)/shard_map/cond/branch_0_fun/cond/branch_1_fun/all_to_all | solution.py:603
  78.8 5.1 %collective-permute-start.4 = (bf16[192,128]{1,0:T(8,128)(2,1)S(1)}, bf16[192,128]{1,0:T(8,128)(2,1)}, u32[]{:S(2)}, u32[]{:S(2)}) collective-permute-start(bf16[192,128]{1,0:T(8,128)(2,1)S(1)} %get-tuple-element.233), channel_id=1, source_target_pairs={{8,9},{9,10},{10,11},{11,12},{12,13},{13,14},{14,15}} | collective-permute-start | bytes 147464 | tf_op jit(solution)/shard_map/cond/branch_0_fun/cond/branch_1_fun/ppermute | solution.py:598
  82.6 4.9 %collective-permute-start.5 = (bf16[192,128]{1,0:T(8,128)(2,1)S(1)}, bf16[192,128]{1,0:T(8,128)(2,1)}, u32[]{:S(2)}, u32[]{:S(2)}) collective-permute-start(bf16[192,128]{1,0:T(8,128)(2,1)S(1)} %copy-done.10), channel_id=1, source_target_pairs={{9,8},{10,9},{11,10},{12,11},{13,12},{14,13},{15,14}} | collective-permute-start | bytes 147464 | tf_op jit(solution)/shard_map/cond/branch_0_fun/cond/branch_1_fun/ppermute | solution.py:599
  (6 other events, 4.2 us)

commit v8 on v7

--- a/solution.py
+++ b/solution.py
@@ -169,7 +169,7 @@
             put_slab(out, a, i, force)
 
 
-def advance(ref, rates, filled, base, recv, sel, low, high, fills, out, pressure, stress, partial):
+def advance(ref, mat, filled, base, recv, sel, low, high, fills, out, pressure, stress, partial):
     e = filled.shape[-1]
     pressure[...] = dot(recv[...], sel[...], ((0,), (0,))) * PRESSURE_SCALE
     for i in range(8):
@@ -182,7 +182,7 @@
     penalty = PENALTY * UNIT_LENGTH
     fill_low, fill_high = fills[0].reshape(1, 1, e), fills[1].reshape(1, 1, e)
     for i in range(8):
-        rate = slab(rates, 0, i)
+        rate = (TIME_STEP / UNIT_LENGTH) * slab(mat, 2, i) * filled
         for a in range(3):
             here = slab(ref, a, i)
             force = slab(partial, a, i) - diff_i(
@@ -429,13 +429,6 @@
     return body
 
 
-def elastic_and_rate(state, mat, occ, out, rate, *scratch):
-    filled = occ[pl.ds(0, 1), :].reshape(1, 1, occ.shape[-1])
-    for i in range(8):
-        put_slab(rate, 0, i, (TIME_STEP / UNIT_LENGTH) * slab(mat, 2, i) * filled)
-    elastic(state, mat, filled, out, *scratch)
-
-
 def elastic_forces(state, mat, occ, out, *scratch):
     elastic(state, mat, occ[pl.ds(0, 1), :].reshape(1, 1, occ.shape[-1]), out, *scratch[-2:])
 
@@ -444,20 +437,20 @@
     pass
 
 
-def first_step(state, rates, occ, base, sel, recv, low, high, out, send, up, down, *scratch):
+def first_step(state, mat, occ, base, sel, recv, low, high, out, send, up, down, *scratch):
     filled = occ[pl.ds(0, 1), :].reshape(1, 1, occ.shape[-1])
     fills = [ref[pl.ds(192, 8), :].astype(F32)[:1] for ref in (low, high)]
-    advance(state, rates, filled, base, recv, sel, low, high, fills, out, *scratch[:3])
+    advance(state, mat, filled, base, recv, sel, low, high, fills, out, *scratch[:3])
     dil = scratch[3]
     dilate(out, filled, dil)
     send[...] = dot(sel[...], dil[...], ((1,), (1,))).astype(BF16)
     put_faces(out, up, down)
 
 
-def last_step(state, rates, occ, base, sel, recv, low, high, fill_low, fill_high, out, *scratch):
+def last_step(state, mat, occ, base, sel, recv, low, high, fill_low, fill_high, out, *scratch):
     filled = occ[pl.ds(0, 1), :].reshape(1, 1, occ.shape[-1])
     fills = [ref[pl.ds(192, 8), :].astype(F32)[:1] for ref in (fill_low, fill_high)]
-    advance(state, rates, filled, base, recv, sel, low, high, fills, out, *scratch)
+    advance(state, mat, filled, base, recv, sel, low, high, fills, out, *scratch)
 
 
 def deposit(edged):
@@ -664,13 +657,15 @@
         return tuple(call(rates(tiles), (mat,), (layers, ends)))
 
     def mech_elastic():
-        return tuple(call(elastic_and_rate, (current, mat, occ), (layers, ends), work[1:]))
+        return tuple(
+            call(elastic_forces, (current, mat, occ), (layers, ends), work[1:], unused=(1,))
+        )
 
     def mech_first():
         return tuple(
             call(
                 first_step,
-                (current, kap_edge, occ, base, sel, mine, side_low, side_high),
+                (current, mat, occ, base, sel, mine, side_low, side_high),
                 (layers, rows, face, face),
                 work + [pltpu.VMEM((512, e), BF16)],
             )
@@ -741,7 +736,7 @@
         mine, low, high = lax.switch(grp, [swapped(g) for g in groups])
         (out,) = call(
             last_step,
-            (moved, kap_edge, occ, force, sel, mine, low, high, side_low, side_high),
+            (moved, mat, occ, force, sel, mine, low, high, side_low, side_high),
             (flat,),
             work,
         )

time: 91.7 us -> 90.2 us (0.984)
  local copies, waits for them, and re-layouts: 2.91 us -> 1.58 us
    unnamed x14 -> x10, local copies, waits for them, and re-layouts: 2.02 us -> 0.69 us
where the time goes in v8:
time: 90.2 us; the launch traced here: 89.3 us
  starting transfers between devices  52 us (58%)
  waiting for transfers between devices  19.4 us (22%)
  Pallas kernels  16 us (18%)
  local copies, waits for them, and re-layouts  1.58 us (2%)
    all_to_all x4, starting transfers between devices, swap(): return lax.all_to_all(block, 'blk', split_axis=0, concat_axis=0, tiled=True)  21.4 us
    pallas_call x6, Pallas kernels, call(): pl.pallas_call(body, out_shape=outs, in_specs=[ANY if n in away else spec...  16 us
    ppermute x3, starting transfers between devices, shards(): lax.ppermute(block, axes, pairs(False, g) + pairs(True, g))  9.74 us
    ppermute x2, starting transfers between devices, both_ways(): lax.ppermute(up, axes, planes(True, which))  7.2 us
    ppermute x6, waiting for transfers between devices, field_to(): return lax.ppermute(half, axes, route)  6.4 us
    ppermute x6, starting transfers between devices, field_to(): return lax.ppermute(half, axes, route)  6.1 us
    ppermute x2, waiting for transfers between devices, both_ways(): lax.ppermute(down, axes, planes(False, which))  5.1 us
    ppermute x3, starting transfers between devices, shards(): arrived.append(lax.ppermute(recv, axes, pairs(False, g)))  5.01 us
  transfers between devices with their start and end apart: 20, of which 5 were waited for; matrix products, arithmetic and copies ran while one was open for 0% of the time, Pallas kernels for 5%

profile of v8, /device:TPU:1, one launch (start us, length us, event | category | flops | bytes accessed | tf_op | source)
XLA Modules:
  0.0 89.3 jit_solution(1780273513583266763)
XLA Ops:
  0.7 2.8 %shard_map.57 = (bf16[256,640]{1,0:T(8,128)(2,1)}, bf16[256,128]{1,0:T(8,128)(2,1)S(1)}, f32[8,128]{1,0:T(8,128)S(1)}, bf16[256,384]{1,0:T(8,128)(2,1)S(1)}, bf1...) custom-call(s32[1]{0:T(128)} %bitcast.15.grp, ...), custom_call_target="tpu_custom_call" | custom-call | tf_op jit(solution)/shard_map/pallas_call | solution.py:32
  3.5 6.4 %all-to-all-start.6 = ((bf16[8,32,640]{2,1,0:T(8,128)(2,1)}), bf16[8,32,640]{2,1,0:T(8,128)(2,1)S(1)}, u32[]{:S(2)}, u32[]{:S(2)}) async-start(bf16[8,32,640]{2,1,0:T(8,128)(2,1)} %bitcast.20), calls=%async_computation.6 | async-start | bytes 655360 | tf_op jit(solution)/shard_map/all_to_all | solution.py:596
  13.1 6.4 %collective-permute-done.11 = bf16[256,384]{1,0:T(8,128)(2,1)S(1)} collective-permute-done((bf16[256,384]{1,0:T(8,128)(2,1)S(1)}, bf16[256,384]{1,0:T(8,128)(2,1)S(1)}, u32[]{:S(2)}, u32[]{:S(2)}) %collective-permute-start.11) | collective-permute-done | bytes 196640 | tf_op jit(solution)/shard_map/ppermute | solution.py:625
  19.5 1.5 %collective-permute-start.12 = (bf16[256,384]{1,0:T(8,128)(2,1)S(1)}, bf16[256,384]{1,0:T(8,128)(2,1)S(1)}, u32[]{:S(2)}, u32[]{:S(2)}) collective-permute-start(bf16[256,384]{1,0:T(8,128)(2,1)S(1)} %collective-permute-done.11), channel_id=1, source_target_pairs={{8,0},{9,1},{10,2},{11,3},{12,4},{13,5},{14,6},{15,7}} | collective-permute-start | bytes 589832 | tf_op jit(solution)/shard_map/ppermute | solution.py:625
  23.6 5.7 %all-to-all-start.7 = ((bf16[8,32,512]{2,1,0:T(8,128)(2,1)}), bf16[8,32,512]{2,1,0:T(8,128)(2,1)}, u32[]{:S(2)}, u32[]{:S(2)}) async-start(bf16[8,32,512]{2,1,0:T(8,128)(2,1)} %bitcast.22), calls=%async_computation.7 | async-start | bytes 524288 | tf_op jit(solution)/shard_map/all_to_all | solution.py:596
  30.7 2.2 %collective-permute-start.19 = (bf16[256,640]{1,0:T(8,128)(2,1)S(1)}, bf16[256,640]{1,0:T(8,128)(2,1)}, u32[]{:S(2)}, u32[]{:S(2)}) collective-permute-start(bf16[256,640]{1,0:T(8,128)(2,1)S(1)} %bitcast.41), channel_id=1, source_target_pairs={{8,24},{9,25},{10,26},{11,27},{12,28},{13,29},{14,30},{15,31}} | collective-permute-start | bytes 983048 | tf_op jit(solution)/shard_map/ppermute | solution.py:654
  34.3 3.4 %collective-permute-start.16 = (bf16[200,128]{1,0:T(8,128)(2,1)S(1)}, bf16[200,128]{1,0:T(8,128)(2,1)S(1)}, u32[]{:S(2)}, u32[]{:S(2)}) collective-permute-start(bf16[200,128]{1,0:T(8,128)(2,1)S(1)} %get-tuple-element.301), channel_id=1, source_target_pairs={{0,1},{1,2},{2,3},{3,4},{4,5},{5,6},{6,7},{8,9},{9,10},{10,11},{11... | collective-permute-start | bytes 153608 | tf_op jit(solution)/shard_map/ppermute | solution.py:591
  39.0 2.0 %conditional.7 = ((f32[2048,128]{1,0:T(8,128)S(1)}, f32[512,128]{1,0:T(8,128)S(1)})) conditional(s32[]{:T(128)} %convert_element_type.2, (f32[1536,128]{1,0:T(8,128)S(1)}, f32[1536,128]{1,0:T(8,128)S(1)}, f32[8,128]{1,0:T(8,128)S(1)}) %tuple.107, f32[1536,128]{1,0:T(8,128)S(1)} %bitcast.27), branch_computations={%region_0.0_spmd, %region_1.0_spmd} | conditional | bytes 8 | solution.py:675
  39.0 2.0 %branch_0_fun.5 = (f32[2048,128]{1,0:T(8,128)S(1)}, f32[512,128]{1,0:T(8,128)S(1)}) custom-call(f32[1536,128]{1,0:T(8,128)S(1)} %get-tuple-element.156.state, f32[1536,128]{1,0:T(8,128)S(1)} %get-tuple-element.157.mat, f32[8,128]{1,0:T(8,128)S(1)} %get-tuple-element.158.occ), custom_call_target="tpu_custom_call" | custom-call | tf_op jit(solution)/shard_map/cond/branch_0_fun/pallas_call | solution.py:32
  41.0 1.5 %collective-permute-done.17 = bf16[200,128]{1,0:T(8,128)(2,1)S(1)} collective-permute-done((bf16[200,128]{1,0:T(8,128)(2,1)S(1)}, bf16[200,128]{1,0:T(8,128)(2,1)S(1)}, u32[]{:S(2)}, u32[]{:S(2)}) %collective-permute-start.17) | collective-permute-done | bytes 51232 | tf_op jit(solution)/shard_map/ppermute | solution.py:592
  42.5 4.9 %conditional.8 = ((f32[2048,128]{1,0:T(8,128)S(1)}, bf16[256,512]{1,0:T(8,128)(2,1)}, bf16[192,128]{1,0:T(8,128)(2,1)S(1)}, bf16[192,128]{1,0:T(8,128)(2,1)S(1)})) conditional(s32[]{:T(128)} %convert_element_type.2, (bf16[8,32,512]{2,1,0:T(8,128)(2,1)}, f32[1536,128]{1,0:T(8,128)S(1)}, f32[1536,128]{1,0:T(8,128)S(1)}, f32[8,128]{1,0:T(8,128)S(1)}, ...), branch_computations={%region_6.0_spmd, %region_7.0_spmd} | conditional | bytes 3145764 | solution.py:678
  43.4 4.0 %branch_0_fun.7 = (f32[2048,128]{1,0:T(8,128)S(1)}, bf16[256,512]{1,0:T(8,128)(2,1)}, bf16[192,128]{1,0:T(8,128)(2,1)S(1)}, bf16[192,128]{1,0:T(8,128)(2,1)S(1)}) custom-call(f32[1536,128]{1,0:T(8,128)} %copy-done.5, f32[1536,128]{1,0:T(8,128)S(1)} %get-tuple-element.169.mat, f32[8,128]{1,0:T(8,128)S(1)} %get-tuple-element.170.occ, ...), custom_call_target="tpu_custom_call" | custom-call | tf_op jit(solution)/shard_map/cond/branch_0_fun/pallas_call | solution.py:32
  47.4 12.3 %conditional.9 = (f32[2048,128]{1,0:T(8,128)}, f32[512,128]{1,0:T(8,128)}, bf16[768,128]{1,0:T(8,128)(2,1)}, f32[1536,128]{1,0:T(8,128)}, bf16[384,128]{1,0:T(8,...) conditional(s32[]{:T(128)} %clamp.7, ...), branch_computations={%region_8.0_spmd, %region_9.0_spmd, %region_10.0_spmd, %region_11.... | conditional | bytes 4980916 | solution.py:711
  47.4 5.2 %all-to-all-start.1 = ((bf16[8,32,512]{2,1,0:T(8,128)(2,1)}), bf16[8,32,512]{2,1,0:T(8,128)(2,1)}, u32[]{:S(2)}, u32[]{:S(2)}) async-start(bf16[8,32,512]{2,1,0:T(8,128)(2,1)} %bitcast.3), calls=%async_computation.1 | async-start | bytes 524288 | tf_op jit(solution)/shard_map/cond/branch_1_fun/all_to_all | solution.py:596
  52.6 2.8 %branch_1_fun.10 = (f32[1536,128]{1,0:T(8,128)}, f32[2048,128]{1,0:T(8,128)}, f32[512,128]{1,0:T(8,128)}, bf16[768,128]{1,0:T(8,128)(2,1)}, bf16[384,128]{1,0:T(...) custom-call(f32[2048,128]{1,0:T(8,128)S(1)} %get-tuple-element.188.state, ...), custom_call_target="tpu_custom_call" | custom-call | tf_op jit(solution)/shard_map/cond/branch_1_fun/pallas_call | solution.py:32
  55.4 4.3 %all-to-all-done.1 = bf16[8,32,512]{2,1,0:T(8,128)(2,1)} async-done(((bf16[8,32,512]{2,1,0:T(8,128)(2,1)}), bf16[8,32,512]{2,1,0:T(8,128)(2,1)}, u32[]{:S(2)}, u32[]{:S(2)}) %all-to-all-start.1) | async-done | bytes 262176 | tf_op jit(solution)/shard_map/cond/branch_1_fun/all_to_all | solution.py:596
  61.1 7.0 %collective-permute-start.22 = (bf16[256,512]{1,0:T(8,128)(2,1)}, bf16[256,512]{1,0:T(8,128)(2,1)}, u32[]{:S(2)}, u32[]{:S(2)}) collective-permute-start(bf16[256,512]{1,0:T(8,128)(2,1)} %get-tuple-element.311), channel_id=1, source_target_pairs={{8,24},{9,25},{10,26},{11,27},{12,28},{13,29},{14,30},{15,31},{24,... | collective-permute-start | bytes 786440 | tf_op jit(solution)/shard_map/ppermute | solution.py:713
  69.5 3.6 %collective-permute-done.22 = bf16[256,512]{1,0:T(8,128)(2,1)} collective-permute-done((bf16[256,512]{1,0:T(8,128)(2,1)}, bf16[256,512]{1,0:T(8,128)(2,1)}, u32[]{:S(2)}, u32[]{:S(2)}) %collective-permute-start.22) | collective-permute-done | bytes 262176 | tf_op jit(solution)/shard_map/ppermute | solution.py:713
  73.1 16.2 %conditional.10 = (f32[1,3,512,128]{3,2,1,0:T(8,128)}) conditional(s32[]{:T(128)} %convert_element_type.2, (s32[]{:T(128)}, bf16[256,512]{1,0:T(8,128)(2,1)}, bf16[192,128]{1,0:T(8,128)(2,1)S(1)}, bf16[192,128]{1,0:T(8,128)(2,1)S(1)}, bf16[256,512]{1,0:T(8,128)(2,1)}, /*index=5*/bf16[256,512]{1,0:T(8,128)(2,1)}, f32[2048,128]{1,0:T(8,128)S(1)}, ...), branch_computations={%region_12.0_spmd, %region_16.0_spmd} | conditional | flops 1 | bytes 4325636 | solution.py:745
  73.1 13.0 %conditional = (bf16[256,512]{1,0:T(8,128)(2,1)}, bf16[192,128]{1,0:T(8,128)(2,1)}, bf16[192,128]{1,0:T(8,128)(2,1)}) conditional(s32[]{:T(128)} %clamp.1, (bf16[256,512]{1,0:T(8,128)(2,1)}, bf16[192,128]{1,0:T(8,128)(2,1)S(1)}, bf16[192,128]{1,0:T(8,128)(2,1)S(1)}) %tuple.49, (bf16[256,512]{1,0:T(8,128)(2,1)}, ...), branch_computations={%region_13.0_spmd, %region_14.0_spmd, %region_15.0_spmd} | conditional | bytes 1179784 | solution.py:736
  73.1 4.2 %all-to-all-start.4 = ((bf16[8,32,512]{2,1,0:T(8,128)(2,1)}), bf16[8,32,512]{2,1,0:T(8,128)(2,1)}, u32[]{:S(2)}, u32[]{:S(2)}) async-start(bf16[8,32,512]{2,1,0:T(8,128)(2,1)} %bitcast.9), calls=%async_computation.4 | async-start | bytes 524288 | tf_op jit(solution)/shard_map/cond/branch_0_fun/cond/branch_1_fun/all_to_all | solution.py:596
  77.3 3.8 %collective-permute-start.4 = (bf16[192,128]{1,0:T(8,128)(2,1)S(1)}, bf16[192,128]{1,0:T(8,128)(2,1)}, u32[]{:S(2)}, u32[]{:S(2)}) collective-permute-start(bf16[192,128]{1,0:T(8,128)(2,1)S(1)} %get-tuple-element.233), channel_id=1, source_target_pairs={{8,9},{9,10},{10,11},{11,12},{12,13},{13,14},{14,15}} | collective-permute-start | bytes 147464 | tf_op jit(solution)/shard_map/cond/branch_0_fun/cond/branch_1_fun/ppermute | solution.py:591
  82.4 3.6 %collective-permute-done.5 = bf16[192,128]{1,0:T(8,128)(2,1)} collective-permute-done((bf16[192,128]{1,0:T(8,128)(2,1)S(1)}, bf16[192,128]{1,0:T(8,128)(2,1)}, u32[]{:S(2)}, u32[]{:S(2)}) %collective-permute-start.5) | collective-permute-done | bytes 49184 | tf_op jit(solution)/shard_map/cond/branch_0_fun/cond/branch_1_fun/ppermute | solution.py:592
  86.0 3.3 %branch_0_fun.9 = f32[1536,128]{1,0:T(8,128)} custom-call(f32[2048,128]{1,0:T(8,128)S(1)} %get-tuple-element.238.state, f32[1536,128]{1,0:T(8,128)S(1)} %get-tuple-element.239.mat, f32[8,128]{1,0:T(8,128)S(1)} %get-tuple-element.240.occ, f32[1536,128]{1,0:T(8,128)S(1)} %copy-done.7, bf16[256,128]{1,0:T(8,128)(2,1)S(1)} %get-tuple-element.242.sel, ...), custom_call_target="tpu_custom_call" | custom-call | tf_op jit(solution)/shard_map/cond/branch_0_fun/pallas_call | solution.py:32
  (42 shorter events, 16.4 us)
Async XLA Ops:
  3.5 18.9 %all-to-all-start.6 = ((bf16[8,32,640]{2,1,0:T(8,128)(2,1)}), bf16[8,32,640]{2,1,0:T(8,128)(2,1)S(1)}, u32[]{:S(2)}, u32[]{:S(2)}) async-start(bf16[8,32,640]{2,1,0:T(8,128)(2,1)} %bitcast.20), calls=%async_computation.6 | async-start | bytes 655360 | tf_op jit(solution)/shard_map/all_to_all | solution.py:596
  9.9 2.0 %collective-permute-start.10 = (bf16[256,384]{1,0:T(8,128)(2,1)S(1)}, bf16[256,384]{1,0:T(8,128)(2,1)S(1)}, u32[]{:S(2)}, u32[]{:S(2)}) collective-permute-start(bf16[256,384]{1,0:T(8,128)(2,1)S(1)} %get-tuple-element.295), channel_id=1, source_target_pairs={{24,0},{25,1},{26,2},{27,3},{28,4},{29,5},{30,6},{31,7}} | collective-permute-start | bytes 589832 | tf_op jit(solution)/shard_map/ppermute | solution.py:625
  10.5 9.0 %collective-permute-start.11 = (bf16[256,384]{1,0:T(8,128)(2,1)S(1)}, bf16[256,384]{1,0:T(8,128)(2,1)S(1)}, u32[]{:S(2)}, u32[]{:S(2)}) collective-permute-start(bf16[256,384]{1,0:T(8,128)(2,1)S(1)} %get-tuple-element.296), channel_id=1, source_target_pairs={{24,8},{25,9},{26,10},{27,11},{28,12},{29,13},{30,14},{31,15}} | collective-permute-start | bytes 589832 | tf_op jit(solution)/shard_map/ppermute | solution.py:625
  11.8 10.6 %collective-permute-start.13 = (bf16[256,384]{1,0:T(8,128)(2,1)S(1)}, bf16[256,384]{1,0:T(8,128)(2,1)S(1)}, u32[]{:S(2)}, u32[]{:S(2)}) collective-permute-start(bf16[256,384]{1,0:T(8,128)(2,1)S(1)} %collective-permute-done.10), channel_id=1, source_target_pairs={{0,8},{1,9},{2,10},{3,11},{4,12},{5,13},{6,14},{7,15}} | collective-permute-start | bytes 589832 | tf_op jit(solution)/shard_map/ppermute | solution.py:625
  19.5 2.9 %collective-permute-start.12 = (bf16[256,384]{1,0:T(8,128)(2,1)S(1)}, bf16[256,384]{1,0:T(8,128)(2,1)S(1)}, u32[]{:S(2)}, u32[]{:S(2)}) collective-permute-start(bf16[256,384]{1,0:T(8,128)(2,1)S(1)} %collective-permute-done.11), channel_id=1, source_target_pairs={{8,0},{9,1},{10,2},{11,3},{12,4},{13,5},{14,6},{15,7}} | collective-permute-start | bytes 589832 | tf_op jit(solution)/shard_map/ppermute | solution.py:625
  21.1 1.4 %collective-permute-start.14 = (bf16[256,384]{1,0:T(8,128)(2,1)S(1)}, bf16[256,384]{1,0:T(8,128)(2,1)S(1)}, u32[]{:S(2)}, u32[]{:S(2)}) collective-permute-start(bf16[256,384]{1,0:T(8,128)(2,1)S(1)} %get-tuple-element.295), channel_id=1, source_target_pairs={{24,16},{25,17},{26,18},{27,19},{28,20},{29,21},{30,22},{31,23}} | collective-permute-start | bytes 589832 | tf_op jit(solution)/shard_map/ppermute | solution.py:625
  21.7 0.7 collective-permute-start.15
  22.5 16.5 %copy-start.3 = (f32[1,3,512,128]{3,2,1,0:T(8,128)S(1)}, f32[1,3,512,128]{3,2,1,0:T(8,128)}, u32[]{:S(2)}) copy-start(f32[1,3,512,128]{3,2,1,0:T(8,128)} %param.23) | copy-start | bytes 2359300
  22.5 16.5 %copy-start.4 = (f32[1,3,512,128]{3,2,1,0:T(8,128)S(1)}, f32[1,3,512,128]{3,2,1,0:T(8,128)}, u32[]{:S(2)}) copy-start(f32[1,3,512,128]{3,2,1,0:T(8,128)} %param.22) | copy-start | bytes 2359300
  23.6 18.9 %all-to-all-start.7 = ((bf16[8,32,512]{2,1,0:T(8,128)(2,1)}), bf16[8,32,512]{2,1,0:T(8,128)(2,1)}, u32[]{:S(2)}, u32[]{:S(2)}) async-start(bf16[8,32,512]{2,1,0:T(8,128)(2,1)} %bitcast.22), calls=%async_computation.7 | async-start | bytes 524288 | tf_op jit(solution)/shard_map/all_to_all | solution.py:596
  29.3 11.7 %collective-permute-start.20 = (bf16[256,640]{1,0:T(8,128)(2,1)S(1)}, bf16[256,640]{1,0:T(8,128)(2,1)}, u32[]{:S(2)}, u32[]{:S(2)}) collective-permute-start(bf16[256,640]{1,0:T(8,128)(2,1)S(1)} %bitcast.40), channel_id=1, source_target_pairs={{16,24},{17,25},{18,26},{19,27},{20,28},{21,29},{22,30},{23,31}} | collective-permute-start | bytes 983048 | tf_op jit(solution)/shard_map/ppermute | solution.py:654
  30.7 10.3 %collective-permute-start.19 = (bf16[256,640]{1,0:T(8,128)(2,1)S(1)}, bf16[256,640]{1,0:T(8,128)(2,1)}, u32[]{:S(2)}, u32[]{:S(2)}) collective-permute-start(bf16[256,640]{1,0:T(8,128)(2,1)S(1)} %bitcast.41), channel_id=1, source_target_pairs={{8,24},{9,25},{10,26},{11,27},{12,28},{13,29},{14,30},{15,31}} | collective-permute-start | bytes 983048 | tf_op jit(solution)/shard_map/ppermute | solution.py:654
  32.9 8.1 %collective-permute-start.18 = (bf16[256,640]{1,0:T(8,128)(2,1)S(1)}, bf16[256,640]{1,0:T(8,128)(2,1)}, u32[]{:S(2)}, u32[]{:S(2)}) collective-permute-start(bf16[256,640]{1,0:T(8,128)(2,1)S(1)} %bitcast.42), channel_id=1, source_target_pairs={{0,24},{1,25},{2,26},{3,27},{4,28},{5,29},{6,30},{7,31}} | collective-permute-start | bytes 983048 | tf_op jit(solution)/shard_map/ppermute | solution.py:654
  34.3 6.7 %collective-permute-start.16 = (bf16[200,128]{1,0:T(8,128)(2,1)S(1)}, bf16[200,128]{1,0:T(8,128)(2,1)S(1)}, u32[]{:S(2)}, u32[]{:S(2)}) collective-permute-start(bf16[200,128]{1,0:T(8,128)(2,1)S(1)} %get-tuple-element.301), channel_id=1, source_target_pairs={{0,1},{1,2},{2,3},{3,4},{4,5},{5,6},{6,7},{8,9},{9,10},{10,11},{11... | collective-permute-start | bytes 153608 | tf_op jit(solution)/shard_map/ppermute | solution.py:591
  37.6 4.9 %collective-permute-start.17 = (bf16[200,128]{1,0:T(8,128)(2,1)S(1)}, bf16[200,128]{1,0:T(8,128)(2,1)S(1)}, u32[]{:S(2)}, u32[]{:S(2)}) collective-permute-start(bf16[200,128]{1,0:T(8,128)(2,1)S(1)} %get-tuple-element.302), channel_id=1, source_target_pairs={{1,0},{2,1},{3,2},{4,3},{5,4},{6,5},{7,6},{9,8},{10,9},{11,10},{12... | collective-permute-start | bytes 153608 | tf_op jit(solution)/shard_map/ppermute | solution.py:592
  42.5 0.9 copy-start.5
  47.4 12.3 %all-to-all-start.1 = ((bf16[8,32,512]{2,1,0:T(8,128)(2,1)}), bf16[8,32,512]{2,1,0:T(8,128)(2,1)}, u32[]{:S(2)}, u32[]{:S(2)}) async-start(bf16[8,32,512]{2,1,0:T(8,128)(2,1)} %bitcast.3), calls=%async_computation.1 | async-start | bytes 524288 | tf_op jit(solution)/shard_map/cond/branch_1_fun/all_to_all | solution.py:596
  59.8 9.7 %collective-permute-start.21 = (bf16[256,512]{1,0:T(8,128)(2,1)}, bf16[256,512]{1,0:T(8,128)(2,1)}, u32[]{:S(2)}, u32[]{:S(2)}) collective-permute-start(bf16[256,512]{1,0:T(8,128)(2,1)} %get-tuple-element.308), channel_id=1, source_target_pairs={{0,24},{1,25},{2,26},{3,27},{4,28},{5,29},{6,30},{7,31},{24,0},{25... | collective-permute-start | bytes 786440 | tf_op jit(solution)/shard_map/ppermute | solution.py:713
  61.1 11.9 %collective-permute-start.22 = (bf16[256,512]{1,0:T(8,128)(2,1)}, bf16[256,512]{1,0:T(8,128)(2,1)}, u32[]{:S(2)}, u32[]{:S(2)}) collective-permute-start(bf16[256,512]{1,0:T(8,128)(2,1)} %get-tuple-element.311), channel_id=1, source_target_pairs={{8,24},{9,25},{10,26},{11,27},{12,28},{13,29},{14,30},{15,31},{24,... | collective-permute-start | bytes 786440 | tf_op jit(solution)/shard_map/ppermute | solution.py:713
  68.1 4.9 %collective-permute-start.23 = (bf16[256,512]{1,0:T(8,128)(2,1)}, bf16[256,512]{1,0:T(8,128)(2,1)}, u32[]{:S(2)}, u32[]{:S(2)}) collective-permute-start(bf16[256,512]{1,0:T(8,128)(2,1)} %get-tuple-element.312), channel_id=1, source_target_pairs={{16,24},{17,25},{18,26},{19,27},{20,28},{21,29},{22,30},{23,31},{2... | collective-permute-start | bytes 786440 | tf_op jit(solution)/shard_map/ppermute | solution.py:713
  73.1 13.0 %copy-start.7 = (f32[1536,128]{1,0:T(8,128)S(1)}, f32[1536,128]{1,0:T(8,128)}, u32[]{:S(2)}) copy-start(f32[1536,128]{1,0:T(8,128)} %get-tuple-element.241.base) | copy-start | bytes 2359300 | tf_op jit(solution)/shard_map/cond
  73.1 13.0 %all-to-all-start.4 = ((bf16[8,32,512]{2,1,0:T(8,128)(2,1)}), bf16[8,32,512]{2,1,0:T(8,128)(2,1)}, u32[]{:S(2)}, u32[]{:S(2)}) async-start(bf16[8,32,512]{2,1,0:T(8,128)(2,1)} %bitcast.9), calls=%async_computation.4 | async-start | bytes 524288 | tf_op jit(solution)/shard_map/cond/branch_0_fun/cond/branch_1_fun/all_to_all | solution.py:596
  77.3 5.1 %collective-permute-start.4 = (bf16[192,128]{1,0:T(8,128)(2,1)S(1)}, bf16[192,128]{1,0:T(8,128)(2,1)}, u32[]{:S(2)}, u32[]{:S(2)}) collective-permute-start(bf16[192,128]{1,0:T(8,128)(2,1)S(1)} %get-tuple-element.233), channel_id=1, source_target_pairs={{8,9},{9,10},{10,11},{11,12},{12,13},{13,14},{14,15}} | collective-permute-start | bytes 147464 | tf_op jit(solution)/shard_map/cond/branch_0_fun/cond/branch_1_fun/ppermute | solution.py:591
  81.1 4.9 %collective-permute-start.5 = (bf16[192,128]{1,0:T(8,128)(2,1)S(1)}, bf16[192,128]{1,0:T(8,128)(2,1)}, u32[]{:S(2)}, u32[]{:S(2)}) collective-permute-start(bf16[192,128]{1,0:T(8,128)(2,1)S(1)} %get-tuple-element.234), channel_id=1, source_target_pairs={{9,8},{10,9},{11,10},{12,11},{13,12},{14,13},{15,14}} | collective-permute-start | bytes 147464 | tf_op jit(solution)/shard_map/cond/branch_0_fun/cond/branch_1_fun/ppermute | solution.py:592
  (3 other events, 2.0 us)
